TPU v7x, 32 devices: a whole 2x2x4 slice. The times are simulated.
32 devices in a mesh: fsdp: 16 (over z, y, core), sp: 2 (over x).
Axes of the slice: x: 2, y: 2, z: 4, core: 2. Of those that a mesh axis runs over, the one named last changes fastest.
Arguments:
- image: bfloat16 [16, 16, 64, 512], P('fsdp', 'sp'), may hold values from -6 to 6
- embedding: bfloat16 [16, 2048], P('fsdp'), may hold values from -6 to 6
- text: bfloat16 [16, 128, 2048], P('fsdp'), may hold values from -6 to 6
- heights: int32 [16], P('fsdp'), may hold values from 8 to 16, as said below
- gain_one: bfloat16 [512], P('fsdp'), may hold values from 0.099609375 to 1.8984375
- conv_one: bfloat16 [4608, 512], P('fsdp'), may hold values from -0.09375 to 0.09375
- emb_proj: bfloat16 [2048, 1024], P('fsdp'), may hold values from -0.125 to 0.125
- gain_two: bfloat16 [512], P('fsdp'), may hold values from 0.099609375 to 1.8984375
- conv_two: bfloat16 [4608, 512], P('fsdp'), may hold values from -0.09375 to 0.09375
- gain_three: bfloat16 [512], P('fsdp'), may hold values from 0.099609375 to 1.8984375
- qkv_proj: bfloat16 [512, 1536], P('fsdp'), may hold values from -0.25 to 0.25
- text_proj: bfloat16 [2048, 1024], P('fsdp'), may hold values from -0.125 to 0.125
- out_proj: bfloat16 [512, 512], P('fsdp'), may hold values from -6 to 6
- cotangent: bfloat16 [16, 16, 64, 512], P('fsdp', 'sp'), may hold values from -6 to 6
Outputs:
- output: bfloat16 [16, 16, 64, 512], P('fsdp', 'sp')
- image_grad: float32 [16, 16, 64, 512], P('fsdp', 'sp')
- embedding_grad: float32 [16, 2048], P('fsdp')
- text_grad: float32 [16, 128, 2048], P('fsdp')
- gain_one_grad: float32 [512], P('fsdp')
- conv_one_grad: float32 [4608, 512], P('fsdp')
- emb_proj_grad: float32 [2048, 1024], P('fsdp')
- gain_two_grad: float32 [512], P('fsdp')
- conv_two_grad: float32 [4608, 512], P('fsdp')
- gain_three_grad: float32 [512], P('fsdp')
- qkv_proj_grad: float32 [512, 1536], P('fsdp')
- text_proj_grad: float32 [2048, 1024], P('fsdp')
- out_proj_grad: float32 [512, 512], P('fsdp')
Inputs may be any that keep to these rules, and one draw needn't show every extreme that they name: `heights`: each item's image has this many rows; some item has 16 rows.
All inputs are finite; a program needn't handle non-finite values.
Results may differ from a plain program's by a relative error of at most 0.015.
Values may be sent and summed in bfloat16 or wider, within the bound.
A program may use at most 192 MiB of HBM per device.

v0:
```python
import jax
import jax.numpy as jnp
from jax import lax
from jax.sharding import PartitionSpec as P

C = 512
GROUPS = 32
HEAD = 64


EPSILON = 1e-05
MASKED = -1e30


def padded_2(cells, sides, width):
    for axis, dim in sides:
        count = lax.axis_size(axis)
        ends = count - 1
        head = lax.slice_in_dim(cells, 0, width, axis=dim)
        tail = lax.slice_in_dim(cells, cells.shape[dim] - width, cells.shape[dim], axis=dim)
        cells = jnp.concatenate(
            [
                lax.ppermute(tail, axis, [(i, (i + 1) % count) for i in range(ends)]),
                cells,
                lax.ppermute(head, axis, [((i + 1) % count, i) for i in range(ends)]),
            ],
            axis=dim,
        )
    return cells


def group_sums(values):
    return jnp.sum(values, axis=0).reshape(GROUPS, -1).sum(axis=1)


def spread(per_group):
    return jnp.repeat(per_group, C // GROUPS)


def normalize(field, pixel_mask, count):
    mean = lax.psum(group_sums(field * pixel_mask), "sp") / count
    centered = (field - spread(mean)) * pixel_mask
    variance = lax.psum(group_sums(centered * centered), "sp") / count
    inv_std = lax.rsqrt(variance + EPSILON)
    return (centered * spread(inv_std), inv_std)


def norm_back(grad_normed, normed, inv_std, count, extra):
    sums = jnp.concatenate([group_sums(grad_normed), group_sums(grad_normed * normed), extra])
    totals = lax.psum(sums, "sp")
    first = totals[:GROUPS] / count
    second = totals[GROUPS : 2 * GROUPS] / count
    grad_input = spread(inv_std) * (grad_normed - spread(first) - normed * spread(second))
    return (grad_input, totals[2 * GROUPS :])


def widen(field):
    padded = padded_2(field, (("sp", 0),), 1)
    return jnp.pad(padded, ((0, 0), (1, 1), (0, 0)))


def unfold(padded):
    rows = padded.shape[0] - 2
    columns = padded.shape[1] - 2
    taps = [
        padded[down : down + rows, across : across + columns]
        for down in range(3)
        for across in range(3)
    ]
    return jnp.concatenate(taps, axis=2).reshape(rows * columns, -1)


def conv_back(grad_out, weight, rows, columns):
    patches = unfold(widen(grad_out.reshape(rows, columns, C)))
    flipped = weight.reshape(9, C, C)[::-1]
    return lax.dot_general(
        patches.reshape(rows * columns, 9, C),
        flipped,
        (((1, 2), (0, 2)), ((), ())),
        preferred_element_type=jnp.float32,
    )


def weight_grad(padded, grad_out):
    return lax.dot_general(
        unfold(padded), grad_out, (((0,), (0,)), ((), ())), preferred_element_type=jnp.float32
    )


def silu_slope(value):
    sigmoid_value = jax.nn.sigmoid(value)
    return sigmoid_value * (1.0 + value * (1.0 - sigmoid_value))


def res_forward(masked, emb_act, weights, pixel_mask, count, rows, columns):
    gain_one, conv_one, emb_proj, gain_two, conv_two = weights
    normed_one, inv_one = normalize(masked, pixel_mask, count)
    hidden_one = normed_one * gain_one.astype(jnp.float32)
    act_one = (jax.nn.silu(hidden_one) * pixel_mask).astype(jnp.bfloat16)
    padded_one = widen(act_one.reshape(rows, columns, C))
    conv_out = (
        jnp.dot(unfold(padded_one), conv_one, preferred_element_type=jnp.float32) * pixel_mask
    )
    scales = jnp.dot(emb_act, emb_proj, preferred_element_type=jnp.float32)
    normed_two, inv_two = normalize(conv_out, pixel_mask, count)
    hidden_two = normed_two * gain_two.astype(jnp.float32) * (1.0 + scales[:, :C]) + scales[:, C:]
    act_two = (jax.nn.silu(hidden_two) * pixel_mask).astype(jnp.bfloat16)
    padded_two = widen(act_two.reshape(rows, columns, C))
    resid = (
        masked
        + jnp.dot(unfold(padded_two), conv_two, preferred_element_type=jnp.float32) * pixel_mask
    )
    return (
        resid,
        (
            normed_one,
            inv_one,
            hidden_one,
            padded_one,
            scales,
            normed_two,
            inv_two,
            hidden_two,
            padded_two,
        ),
    )


def per_device(
    image,
    embedding,
    text,
    heights,
    gain_one,
    conv_one,
    emb_proj,
    gain_two,
    conv_two,
    gain_three,
    qkv_proj,
    text_proj,
    out_proj,
    cotangent,
):
    rows = image.shape[1]
    columns = image.shape[2]
    pixels = rows * columns
    replicas = lax.axis_size("sp")
    height = heights[0]
    row_ids = lax.axis_index("sp") * rows + jnp.arange(rows, dtype=jnp.int32)
    pixel_mask = jnp.repeat((row_ids < height).astype(jnp.float32), columns)[:, None]
    count = (height * columns * (C // GROUPS)).astype(jnp.float32)
    nothing = jnp.zeros((0,), jnp.float32)
    factor = HEAD ** (-0.5)
    res_weights = (
        lax.all_gather(gain_one, "fsdp", axis=0, tiled=True),
        lax.all_gather(conv_one, "fsdp", axis=0, tiled=True),
        lax.all_gather(emb_proj, "fsdp", axis=0, tiled=True),
        lax.all_gather(gain_two, "fsdp", axis=0, tiled=True),
        lax.all_gather(conv_two, "fsdp", axis=0, tiled=True),
    )
    emb_float = embedding.astype(jnp.float32)
    emb_act = jax.nn.silu(emb_float).astype(jnp.bfloat16)
    masked = image[0].reshape(pixels, C).astype(jnp.float32) * pixel_mask
    resid, saved = res_forward(masked, emb_act, res_weights, pixel_mask, count, rows, columns)
    attn_weights = (
        lax.all_gather(gain_three, "fsdp", axis=0, tiled=True),
        lax.all_gather(qkv_proj, "fsdp", axis=0, tiled=True),
        lax.all_gather(text_proj, "fsdp", axis=0, tiled=True),
        lax.all_gather(out_proj, "fsdp", axis=0, tiled=True),
    )
    full_gain_three, full_qkv, full_text, full_out = attn_weights
    normed_three, inv_three = normalize(resid, pixel_mask, count)
    normed_low = (normed_three * full_gain_three.astype(jnp.float32)).astype(jnp.bfloat16)
    projected = jnp.dot(normed_low, full_qkv, preferred_element_type=jnp.float32).astype(
        jnp.bfloat16
    )
    text_kv = jnp.dot(text[0], full_text, preferred_element_type=jnp.float32).astype(jnp.bfloat16)
    gathered = lax.all_gather(projected[:, C:], "sp", axis=0, tiled=True)
    pixel_keys = gathered.shape[0]
    keys = jnp.concatenate([gathered[:, :C], text_kv[:, :C]], axis=0)
    values = jnp.concatenate([gathered[:, C:], text_kv[:, C:]], axis=0)
    key_rows = jnp.arange(pixel_keys, dtype=jnp.int32) // columns
    keep = jnp.concatenate([key_rows < height, jnp.ones((text_kv.shape[0],), dtype=bool)])

    def by_head(matrix):
        return matrix.reshape(matrix.shape[0], -1, HEAD).transpose(1, 0, 2)

    def join_heads(stack):
        return stack.transpose(1, 0, 2).reshape(stack.shape[1], -1)

    def scores_of(query, key):
        raw = (
            lax.dot_general(
                query, key, (((1,), (1,)), ((), ())), preferred_element_type=jnp.float32
            )
            * factor
        )
        return jnp.where(keep[None, :], raw, MASKED)

    def forward_head(parts):
        query, key, value = parts
        scores = scores_of(query, key)
        top = jnp.max(scores, axis=1, keepdims=True)
        raised = jnp.exp(scores - top)
        total = jnp.sum(raised, axis=1, keepdims=True)
        chances = (raised / total).astype(jnp.bfloat16)
        return (
            jnp.dot(chances, value, preferred_element_type=jnp.float32),
            (top + jnp.log(total))[:, 0],
        )

    def back_head(parts):
        query, key, value, log_total, grad_head = parts
        scores = scores_of(query, key)
        chances = jnp.exp(scores - log_total[:, None])
        grad_chances = lax.dot_general(
            grad_head, value, (((1,), (1,)), ((), ())), preferred_element_type=jnp.float32
        )
        grad_scores = (
            chances * (grad_chances - jnp.sum(chances * grad_chances, axis=1, keepdims=True))
        ).astype(jnp.bfloat16)
        grad_query = jnp.dot(grad_scores, key, preferred_element_type=jnp.float32) * factor
        grad_key = (
            lax.dot_general(
                grad_scores, query, (((0,), (0,)), ((), ())), preferred_element_type=jnp.float32
            )
            * factor
        )
        grad_value = lax.dot_general(
            chances.astype(jnp.bfloat16),
            grad_head,
            (((0,), (0,)), ((), ())),
            preferred_element_type=jnp.float32,
        )
        return (grad_query, grad_key, grad_value)

    query_heads = by_head(projected[:, :C])
    key_heads = by_head(keys)
    value_heads = by_head(values)
    attended, log_totals = lax.map(forward_head, (query_heads, key_heads, value_heads))
    attn_low = join_heads(attended).astype(jnp.bfloat16)
    branch = jnp.dot(attn_low, full_out, preferred_element_type=jnp.float32) * pixel_mask
    output = (resid + branch).astype(jnp.bfloat16).reshape(1, rows, columns, C)
    again = (
        lax.all_gather(gain_one, "fsdp", axis=0, tiled=True),
        lax.all_gather(conv_one, "fsdp", axis=0, tiled=True),
        lax.all_gather(emb_proj, "fsdp", axis=0, tiled=True),
        lax.all_gather(gain_two, "fsdp", axis=0, tiled=True),
        lax.all_gather(conv_two, "fsdp", axis=0, tiled=True),
        lax.all_gather(gain_three, "fsdp", axis=0, tiled=True),
        lax.all_gather(qkv_proj, "fsdp", axis=0, tiled=True),
        lax.all_gather(text_proj, "fsdp", axis=0, tiled=True),
        lax.all_gather(out_proj, "fsdp", axis=0, tiled=True),
    )
    back_res = again[:5]
    back_gain_three, back_qkv, back_text, back_out = again[5:]
    grad_y = cotangent[0].reshape(pixels, C).astype(jnp.float32) * pixel_mask
    grad_low = grad_y.astype(jnp.bfloat16)
    grad_out_proj = lax.dot_general(
        attn_low, grad_low, (((0,), (0,)), ((), ())), preferred_element_type=jnp.float32
    )
    grad_attn = lax.dot_general(
        grad_low, back_out, (((1,), (1,)), ((), ())), preferred_element_type=jnp.float32
    ).astype(jnp.bfloat16)
    grad_queries, grad_keys, grad_values = lax.map(
        back_head, (query_heads, key_heads, value_heads, log_totals, by_head(grad_attn))
    )
    grad_query_rows = join_heads(grad_queries)
    grad_key_rows = join_heads(grad_keys)
    grad_value_rows = join_heads(grad_values)
    kv_terms = jnp.concatenate([grad_key_rows[:pixel_keys], grad_value_rows[:pixel_keys]], axis=1)
    grad_kv_local = lax.psum_scatter(
        kv_terms.astype(jnp.bfloat16), "sp", scatter_dimension=0, tiled=True
    ).astype(jnp.float32)
    text_terms = jnp.concatenate([grad_key_rows[pixel_keys:], grad_value_rows[pixel_keys:]], axis=1)
    grad_text_kv = lax.psum(text_terms.astype(jnp.bfloat16), "sp")
    grad_qkv = jnp.concatenate([grad_query_rows, grad_kv_local], axis=1).astype(jnp.bfloat16)
    grad_qkv_proj = lax.dot_general(
        normed_low, grad_qkv, (((0,), (0,)), ((), ())), preferred_element_type=jnp.float32
    )
    grad_text_proj = lax.dot_general(
        text[0], grad_text_kv, (((0,), (0,)), ((), ())), preferred_element_type=jnp.float32
    ) * (1.0 / replicas)
    grad_text = lax.dot_general(
        grad_text_kv, back_text, (((1,), (1,)), ((), ())), preferred_element_type=jnp.float32
    )
    grad_normed_three = (
        lax.dot_general(
            grad_qkv, back_qkv, (((1,), (1,)), ((), ())), preferred_element_type=jnp.float32
        )
        * pixel_mask
    )
    grad_gain_three = jnp.sum(grad_normed_three * normed_three, axis=0)
    from_three, _ = norm_back(
        grad_normed_three * back_gain_three.astype(jnp.float32),
        normed_three,
        inv_three,
        count,
        nothing,
    )
    grad_resid = grad_y + from_three * pixel_mask
    attn_shards = (
        lax.psum_scatter(grad_gain_three, "fsdp", scatter_dimension=0, tiled=True),
        lax.psum_scatter(grad_qkv_proj, "fsdp", scatter_dimension=0, tiled=True),
        lax.psum_scatter(grad_text_proj, "fsdp", scatter_dimension=0, tiled=True),
        lax.psum_scatter(grad_out_proj, "fsdp", scatter_dimension=0, tiled=True),
    )
    _, saved_back = res_forward(masked, emb_act, back_res, pixel_mask, count, rows, columns)
    (
        normed_one,
        inv_one,
        hidden_one,
        padded_one,
        scales,
        normed_two,
        inv_two,
        hidden_two,
        padded_two,
    ) = saved_back
    back_gain_one, back_conv_one, back_emb, back_gain_two, back_conv_two = back_res
    grad_conv_two = (grad_resid * pixel_mask).astype(jnp.bfloat16)
    grad_conv_two_w = weight_grad(padded_two, grad_conv_two)
    grad_act_two = conv_back(grad_conv_two, back_conv_two, rows, columns)
    grad_hidden_two = grad_act_two * pixel_mask * silu_slope(hidden_two)
    gain_two_float = back_gain_two.astype(jnp.float32)
    grad_scale = jnp.sum(grad_hidden_two * normed_two * gain_two_float, axis=0)
    grad_shift = jnp.sum(grad_hidden_two, axis=0)
    grad_normed_two = grad_hidden_two * (1.0 + scales[:, :C])
    grad_gain_two = jnp.sum(grad_normed_two * normed_two, axis=0)
    from_two, scale_sums = norm_back(
        grad_normed_two * gain_two_float,
        normed_two,
        inv_two,
        count,
        jnp.concatenate([grad_scale, grad_shift]),
    )
    grad_scales = scale_sums.astype(jnp.bfloat16)[None, :]
    grad_conv_one = (from_two * pixel_mask).astype(jnp.bfloat16)
    grad_conv_one_w = weight_grad(padded_one, grad_conv_one)
    grad_emb_proj = lax.dot_general(
        emb_act, grad_scales, (((0,), (0,)), ((), ())), preferred_element_type=jnp.float32
    ) * (1.0 / replicas)
    grad_embedding = lax.dot_general(
        grad_scales, back_emb, (((1,), (1,)), ((), ())), preferred_element_type=jnp.float32
    ) * silu_slope(emb_float)
    grad_act_one = conv_back(grad_conv_one, back_conv_one, rows, columns)
    grad_hidden_one = grad_act_one * pixel_mask * silu_slope(hidden_one)
    grad_gain_one = jnp.sum(grad_hidden_one * normed_one, axis=0)
    from_one, _ = norm_back(
        grad_hidden_one * back_gain_one.astype(jnp.float32), normed_one, inv_one, count, nothing
    )
    grad_image = ((grad_resid + from_one) * pixel_mask).reshape(1, rows, columns, C)
    shard_gain_three, shard_qkv, shard_text, shard_out = attn_shards
    shard_gain_one, shard_conv_one, shard_emb, shard_gain_two, shard_conv_two = (
        lax.psum_scatter(grad_gain_one, "fsdp", scatter_dimension=0, tiled=True),
        lax.psum_scatter(grad_conv_one_w, "fsdp", scatter_dimension=0, tiled=True),
        lax.psum_scatter(grad_emb_proj, "fsdp", scatter_dimension=0, tiled=True),
        lax.psum_scatter(grad_gain_two, "fsdp", scatter_dimension=0, tiled=True),
        lax.psum_scatter(grad_conv_two_w, "fsdp", scatter_dimension=0, tiled=True),
    )
    summed = (
        lax.psum(shard_gain_one.astype(jnp.bfloat16), "sp").astype(jnp.float32),
        lax.psum(shard_conv_one.astype(jnp.bfloat16), "sp").astype(jnp.float32),
        lax.psum(shard_emb.astype(jnp.bfloat16), "sp").astype(jnp.float32),
        lax.psum(shard_gain_two.astype(jnp.bfloat16), "sp").astype(jnp.float32),
        lax.psum(shard_conv_two.astype(jnp.bfloat16), "sp").astype(jnp.float32),
        lax.psum(shard_gain_three.astype(jnp.bfloat16), "sp").astype(jnp.float32),
        lax.psum(shard_qkv.astype(jnp.bfloat16), "sp").astype(jnp.float32),
        lax.psum(shard_text.astype(jnp.bfloat16), "sp").astype(jnp.float32),
        lax.psum(shard_out.astype(jnp.bfloat16), "sp").astype(jnp.float32),
    )
    return (
        output,
        grad_image,
        grad_embedding,
        grad_text[None],
        summed[0],
        summed[1],
        summed[2],
        summed[3],
        summed[4],
        summed[5],
        summed[6],
        summed[7],
        summed[8],
    )


def solution(mesh):
    in_specs = (
        P("fsdp", "sp", None, None),
        P("fsdp", None),
        P("fsdp", None, None),
        P("fsdp"),
        P("fsdp"),
        P("fsdp", None),
        P("fsdp", None),
        P("fsdp"),
        P("fsdp", None),
        P("fsdp"),
        P("fsdp", None),
        P("fsdp", None),
        P("fsdp", None),
        P("fsdp", "sp", None, None),
    )
    out_specs = (
        P("fsdp", "sp", None, None),
        P("fsdp", "sp", None, None),
        P("fsdp", None),
        P("fsdp", None, None),
        P("fsdp"),
        P("fsdp", None),
        P("fsdp", None),
        P("fsdp"),
        P("fsdp", None),
        P("fsdp"),
        P("fsdp", None),
        P("fsdp", None),
        P("fsdp", None),
    )
    return jax.shard_map(
        per_device, mesh=mesh, in_specs=in_specs, out_specs=out_specs, check_vma=False
    )
```

profile of v0, /device:TPU:0, one launch (start us, length us, event | category | flops | bytes accessed | tf_op | source)
XLA Modules:
  0.0 1138.2 jit_solution(15441225479098122973)
XLA Ops:
  15.2 35.9 %all-reduce.12 = (bf16[512]{0:T(512)(128)(2,1)S(1)}, bf16[512]{0:T(512)(128)(2,1)S(1)}, bf16[512]{0:T(512)(128)(2,1)S(1)}) all-reduce(bf16[512]{0:T(512)(128)(2,1)S(1)} %dynamic-update-slice.2, bf16[512]{0:T(512)(128)(2,1)S(1)} %dynamic-update-slice.1, bf16[512]{0:T(512)(128)(2,1)S(1)} %dynamic-update-slice), channel_id=1, replica_groups=mesh['fsdp'=16,'sp'=2] {'fsdp'}, use_global_device_ids=true, to_apply=%add.7 | all-reduce | flops 1536 | bytes 6144
  89.9 27.5 %all-gather.7.cloned.1.call-done = bf16[4608,512]{1,0:T(8,128)(2,1)} async-done(((bf16[288,512]{1,0:T(8,128)(2,1)}), bf16[4608,512]{1,0:T(8,128)(2,1)}) %all-gather.7.cloned.1.call-update) | async-done | bytes 4718608 | tf_op jit(solution)/shard_map/all_gather | solution.py:157
  153.7 17.7 %all-gather.11.cloned.1.call-done = bf16[4608,512]{1,0:T(8,128)(2,1)} async-done(((bf16[288,512]{1,0:T(8,128)(2,1)}), bf16[4608,512]{1,0:T(8,128)(2,1)}) %all-gather.11.cloned.1.call-update) | async-done | bytes 4718608 | tf_op jit(solution)/shard_map/all_gather | solution.py:160
  188.9 22.8 %all-gather.13.cloned.1.call-done = bf16[512,1536]{1,0:T(8,128)(2,1)} async-done(((bf16[32,1536]{1,0:T(8,128)(2,1)}), bf16[512,1536]{1,0:T(8,128)(2,1)}) %all-gather.13.cloned.1.call-update) | async-done | bytes 1572880 | tf_op jit(solution)/shard_map/all_gather | solution.py:168
  216.5 22.0 %all_gather.48 = bf16[512,512]{1,0:T(8,128)(2,1)S(1)} all-gather(bf16[32,512]{1,0:T(8,128)(2,1)S(1)} %copy-done.11), channel_id=1, replica_groups=mesh['fsdp'=16,'sp'=2] {'fsdp'}, dimensions={0}, use_global_device_ids=true | all-gather | bytes 557056 | tf_op jit(solution)/shard_map/all_gather | solution.py:170
  241.2 22.5 %all-gather.17.cloned.1.call-done = bf16[2048,1024]{1,0:T(8,128)(2,1)} async-done(((bf16[128,1024]{1,0:T(8,128)(2,1)}), bf16[2048,1024]{1,0:T(8,128)(2,1)}) %all-gather.17.cloned.1.call-update) | async-done | bytes 4194320 | tf_op jit(solution)/shard_map/all_gather | solution.py:169
  269.2 28.1 %all-gather.15.cloned.1.call-done = bf16[1024,1024]{1,0:T(8,128)(2,1)} async-done(((bf16[512,1024]{1,0:T(8,128)(2,1)}), bf16[1024,1024]{1,0:T(8,128)(2,1)}) %all-gather.15.cloned.1.call-update) | async-done | bytes 2097168 | tf_op jit(solution)/shard_map/all_gather | solution.py:179
  313.7 35.6 %while.26 = (s32[]{:T(128)}, bf16[8,512,64]{1,2,0:T(8,128)(2,1)}, f32[8,512]{1,0:T(8,128)S(1)}, pred[1152]{0:T(1024)(128)(4,1)S(1)}, bf16[8,512,64]{2,1,0:T(8,12...) while((s32[]{:T(128)}, bf16[8,512,64]{1,2,0:T(8,128)(2,1)}, ...), condition=%wide.region_21.22_spmd, body=%wide.region_18.21_spmd.sunk | while | flops 155713024 | bytes 7954537 | solution.py:241
  350.1 69.8 %while.27 = (s32[]{:T(128)}, bf16[8,512,64]{1,2,0:T(8,128)(2,1)}, bf16[8,1152,64]{1,2,0:T(8,128)(2,1)}, bf16[8,1152,64]{1,2,0:T(8,128)(2,1)}, pred[1152]{0:T(102...) while((s32[]{:T(128)}, bf16[8,512,64]{1,2,0:T(8,128)(2,1)}, ...), condition=%wide.region_24.25_spmd, body=%wide.region_22.24_spmd.sunk | while | flops 382901760 | bytes 19842168 | solution.py:266
  429.4 26.7 %reduce-scatter.8.cloned.1.call-done = bf16[512,1024]{0,1:T(8,128)(2,1)} async-done(((bf16[1024,1024]{0,1:T(8,128)(2,1)}), bf16[512,1024]{0,1:T(8,128)(2,1)}) %reduce-scatter.8.cloned.1.call-update) | async-done | bytes 1048592 | tf_op jit(solution)/shard_map/reduce_scatter | solution.py:273
  460.4 22.0 %all-reduce.18.cloned.1.call-done = bf16[128,1024]{0,1:T(8,128)(2,1)} async-done(((bf16[128,1024]{0,1:T(8,128)(2,1)}), bf16[128,1024]{0,1:T(8,128)(2,1)}) %all-reduce.18.cloned.1.call-update) | async-done | bytes 262160 | tf_op jit(solution)/shard_map/psum | solution.py:277
  517.6 9.9 reshape_reshape.6
  527.5 12.2 %multiply_reduce_fusion.2 = (f32[512]{0:T(512)S(1)}, f32[512]{0:T(512)S(1)}, f32[512]{0:T(512)S(1)}, f32[512]{0:T(512)S(1)}, f32[512]{0:T(512)S(1)}, /*index=5*/f32[512,512]{1,0:T(8,128)}) fusion(f32[512]{0:T(512)S(1)} %bitcast.288, f32[512]{0:T(512)S(1)} %mul.489, f32[512]{0:T(512)S(1)} %mul.233, f32[512,512]{1,0:T(8,128)} %copy-done.2, f32[512]{0:T(512)S(1)} %sub.135, ...), kind=kOutput, calls=%fused_computation.95 | convolution fusion | flops 2422732288 | bytes 11556864 | tf_op jit(solution)/shard_map/dot_general | solution.py:76
  549.1 7.5 fusion.108
  559.3 7.8 fusion.107
  592.5 9.9 reshape_reshape.7
  602.3 10.4 reduce-scatter.16.cloned.1.call-done
  614.4 104.9 %reduce-scatter.18.cloned.1.call-done = f32[128,1024]{0,1:T(8,128)} async-done(((f32[2048,1024]{0,1:T(8,128)}), f32[128,1024]{0,1:T(8,128)}) %reduce-scatter.18.cloned.1.call-update) | async-done | bytes 524304 | tf_op jit(solution)/shard_map/reduce_scatter | solution.py:306
  721.0 105.3 %reduce-scatter.12.cloned.1.call-done = f32[128,1024]{1,0:T(8,128)} async-done(((f32[2048,1024]{1,0:T(8,128)}), f32[128,1024]{1,0:T(8,128)}) %reduce-scatter.12.cloned.1.call-update) | async-done | bytes 524304 | tf_op jit(solution)/shard_map/reduce_scatter | solution.py:358
  828.1 113.2 %reduce-scatter.14.cloned.1.call-done = f32[288,512]{1,0:T(8,128)} async-done(((f32[4608,512]{1,0:T(8,128)}), f32[288,512]{1,0:T(8,128)}) %reduce-scatter.14.cloned.1.call-update) | async-done | bytes 589840 | tf_op jit(solution)/shard_map/reduce_scatter | solution.py:360
  943.1 113.1 %reduce-scatter.10.cloned.1.call-done = f32[288,512]{1,0:T(8,128)} async-done(((f32[4608,512]{1,0:T(8,128)}), f32[288,512]{1,0:T(8,128)}) %reduce-scatter.10.cloned.1.call-update) | async-done | bytes 589840 | tf_op jit(solution)/shard_map/reduce_scatter | solution.py:357
  1058.0 11.9 %multiply_reduce_fusion.3 = (f32[512]{0:T(512)S(1)}, f32[512]{0:T(512)S(1)}, f32[512]{0:T(512)S(1)}, f32[512,512]{1,0:T(8,128)}) fusion(f32[512]{0:T(512)S(1)} %mul.469, f32[512]{0:T(512)S(1)} %sub.128, f32[512]{0:T(512)S(1)} %mul.233, bf16[1,8,64,512]{3,2,1,0:T(8,128)(2,1)S(1)} %copy-done.1, f32[512]{0:T(512)S(1)} %convert_element_type.182, ...), kind=kOutput, calls=%fused_computation.96 | convolution fusion | flops 2421422592 | bytes 12072960 | tf_op jit(solution)/shard_map/dot_general | solution.py:76
  1070.0 32.6 %all-reduce.11 = (bf16[512]{0:T(512)(128)(2,1)S(1)}, bf16[512]{0:T(512)(128)(2,1)S(1)}, bf16[512]{0:T(512)(128)(2,1)S(1)}) all-reduce(f32[512]{0:T(512)S(1)} %get-tuple-element.188, f32[512]{0:T(512)S(1)} %get-tuple-element.183, f32[512]{0:T(512)S(1)} %get-tuple-element.186), channel_id=3, replica_groups=mesh['fsdp'=16,'sp'=2] {'fsdp'}, use_global_device_ids=true, to_apply=%region_45.46.clone | all-reduce | flops 1536 | bytes 9216
  1102.8 8.4 all-reduce.13
  (370 shorter events, 348.8 us)
Async XLA Ops:
  7.2 256.6 %copy-start = (bf16[1,128,2048]{2,1,0:T(8,128)(2,1)S(1)}, bf16[1,128,2048]{2,1,0:T(8,128)(2,1)}, u32[]{:S(2)}) copy-start(bf16[1,128,2048]{2,1,0:T(8,128)(2,1)} %param.20) | copy-start | bytes 1572868
  7.2 79.9 %all-gather.9.cloned.1.call-start = ((), (), s32[]{:S(2)}) async-start(), calls=%async_computation.8 | async-start | bytes 4456448 | tf_op jit(solution)/shard_map/all_gather | solution.py:158
  7.9 109.5 %all-gather.7.cloned.1.call-start = ((), (), s32[]{:S(2)}) async-start(), calls=%async_computation.7 | async-start | bytes 5013504 | tf_op jit(solution)/shard_map/all_gather | solution.py:157
  8.7 162.7 %all-gather.11.cloned.1.call-start = ((), (), s32[]{:S(2)}) async-start(), calls=%async_computation.9 | async-start | bytes 5013504 | tf_op jit(solution)/shard_map/all_gather | solution.py:160
  9.4 202.3 %all-gather.13.cloned.1.call-start = ((), (), s32[]{:S(2)}) async-start(), calls=%async_computation.10 | async-start | bytes 1671168 | tf_op jit(solution)/shard_map/all_gather | solution.py:168
  10.0 253.7 %all-gather.17.cloned.1.call-start = ((), (), s32[]{:S(2)}) async-start(), calls=%async_computation.12 | async-start | bytes 4456448 | tf_op jit(solution)/shard_map/all_gather | solution.py:169
  68.7 5.3 collective-permute-start
  72.1 6.2 collective-permute-start.1
  73.4 224.0 %all-gather.15.cloned.1.call-start = ((), (), s32[]{:S(2)}) async-start(), calls=%async_computation.11 | async-start | bytes 3145728 | tf_op jit(solution)/shard_map/all_gather | solution.py:179
  135.0 5.3 collective-permute-start.2
  138.4 6.2 collective-permute-start.3
  216.4 239.7 %reduce-scatter.8.cloned.1.call-start = ((), (), s32[]{:S(2)}) async-start(), calls=%async_computation.13 | async-start | bytes 3145728 | tf_op jit(solution)/shard_map/reduce_scatter | solution.py:273
  424.1 58.2 %all-reduce.18.cloned.1.call-start = ((), (), s32[]{:S(2)}) async-start(), calls=%async_computation.14 | async-start | bytes 524288 | tf_op jit(solution)/shard_map/psum | solution.py:277
  426.7 148.3 %reduce-scatter.20.cloned.1.call-start = ((), (), s32[]{:S(2)}) async-start(), calls=%async_computation.20 | async-start | bytes 1114112 | tf_op jit(solution)/shard_map/reduce_scatter | solution.py:307
  429.3 183.4 %reduce-scatter.16.cloned.1.call-start = ((), (), s32[]{:S(2)}) async-start(), calls=%async_computation.18 | async-start | bytes 3342336 | tf_op jit(solution)/shard_map/reduce_scatter | solution.py:305
  460.3 259.0 %reduce-scatter.18.cloned.1.call-start = ((), (), s32[]{:S(2)}) async-start(), calls=%async_computation.19 | async-start | bytes 8912896 | tf_op jit(solution)/shard_map/reduce_scatter | solution.py:306
  487.9 338.5 %reduce-scatter.12.cloned.1.call-start = ((), (), s32[]{:S(2)}) async-start(), calls=%async_computation.16 | async-start | bytes 8912896 | tf_op jit(solution)/shard_map/reduce_scatter | solution.py:358
  500.8 4.1 collective-permute-start.4
  503.0 6.2 collective-permute-start.5
  549.1 392.2 %reduce-scatter.14.cloned.1.call-start = ((), (), s32[]{:S(2)}) async-start(), calls=%async_computation.17 | async-start | bytes 10027008 | tf_op jit(solution)/shard_map/reduce_scatter | solution.py:360
  556.7 499.5 %reduce-scatter.10.cloned.1.call-start = ((), (), s32[]{:S(2)}) async-start(), calls=%async_computation.15 | async-start | bytes 10027008 | tf_op jit(solution)/shard_map/reduce_scatter | solution.py:357
  567.2 555.4 %all-reduce.20.cloned.1.call-start = ((), (), s32[]{:S(2)}) async-start(), calls=%async_computation.21 | async-start | bytes 2424832 | tf_op jit(solution)/shard_map/psum | solution.py:370
  575.9 7.3 collective-permute-start.6
  577.9 6.2 collective-permute-start.7
  (12 other events, 212.6 us)
Sparse Core Ops, SparseCore 0:
  10.2 53.1 all-gather.8
  65.7 51.7 all-gather.6
  119.7 51.6 all-gather.10
  173.6 38.1 all-gather.12
  213.8 49.9 all-gather.16
  265.7 31.6 all-gather.14
  424.2 31.8 reduce-scatter.7
  459.0 23.2 all-reduce.17
  485.9 57.6 reduce-scatter.19
  547.2 65.4 reduce-scatter.15
  616.9 102.3 reduce-scatter.17
  723.2 103.0 reduce-scatter.11
  830.4 110.8 reduce-scatter.13
  945.3 110.8 reduce-scatter.9
  1059.7 43.3 all-reduce.19
where the time goes:
time: 1150 us; the launch traced here: 1140 us
  waiting for transfers between devices  632 us (55%)
  matrix products  187 us (16%)
  blocking collectives  144 us (13%)
  local copies, waits for them, and re-layouts  83 us (7%)
  other arithmetic  59.3 us (5%)
  starting transfers between devices  16.8 us (1%)
  between operations  16.6 us (1%)
    reduce_scatter x1, waiting for transfers between devices, per_device(): lax.psum_scatter(grad_conv_two_w, 'fsdp', scatter_dimension=0, tiled=True)  113 us
    reduce_scatter x1, waiting for transfers between devices, per_device(): lax.psum_scatter(grad_conv_one_w, 'fsdp', scatter_dimension=0, tiled=True)  113 us
    reduce_scatter x1, waiting for transfers between devices, per_device(): lax.psum_scatter(grad_emb_proj, 'fsdp', scatter_dimension=0, tiled=True)  105 us
    reduce_scatter x1, waiting for transfers between devices, per_device(): lax.psum_scatter(grad_text_proj, 'fsdp', scatter_dimension=0, tiled=True)  105 us
    unnamed x2, blocking collectives  68.5 us
    unnamed x59, local copies, waits for them, and re-layouts  30.6 us
    all_gather x1, waiting for transfers between devices, per_device(): gathered = lax.all_gather(projected[:, C:], 'sp', axis=0, tiled=True)  28.1 us
    dot_general x16, matrix products, scores_of(): lax.dot_general(query, key, (((1,), (1,)), ((), ())), preferred_element_t...  27.7 us
  transfers between devices with their start and end apart: 23, of which 18 were waited for; matrix products, arithmetic and copies ran while one was open for 17% of the time, Pallas kernels for 0%

commit v1 on v0

v1 whole, which is shorter than its diff:
```python
import functools

import jax
import jax.numpy as jnp
from jax import lax
from jax.experimental import pallas as pl
from jax.experimental.pallas import tpu as pltpu
from jax.sharding import PartitionSpec as P

C = 512
GROUPS = 32
HEAD = 64
EPSILON = 1e-05
MASKED = -1e30
LIMIT = 60 * 1024 * 1024

F32 = jnp.float32
BF16 = jnp.bfloat16
DMA = pltpu.SemaphoreType.DMA
ANY = pl.BlockSpec(memory_space=pl.ANY)
VMEM = pl.BlockSpec(memory_space=pltpu.VMEM)
SMEM = pl.BlockSpec(memory_space=pltpu.SMEM)


def sizes_of(fsdp, sp):
    lines = sp if fsdp % (2 * sp) == 0 else 1
    return fsdp // (2 * lines), lines, 2


def remote(src, dst, send, recv, device):
    return pltpu.make_async_remote_copy(
        src, dst, send, recv, device_id=device, device_id_type=pl.DeviceIdType.MESH
    )


def greet(peers):
    barrier = pltpu.get_barrier_semaphore()
    for peer in peers:
        pl.semaphore_signal(
            barrier, inc=1, device_id=peer, device_id_type=pl.DeviceIdType.MESH
        )
    pl.semaphore_wait(barrier, len(peers))


def params(cid):
    return pltpu.CompilerParams(
        collective_id=cid, has_side_effects=True, vmem_limit_bytes=LIMIT
    )


def tiles_start(fsdp, source, dest, send, recv, pick):
    me, x = lax.axis_index("fsdp"), lax.axis_index("sp")
    copies = []
    for d in range(1, fsdp):
        to = (me + d) % fsdp
        copy = remote(pick(source, to), dest.at[me], send.at[d], recv.at[d], (to, x))
        copy.start()
        copies.append(copy)
    return copies


def gather_kernel(dims, fsdp, sp, shapes, *refs):
    zs, ys, cs = dims
    count = len(shapes)
    shards, tiles, table = refs[:count], refs[count], refs[count + 1]
    refs = refs[count + 2 :]
    outs, tiles_out, scales_out = refs[:count], refs[count], refs[count + 1]
    refs = refs[count + 2 :]
    bufs, got, part, part_in = refs[:count], refs[count], refs[count + 1], refs[count + 2]
    zsend, zrecv, ysend, yrecv, xsend, xrecv, csend, crecv, local, tsem, psem = refs[count + 3 :]
    me, x = lax.axis_index("fsdp"), lax.axis_index("sp")
    z, y, c = me // (ys * cs), (me // cs) % ys, me % cs

    def dev(zz, yy, cc):
        return ((zz * ys + yy) * cs + cc, x)

    peers = [((me + d) % fsdp, x) for d in range(1, fsdp)]
    peers += [(me, (x + d) % sp) for d in range(1, sp)]
    greet(peers)
    flying = tiles_start(fsdp, tiles, got, tsem.at[0], tsem.at[1], lambda ref, to: ref.at[to])

    def owner(dz, dy):
        return (z - dz + zs) % zs, (y - dy + ys) % ys

    def piece(a):
        return x if shapes[a][0] > 1 else 0

    def zcopy(a, dz):
        h = piece(a)
        return remote(
            shards[a].at[h],
            outs[a].at[z, y, c, h],
            zsend.at[a, dz],
            zrecv.at[a, dz],
            dev((z + dz) % zs, y, c),
        )

    def ycopy(a, dz, dy):
        h = piece(a)
        zz, _ = owner(dz, 0)
        src = shards[a].at[h] if dz == 0 else outs[a].at[zz, y, c, h]
        return remote(
            src,
            outs[a].at[zz, y, c, h],
            ysend.at[a, dz, dy],
            yrecv.at[a, dz, dy],
            dev(z, (y + dy) % ys, c),
        )

    def xcopy(a, dz, dy, dx):
        zz, yy = owner(dz, dy)
        return remote(
            outs[a].at[zz, yy, c, x],
            outs[a].at[zz, yy, c, x],
            xsend.at[a, dz, dy, dx],
            xrecv.at[a, dz, dy, dx],
            (me, (x + dx) % sp),
        )

    def ccopy(a, dz, dy, dx):
        zz, yy = owner(dz, dy)
        if dz == 0 and dy == 0:
            src, dst = shards[a], outs[a].at[zz, yy, c]
        else:
            h = (x - dx + sp) % sp if shapes[a][0] > 1 else 0
            src = dst = outs[a].at[zz, yy, c, h]
        return remote(src, dst, csend.at[a, dz, dy, dx], crecv.at[a, dz, dy, dx], dev(z, y, 1 - c))

    def launch(copy):
        copy.start()
        flying.append(copy)

    def onward(a, dz, dy):
        if shapes[a][0] > 1:
            for dx in range(1, sp):
                launch(xcopy(a, dz, dy, dx))
        launch(ccopy(a, dz, dy, 0))

    for a in range(count):
        for dz in range(1, zs):
            launch(zcopy(a, dz))
        for dy in range(1, ys):
            launch(ycopy(a, 0, dy))
        launch(ccopy(a, 0, 0, 0))
        pltpu.make_async_copy(shards[a], bufs[a], local.at[a]).start()

    got[me] = tiles[me]
    for copy in flying[: fsdp - 1]:
        copy.wait_recv()
    rows = got[:, 0, :].astype(BF16)
    for j in range(8):
        part[:, j, :] = jnp.dot(
            rows, table[:, j * 128 : (j + 1) * 128], preferred_element_type=F32
        )
    part_in[me] = part[me]
    for a in range(count):
        pltpu.make_async_copy(shards[a], bufs[a], local.at[a]).wait()
        pltpu.make_async_copy(bufs[a], outs[a].at[z, y, c], local.at[a]).start()
    second = tiles_start(fsdp, part, part_in, psem.at[0], psem.at[1], lambda ref, to: ref.at[to])
    flying += second

    def over_z(a):
        for dz in range(1, zs):
            zcopy(a, dz).wait_recv()
            for dy in range(1, ys):
                launch(ycopy(a, dz, dy))
            onward(a, dz, 0)

    def over_y(a):
        for dz in range(zs):
            for dy in range(1, ys):
                ycopy(a, dz, dy).wait_recv()
                onward(a, dz, dy)

    def over_x(a):
        if shapes[a][0] > 1:
            for dz in range(zs):
                for dy in range(ys):
                    if dz + dy:
                        for dx in range(1, sp):
                            xcopy(a, dz, dy, dx).wait_recv()
                            launch(ccopy(a, dz, dy, dx))

    for step in range(count + 2):
        if step < count:
            over_z(step)
        if 1 <= step <= count:
            over_y(step - 1)
        if step >= 2:
            over_x(step - 2)
    for copy in second:
        copy.wait_recv()
    total = part_in[0]
    for f in range(1, fsdp):
        total = total + part_in[f]
    scales_out[...] = total
    tiles_out[...] = got[...]
    for a in range(count):
        for dz in range(zs):
            for dy in range(ys):
                many = sp if shapes[a][0] > 1 and dz + dy else 1
                for dx in range(many):
                    ccopy(a, dz, dy, dx).wait_recv()
        pltpu.make_async_copy(bufs[a], outs[a].at[z, y, c], local.at[a]).wait()
    for copy in flying:
        copy.wait_send()


def parts_of(rows, sp):
    return sp if rows % (16 * sp) == 0 else 1


def gather(shards, kinds, tiles, table, fsdp, sp):
    dims = sizes_of(fsdp, sp)
    zs, ys, cs = dims
    count = len(shards)
    split = []
    for shard, kind in zip(shards, kinds, strict=True):
        rows, width = shard.shape
        h = parts_of(rows, sp) if kind else 1
        split.append(shard.reshape(h, rows // h, width))
    shapes = [s.shape for s in split]
    outs = pl.pallas_call(
        functools.partial(gather_kernel, dims, fsdp, sp, shapes),
        out_shape=[jax.ShapeDtypeStruct(dims + s, BF16) for s in shapes]
        + [
            jax.ShapeDtypeStruct((fsdp, 8, 128), F32),
            jax.ShapeDtypeStruct((8, 128), F32),
        ],
        in_specs=[ANY] * count + [VMEM] * 2,
        out_specs=[ANY] * count + [VMEM] * 2,
        scratch_shapes=[pltpu.VMEM(s, BF16) for s in shapes]
        + [pltpu.VMEM((fsdp, 8, 128), F32)] * 3
        + [DMA((count, zs))] * 2
        + [DMA((count, zs, ys))] * 2
        + [DMA((count, zs, ys, sp))] * 4
        + [DMA((count,)), DMA((2, fsdp)), DMA((2, fsdp))],
        compiler_params=params(0),
        name="gather",
    )(*split, tiles, table)
    whole = [
        o.reshape(fsdp * s.shape[0], s.shape[1]) for o, s in zip(outs[:count], shards, strict=True)
    ]
    return whole, outs[count], outs[count + 1]


def add_rows(rows, first, second, put):
    step = 32 if rows % 32 == 0 else (16 if rows % 16 == 0 else 8)

    def body(i, _):
        at = pl.ds(pl.multiple_of(i * step, step), step)
        put(at, first[at, :].astype(F32) + second[at, :].astype(F32))
        return 0

    lax.fori_loop(0, rows // step, body, 0)


def scatter_kernel(dims, fsdp, sp, shapes, modes, *refs):
    zs, ys, cs = dims
    count = len(shapes)
    grads, tiles = refs[:count], refs[count]
    refs = refs[count + 1 :]
    outs, tiles_out, small_out = refs[:count], refs[count], refs[count + 1]
    refs = refs[count + 2 :]
    own, crecvd, xrecvd, yrecvd, zrecvd, last = (
        refs[k * count : (k + 1) * count] for k in range(6)
    )
    refs = refs[6 * count :]
    got, small = refs[0], refs[1]
    csem, xsem, ysem, zsem, fsem, lsem, tsem, ssem = refs[2:]
    me, x = lax.axis_index("fsdp"), lax.axis_index("sp")
    z, y, c = me // (ys * cs), (me // cs) % ys, me % cs

    def dev(zz, yy, cc):
        return ((zz * ys + yy) * cs + cc, x)

    peers = [((me + d) % fsdp, x) for d in range(1, fsdp)]
    peers += [(me, (x + d) % sp) for d in range(1, sp)]
    greet(peers)
    flying = []

    def launch(copy):
        copy.start()
        flying.append(copy)

    first = tiles_start(fsdp, tiles, got, tsem.at[0], tsem.at[1], lambda ref, to: ref.at[to])
    flying += first

    order = [(dz, dy) for dz in range(zs - 1, -1, -1) for dy in range(ys - 1, -1, -1)]

    def where(dz, dy):
        return (z + dz) % zs, (y + dy) % ys

    def ccopy(a, dz, dy):
        zz, yy = where(dz, dy)
        return remote(
            grads[a].at[zz, yy, 1 - c],
            crecvd[a].at[dz, dy],
            csem.at[0, a, dz, dy],
            csem.at[1, a, dz, dy],
            dev(z, y, 1 - c),
        )

    def mine(a, dz, dy):
        zz, yy = where(dz, dy)
        return pltpu.make_async_copy(grads[a].at[zz, yy, c], own[a].at[dz, dy], lsem.at[a, dz, dy])

    def xcopy(a, dz, dy, dx):
        to = (x + dx) % sp
        return remote(
            own[a].at[dz, dy, to],
            xrecvd[a].at[dz, dy, dx - 1],
            xsem.at[0, a, dz, dy, dx],
            xsem.at[1, a, dz, dy, dx],
            (me, to),
        )

    def ycopy(a, dz, dy):
        h = x if shapes[a][0] > 1 else 0
        return remote(
            own[a].at[dz, dy, h],
            yrecvd[a].at[dz, dy - 1],
            ysem.at[0, a, dz, dy],
            ysem.at[1, a, dz, dy],
            dev(z, (y + dy) % ys, c),
        )

    def zcopy(a, dz):
        h = x if shapes[a][0] > 1 else 0
        return remote(
            own[a].at[dz, 0, h],
            zrecvd[a].at[dz - 1],
            zsem.at[0, a, dz],
            zsem.at[1, a, dz],
            dev((z + dz) % zs, y, c),
        )

    def fcopy(a, dx):
        return remote(
            last[a].at[x],
            last[a].at[x],
            fsem.at[0, a, dx],
            fsem.at[1, a, dx],
            (me, (x + dx) % sp),
        )

    def into(ref):
        def put(at, value):
            ref[at, :] = value.astype(BF16)

        return put

    for a in range(count):
        for dz, dy in order:
            launch(ccopy(a, dz, dy))
            mine(a, dz, dy).start()

    def over_c(a):
        h, rows, _ = shapes[a]
        for dz, dy in order:
            mine(a, dz, dy).wait()
            ccopy(a, dz, dy).wait_recv()
            for k in range(h):
                ref = own[a].at[dz, dy, k]
                add_rows(rows, ref, crecvd[a].at[dz, dy, k], into(ref))
            if h > 1:
                for dx in range(1, sp):
                    launch(xcopy(a, dz, dy, dx))

    def over_x(a):
        h, rows, _ = shapes[a]
        for dz, dy in order:
            if h > 1:
                ref = own[a].at[dz, dy, x]
                for dx in range(1, sp):
                    xcopy(a, dz, dy, dx).wait_recv()
                    add_rows(rows, ref, xrecvd[a].at[dz, dy, dx - 1], into(ref))
            if dy:
                launch(ycopy(a, dz, dy))

    def over_y(a):
        h, rows, _ = shapes[a]
        k = x if h > 1 else 0
        for dz in range(zs - 1, -1, -1):
            ref = own[a].at[dz, 0, k]
            for dy in range(1, ys):
                ycopy(a, dz, dy).wait_recv()
                add_rows(rows, ref, yrecvd[a].at[dz, dy - 1], into(ref))
            if dz:
                launch(zcopy(a, dz))

    def over_z(a):
        h, rows, _ = shapes[a]
        k = x if h > 1 else 0
        ref = own[a].at[0, 0, k]
        for dz in range(1, zs):
            zcopy(a, dz).wait_recv()
            target = last[a].at[x] if dz == zs - 1 else ref
            add_rows(rows, ref, zrecvd[a].at[dz - 1], into(target))
        if zs == 1:
            last[a][x] = ref[...]
        for dx in range(1, sp):
            launch(fcopy(a, dx))

    for step in range(count + 3):
        if step < count:
            over_c(step)
        if 1 <= step <= count:
            over_x(step - 1)
        if 2 <= step <= count + 1:
            over_y(step - 2)
        if step >= 3:
            over_z(step - 3)

    got[me] = tiles[me]
    for copy in first:
        copy.wait_recv()
    total = got[0]
    for f in range(1, fsdp):
        total = total + got[f]
    small[x] = total
    for dx in range(1, sp):
        launch(remote(small.at[x], small.at[x], ssem.at[0, dx], ssem.at[1, dx], (me, (x + dx) % sp)))
    tiles_out[...] = got[...]
    for a in range(count):
        for dx in range(1, sp):
            fcopy(a, dx).wait_recv()
        if modes[a] == "add" and shapes[a][0] == 1:
            value = last[a][0].astype(F32)
            for k in range(1, sp):
                value = value + last[a][k].astype(F32)
            outs[a][0] = value
        else:
            for k in range(sp):
                outs[a][k] = last[a][k].astype(F32)
    for dx in range(1, sp):
        remote(
            small.at[x], small.at[x], ssem.at[0, dx], ssem.at[1, dx], (me, (x + dx) % sp)
        ).wait_recv()
    total = small[0]
    for k in range(1, sp):
        total = total + small[k]
    small_out[...] = total
    for copy in flying:
        copy.wait_send()


def scatter(grads, modes, tiles, fsdp, sp):
    dims = sizes_of(fsdp, sp)
    zs, ys, cs = dims
    count = len(grads)
    split, shapes, outs = [], [], []
    for grad, mode in zip(grads, modes, strict=True):
        rows, width = grad.shape[0] // fsdp, grad.shape[1]
        h = parts_of(rows, sp) if mode == "add" else 1
        shapes.append((h, rows // h, width))
        split.append(grad.reshape(dims + (h, rows // h, width)))
        copies = 1 if mode == "add" and h == 1 else sp
        outs.append(jax.ShapeDtypeStruct((copies, rows // h, width), F32))

    def scratch(shape):
        return pltpu.VMEM(shape, BF16)

    results = pl.pallas_call(
        functools.partial(scatter_kernel, dims, fsdp, sp, shapes, modes),
        out_shape=outs
        + [jax.ShapeDtypeStruct((fsdp, 8, 128), F32), jax.ShapeDtypeStruct((8, 128), F32)],
        in_specs=[ANY] * count + [VMEM],
        out_specs=[VMEM] * (count + 2),
        scratch_shapes=[scratch((zs, ys) + s) for s in shapes]
        + [scratch((zs, ys) + s) for s in shapes]
        + [scratch((zs, ys, sp - 1) + s[1:] if s[0] > 1 else (1, 1, 1, 16, 128)) for s in shapes]
        + [scratch((zs, max(ys - 1, 1)) + s[1:]) for s in shapes]
        + [scratch((max(zs - 1, 1),) + s[1:]) for s in shapes]
        + [scratch((sp,) + s[1:]) for s in shapes]
        + [pltpu.VMEM((fsdp, 8, 128), F32), pltpu.VMEM((sp, 8, 128), F32)]
        + [
            DMA((2, count, zs, ys)),
            DMA((2, count, zs, ys, sp)),
            DMA((2, count, zs, ys)),
            DMA((2, count, zs)),
            DMA((2, count, sp)),
            DMA((count, zs, ys)),
            DMA((2, fsdp)),
            DMA((2, sp)),
        ],
        compiler_params=params(4),
        name="scatter",
    )(*split, tiles)
    return results[:count], results[count], results[count + 1]


def lane_groups(values):
    lane = lax.broadcasted_iota(jnp.int32, values.shape, 1)
    step = 1
    while step < C // GROUPS:
        up = pltpu.roll(values, step, 1)
        down = pltpu.roll(values, C - step, 1)
        values = values + jnp.where((lane & step) != 0, up, down)
        step *= 2
    return values


def column_sums(rows, fields):
    probe = jax.eval_shape(lambda: fields(0))

    def body(r, sums):
        return tuple(
            s + jnp.sum(v.reshape(-1, 8, C), axis=0) for s, v in zip(sums, fields(r), strict=True)
        )

    sums = lax.fori_loop(0, rows, body, tuple(jnp.zeros((8, C), F32) for _ in probe))
    return [jnp.broadcast_to(jnp.sum(s, axis=0, keepdims=True), (8, C)) for s in sums]


def stack_rows(*values):
    row = lax.broadcasted_iota(jnp.int32, (8, C), 0)
    out = jnp.zeros((8, C), F32)
    for k, value in enumerate(values):
        out = jnp.where(row == k, value, out)
    return out


class Swap:
    def __init__(self, sp, sums, ssem, hsem):
        self.sp, self.sums, self.ssem, self.hsem = sp, sums, ssem, hsem
        self.me, self.x = lax.axis_index("fsdp"), lax.axis_index("sp")

    def peers(self):
        return [(self.me, (self.x + d) % self.sp) for d in range(1, self.sp)]

    def _sums(self, k, d):
        return remote(
            self.sums.at[k, self.x],
            self.sums.at[k, self.x],
            self.ssem.at[0, k, d],
            self.ssem.at[1, k, d],
            (self.me, (self.x + d) % self.sp),
        )

    def sums_start(self, k, value):
        self.sums[k, self.x] = value
        for d in range(1, self.sp):
            self._sums(k, d).start()

    def sums_wait(self, k):
        for d in range(1, self.sp):
            self._sums(k, d).wait()
        return [self.sums[k, i] for i in range(self.sp)]

    def _up(self, k, src, dst):
        to = (self.x + self.sp - 1) % self.sp
        return remote(src, dst.at[1], self.hsem.at[0, k, 0], self.hsem.at[1, k, 0], (self.me, to))

    def _down(self, k, src, dst):
        to = (self.x + 1) % self.sp
        return remote(src, dst.at[0], self.hsem.at[0, k, 1], self.hsem.at[1, k, 1], (self.me, to))

    def edges_start(self, k, top, bottom, dst):
        @pl.when(self.x > 0)
        def _():
            self._up(k, top, dst).start()

        @pl.when(self.x < self.sp - 1)
        def _():
            self._down(k, bottom, dst).start()

    def edges_wait(self, k, top, bottom, dst):
        @pl.when(self.x > 0)
        def _():
            self._up(k, top, dst).wait_send()
            self._down(k, bottom, dst).wait_recv()

        @pl.when(self.x < self.sp - 1)
        def _():
            self._down(k, bottom, dst).wait_send()
            self._up(k, top, dst).wait_recv()


def put_shifted(dst, at, value):
    columns = value.shape[0]
    col = lax.broadcasted_iota(jnp.int32, value.shape, 0)
    dst[1, at] = value.astype(BF16)
    dst[0, at] = jnp.where(col == 0, 0.0, pltpu.roll(value, 1, 0)).astype(BF16)
    dst[2, at] = jnp.where(col == columns - 1, 0.0, pltpu.roll(value, columns - 1, 0)).astype(BF16)


def taps(rows, columns, shifted, weight, acc, back):
    pixels = rows * columns

    def body(t, _):
        total = None
        for dc in range(3):
            if back:
                lhs = shifted[2 - dc, pl.ds(2 - t, rows)].reshape(pixels, C)
            else:
                lhs = shifted[dc, pl.ds(t, rows)].reshape(pixels, C)
            rhs = weight[pl.ds(pl.multiple_of((3 * t + dc) * C, C), C), :]
            out = lax.dot_general(
                lhs, rhs, (((1,), (1 if back else 0,)), ((), ())), preferred_element_type=F32
            )
            total = out if total is None else total + out
        total = total.reshape(rows, columns, C)

        @pl.when(t == 0)
        def _():
            acc[...] = total

        @pl.when(t > 0)
        def _():
            acc[...] += total

        return 0

    lax.fori_loop(0, 3, body, 0)


def numbers(height, rows, columns, sp):
    x = lax.axis_index("sp")
    ids = x * rows + jnp.arange(-1, rows + 1, dtype=jnp.int32)
    valid = ((ids >= 0) & (ids < height)).astype(F32)
    count = (height * columns * (C // GROUPS)).astype(F32)
    held = jnp.clip(height - rows * jnp.arange(sp, dtype=jnp.int32), 0, rows)
    held = (held * columns * (C // GROUPS)).astype(F32)
    bias = jnp.where(jnp.arange(sp * rows, dtype=jnp.int32) < height, 0.0, MASKED).astype(F32)
    return jnp.concatenate([valid, count[None], held, held[x][None], bias])


def local_moments(rows, field, mask, held):
    (total,) = column_sums(rows, lambda r: (field(r),))
    total = lane_groups(total)
    mean = (total / jnp.maximum(held, 1.0))[:1]

    def centred(r):
        v = (field(r) - mean) * mask(r)
        return (v * v,)

    (square,) = column_sums(rows, centred)
    return stack_rows(total, lane_groups(square))


def joint_moments(members, counts, count):
    mean = members[0][:1]
    for m in members[1:]:
        mean = mean + m[:1]
    mean = mean / count
    square = None
    for m, n in zip(members, counts, strict=True):
        off = m[:1] / jnp.maximum(n, 1.0) - mean
        term = m[1:2] + n * off * off
        square = term if square is None else square + term
    return mean, lax.rsqrt(square / count + EPSILON)


def forward_kernel(
    sp,
    nums,
    image,
    gains,
    scales,
    w1,
    w2,
    resid,
    normed,
    conv_out,
    s1,
    s2,
    stats,
    w1v,
    w2v,
    edge1,
    edge2,
    acc,
    sums,
    ssem,
    hsem,
    wsem,
):
    rows, columns = image.shape[0], image.shape[1]
    swap = Swap(sp, sums, ssem, hsem)
    load1 = pltpu.make_async_copy(w1, w1v, wsem.at[0])
    load2 = pltpu.make_async_copy(w2, w2v, wsem.at[1])
    load1.start()
    load2.start()
    edge1[...] = jnp.zeros_like(edge1)
    edge2[...] = jnp.zeros_like(edge2)
    greet(swap.peers())
    swap.edges_start(0, image.at[0], image.at[rows - 1], edge1)
    count = nums[rows + 2]
    counts = [nums[rows + 3 + i] for i in range(sp)]
    held = nums[rows + 3 + sp]

    def mask(r):
        return nums[r + 1]

    def masked(r):
        return image[r].astype(F32) * mask(r)

    swap.sums_start(0, local_moments(rows, masked, mask, held))
    mean1, inv1 = joint_moments(swap.sums_wait(0), counts, count)
    swap.edges_wait(0, image.at[0], image.at[rows - 1], edge1)
    g1, g2, g3 = gains[0:1], gains[1:2], gains[2:3]

    def first(at, value):
        m = nums[at]
        hidden = (value.astype(F32) * m - mean1) * m * inv1 * g1
        put_shifted(s1, at, hidden * jax.nn.sigmoid(hidden) * m)

    lax.fori_loop(0, rows, lambda r, _: (first(r + 1, image[r]), 0)[1], 0)
    first(0, edge1[0])
    first(rows + 1, edge1[1])
    load1.wait()
    taps(rows, columns, s1, w1v, acc, False)

    def keep(r, _):
        conv_out[r] = acc[r] * mask(r)
        return 0

    lax.fori_loop(0, rows, keep, 0)
    swap.edges_start(1, conv_out.at[0], conv_out.at[rows - 1], edge2)
    swap.sums_start(1, local_moments(rows, lambda r: conv_out[r], mask, held))
    mean2, inv2 = joint_moments(swap.sums_wait(1), counts, count)
    swap.edges_wait(1, conv_out.at[0], conv_out.at[rows - 1], edge2)
    scale, shift = 1.0 + scales[0:1], scales[1:2]

    def second(at, value):
        m = nums[at]
        hidden = (value - mean2) * m * inv2 * g2 * scale + shift
        put_shifted(s2, at, hidden * jax.nn.sigmoid(hidden) * m)

    lax.fori_loop(0, rows, lambda r, _: (second(r + 1, conv_out[r]), 0)[1], 0)
    second(0, edge2[0])
    second(rows + 1, edge2[1])
    load2.wait()
    taps(rows, columns, s2, w2v, acc, False)

    def add(r, _):
        resid[r] = masked(r) + acc[r] * mask(r)
        return 0

    lax.fori_loop(0, rows, add, 0)
    swap.sums_start(2, local_moments(rows, lambda r: resid[r], mask, held))
    mean3, inv3 = joint_moments(swap.sums_wait(2), counts, count)

    def third(r, _):
        normed[r] = ((resid[r] - mean3) * mask(r) * inv3 * g3).astype(BF16)
        return 0

    lax.fori_loop(0, rows, third, 0)
    stats[...] = stack_rows(mean1, inv1, mean2, inv2, mean3, inv3)


def forward(nums, image, gains, scales, w1, w2, sp):
    rows, columns, _ = image.shape
    field = (rows, columns, C)
    shifted = (3, rows + 2, columns, C)
    return pl.pallas_call(
        functools.partial(forward_kernel, sp),
        out_shape=[
            jax.ShapeDtypeStruct(field, F32),
            jax.ShapeDtypeStruct(field, BF16),
            jax.ShapeDtypeStruct(field, F32),
            jax.ShapeDtypeStruct(shifted, BF16),
            jax.ShapeDtypeStruct(shifted, BF16),
            jax.ShapeDtypeStruct((8, C), F32),
        ],
        in_specs=[SMEM, VMEM, VMEM, VMEM, ANY, ANY],
        out_specs=[VMEM] * 6,
        scratch_shapes=[
            pltpu.VMEM(w1.shape, BF16),
            pltpu.VMEM(w2.shape, BF16),
            pltpu.VMEM((2, columns, C), BF16),
            pltpu.VMEM((2, columns, C), F32),
            pltpu.VMEM(field, F32),
            pltpu.VMEM((3, sp, 8, C), F32),
            DMA((2, 3, sp)),
            DMA((2, 2, 2)),
            DMA((2,)),
        ],
        compiler_params=params(1),
        name="forward",
    )(nums, image, gains, scales, w1, w2)


def attention_kernel(
    sp,
    heads,
    nums,
    normed,
    text,
    wq,
    wt,
    wo,
    cot,
    resid,
    output,
    gnorm,
    gq,
    gt,
    go,
    gtext,
    nall,
    gown,
    gall,
    qkv,
    keys,
    values,
    dk,
    dv,
    att,
    attin,
    dqkv,
    gtkv,
    gpart,
    grecv,
    tpart,
    low,
    nsem,
    gsem,
    asem,
    psem,
    tsem,
):
    rows, columns = cot.shape[0], cot.shape[1]
    pixels = rows * columns
    width = heads * HEAD
    total_px = sp * pixels
    me, x = lax.axis_index("fsdp"), lax.axis_index("sp")
    factor = HEAD**-0.5
    greet([(me, (x + d) % sp) for d in range(1, sp)])

    def send(pair, src, dst):
        def copy(d):
            to = (x + d) % sp
            return remote(src(to), dst.at[x], pair.at[0, d], pair.at[1, d], (me, to))

        return [copy(d) for d in range(1, sp)]

    def start(copies):
        for copy in copies:
            copy.start()

    def wait(copies):
        for copy in copies:
            copy.wait()

    moves = send(nsem, lambda to: normed, nall)
    start(moves)

    def lower(r, _):
        low[r] = (cot[r].astype(F32) * nums[r + 1]).astype(BF16)
        return 0

    lax.fori_loop(0, rows, lower, 0)
    low2 = low[...].reshape(pixels, C)
    for k in range(sp):
        gown[k] = lax.dot_general(
            low2,
            wo[k * width : (k + 1) * width, :],
            (((1,), (1,)), ((), ())),
            preferred_element_type=F32,
        ).astype(BF16)
    gmoves = send(gsem, lambda to: gown.at[to], gall)
    start(gmoves)
    gall[x] = gown[x]
    nall[x] = normed[...]
    text_kv = jnp.dot(text[...], wt[...], preferred_element_type=F32).astype(BF16)
    keys[total_px:, :] = text_kv[:, :width]
    values[total_px:, :] = text_kv[:, width:]

    def project(k):
        out = jnp.dot(nall[k], wq[...], preferred_element_type=F32).astype(BF16)
        at = pl.ds(pl.multiple_of(k * pixels, pixels), pixels)
        qkv[at, :] = out
        keys[at, :] = out[:, width : 2 * width]
        values[at, :] = out[:, 2 * width :]

    project(x)
    wait(moves)
    for d in range(1, sp):
        project((x + d) % sp)
    wait(gmoves)

    block = 256
    per = pixels // block
    for h in range(heads):
        lanes = slice(h * HEAD, (h + 1) * HEAD)
        kh, vh = keys[:, lanes], values[:, lanes]
        kt, vt = kh.T, vh.T
        dk[...] = jnp.zeros_like(dk)
        dv[...] = jnp.zeros_like(dv)

        def step(j, _, lanes=lanes, kh=kh, vh=vh, kt=kt, vt=vt):
            at = pl.ds(pl.multiple_of(j * block, block), block)
            inner = pl.ds(pl.multiple_of((j % per) * block, block), block)
            q = qkv[at, lanes]
            g = gall[j // per, inner, lanes]
            s = (
                lax.dot_general(kh, q, (((1,), (1,)), ((), ())), preferred_element_type=F32)
                * factor
            )
            pieces = [
                s[r * columns : (r + 1) * columns] + nums[rows + 4 + sp + r]
                for r in range(sp * rows)
            ]
            s = jnp.concatenate(pieces + [s[total_px:]], axis=0)
            raised = jnp.exp(s - jnp.max(s, axis=0, keepdims=True))
            chances = raised * (1.0 / jnp.sum(raised, axis=0, keepdims=True))
            short = chances.astype(BF16)
            att[j // per, inner, lanes] = jnp.dot(
                vt, short, preferred_element_type=F32
            ).T.astype(BF16)
            slope = lax.dot_general(vh, g, (((1,), (1,)), ((), ())), preferred_element_type=F32)
            mean = jnp.sum(chances * slope, axis=0, keepdims=True)
            grad = (chances * (slope - mean)).astype(BF16)
            dqkv[at, lanes] = (jnp.dot(kt, grad, preferred_element_type=F32) * factor).T.astype(
                BF16
            )
            dk[...] += jnp.dot(grad, q, preferred_element_type=F32)
            dv[...] += jnp.dot(short, g, preferred_element_type=F32)
            return 0

        lax.fori_loop(0, sp * per, step, 0)
        low_k = (dk[...] * factor).astype(BF16)
        low_v = dv[...].astype(BF16)
        dqkv[:, width + h * HEAD : width + (h + 1) * HEAD] = low_k[:total_px]
        dqkv[:, 2 * width + h * HEAD : 2 * width + (h + 1) * HEAD] = low_v[:total_px]
        gtkv[:, h * HEAD : (h + 1) * HEAD] = low_k[total_px:]
        gtkv[:, width + h * HEAD : width + (h + 1) * HEAD] = low_v[total_px:]

    amoves = send(asem, lambda to: att.at[to], attin)
    start(amoves)
    attin[x] = att[x]

    def to_normed(k):
        at = pl.ds(pl.multiple_of(k * pixels, pixels), pixels)
        return lax.dot_general(
            dqkv[at, :], wq[...], (((1,), (1,)), ((), ())), preferred_element_type=F32
        )

    for d in range(1, sp):
        to = (x + d) % sp
        gpart[to] = to_normed(to).astype(BF16)
    pmoves = send(psem, lambda to: gpart.at[to], grecv)
    start(pmoves)
    tpart[x] = lax.dot_general(
        gtkv[...], wt[...], (((1,), (1,)), ((), ())), preferred_element_type=F32
    ).astype(BF16)
    tmoves = send(tsem, lambda to: tpart.at[x], tpart)
    start(tmoves)
    gnorm[...] = to_normed(x)
    wait(amoves)
    joined = jnp.concatenate([attin[k] for k in range(sp)], axis=1)
    branch = jnp.dot(joined, wo[...], preferred_element_type=F32)
    for r in range(rows):
        at = slice(r * columns, (r + 1) * columns)
        output[at, :] = (resid[at, :] + branch[at] * nums[r + 1]).astype(BF16)
    down = (((0,), (0,)), ((), ()))
    go[...] = lax.dot_general(joined, low2, down, preferred_element_type=F32).astype(BF16)
    gq[...] = lax.dot_general(
        nall[...].reshape(total_px, C), dqkv[...], down, preferred_element_type=F32
    ).astype(BF16)
    gt[...] = lax.dot_general(text[...], gtkv[...], down, preferred_element_type=F32).astype(BF16)
    wait(pmoves)
    for d in range(1, sp):
        gnorm[...] += grecv[(x + d) % sp].astype(F32)
    wait(tmoves)
    total = tpart[0].astype(F32)
    for k in range(1, sp):
        total = total + tpart[k].astype(F32)
    gtext[...] = total


def attention(nums, normed, text, wq, wt, wo, cot, resid, sp):
    rows, columns, _ = cot.shape
    pixels = rows * columns
    heads = C // HEAD // sp
    width = heads * HEAD
    tokens, wide = text.shape
    n_keys = sp * pixels + tokens
    return pl.pallas_call(
        functools.partial(attention_kernel, sp, heads),
        out_shape=[
            jax.ShapeDtypeStruct((pixels, C), BF16),
            jax.ShapeDtypeStruct((pixels, C), F32),
            jax.ShapeDtypeStruct(wq.shape, BF16),
            jax.ShapeDtypeStruct(wt.shape, BF16),
            jax.ShapeDtypeStruct(wo.shape, BF16),
            jax.ShapeDtypeStruct(text.shape, F32),
        ],
        in_specs=[SMEM] + [VMEM] * 7,
        out_specs=[VMEM] * 6,
        scratch_shapes=[
            pltpu.VMEM((sp, pixels, C), BF16),
            pltpu.VMEM((sp, pixels, width), BF16),
            pltpu.VMEM((sp, pixels, width), BF16),
            pltpu.VMEM((sp * pixels, 3 * width), BF16),
            pltpu.VMEM((n_keys, width), BF16),
            pltpu.VMEM((n_keys, width), BF16),
            pltpu.VMEM((n_keys, HEAD), F32),
            pltpu.VMEM((n_keys, HEAD), F32),
            pltpu.VMEM((sp, pixels, width), BF16),
            pltpu.VMEM((sp, pixels, width), BF16),
            pltpu.VMEM((sp * pixels, 3 * width), BF16),
            pltpu.VMEM((tokens, 2 * width), BF16),
            pltpu.VMEM((sp, pixels, C), BF16),
            pltpu.VMEM((sp, pixels, C), BF16),
            pltpu.VMEM((sp, tokens, wide), BF16),
            pltpu.VMEM((rows, columns, C), BF16),
        ]
        + [DMA((2, sp))] * 5,
        compiler_params=params(2),
        name="attention",
    )(nums, normed, text, wq, wt, wo, cot, resid)


def backward_kernel(
    fsdp,
    sp,
    nums,
    image,
    gains,
    scales,
    stats,
    resid,
    conv_out,
    s1,
    s2,
    gnorm,
    cot,
    w1,
    w2,
    gw1,
    gw2,
    gimage,
    ggains,
    gscales,
    w1v,
    w2v,
    out1,
    out2,
    p1,
    p2,
    edge1,
    edge2,
    gres,
    acc,
    sums,
    mine,
    every,
    ssem,
    hsem,
    wsem,
    osem,
    tsem,
):
    rows, columns = image.shape[0], image.shape[1]
    pixels = rows * columns
    me, x = lax.axis_index("fsdp"), lax.axis_index("sp")
    swap = Swap(sp, sums, ssem, hsem)
    load1 = pltpu.make_async_copy(w1, w1v, wsem.at[0])
    load2 = pltpu.make_async_copy(w2, w2v, wsem.at[1])
    load2.start()
    load1.start()
    edge1[...] = jnp.zeros_like(edge1)
    edge2[...] = jnp.zeros_like(edge2)
    greet(swap.peers() + [((me + d) % fsdp, x) for d in range(1, fsdp)])
    count = nums[rows + 2]
    g1, g2, g3 = gains[0:1], gains[1:2], gains[2:3]
    mean1, inv1, mean2, inv2, mean3, inv3 = (stats[k : k + 1] for k in range(6))

    def mask(r):
        return nums[r + 1]

    def joint(k):
        members = swap.sums_wait(k)
        total = members[0]
        for m in members[1:]:
            total = total + m
        return total

    def weight_grad(shifted, padded, store, target, sem):
        grad = padded[1, 1 : rows + 1].reshape(pixels, C)

        def body(t, _):
            for dc in range(3):
                lhs = shifted[dc, pl.ds(t, rows)].reshape(pixels, C)
                at = pl.ds(pl.multiple_of((3 * t + dc) * C, C), C)
                store[at, :] = lax.dot_general(
                    lhs, grad, (((0,), (0,)), ((), ())), preferred_element_type=F32
                ).astype(BF16)
            return 0

        lax.fori_loop(0, 3, body, 0)
        pltpu.make_async_copy(store, target, sem).start()

    def hat3(r):
        return (resid[r] - mean3) * mask(r) * inv3

    def from_three(r):
        g = gnorm[r] * mask(r)
        return g, g * hat3(r)

    plain, crossed = column_sums(rows, from_three)
    gain3 = crossed
    swap.sums_start(0, stack_rows(lane_groups(plain * g3), lane_groups(crossed * g3)))
    total = joint(0) / count
    m1, m2 = total[0:1], total[1:2]

    def residual(r, _):
        m = mask(r)
        e = gnorm[r] * m * g3
        value = cot[r].astype(F32) * m + m * inv3 * (e - m1 - hat3(r) * m2)
        gres[r] = value
        put_shifted(p2, r + 1, value * m)
        return 0

    lax.fori_loop(0, rows, residual, 0)
    swap.edges_start(0, p2.at[1, 1], p2.at[1, rows], edge2)
    weight_grad(s2, p2, out2, gw2, osem.at[0])
    swap.edges_wait(0, p2.at[1, 1], p2.at[1, rows], edge2)
    put_shifted(p2, 0, edge2[0].astype(F32))
    put_shifted(p2, rows + 1, edge2[1].astype(F32))
    load2.wait()
    taps(rows, columns, p2, w2v, acc, True)
    scale, shift = 1.0 + scales[0:1], scales[1:2]

    def hat2(r):
        return (conv_out[r] - mean2) * mask(r) * inv2

    def slope(value):
        s = jax.nn.sigmoid(value)
        return s * (1.0 + value * (1.0 - s))

    def from_two(r):
        hat = hat2(r)
        g = acc[r] * mask(r) * slope(hat * g2 * scale + shift)
        acc[r] = g
        return g, g * hat

    plain, crossed = column_sums(rows, from_two)
    gain2 = crossed * scale
    swap.sums_start(
        1,
        stack_rows(
            lane_groups(plain * (scale * g2)),
            lane_groups(crossed * (scale * g2)),
            crossed * g2,
            plain,
        ),
    )
    total = joint(1)
    for k in range(8):
        row = 2 + k // 4
        lanes = slice((k % 4) * 128, (k % 4 + 1) * 128)
        mine[k : k + 1, :] = total[row : row + 1, lanes].astype(BF16).astype(F32)
    copies = tiles_start(fsdp, mine, every, tsem.at[0], tsem.at[1], lambda ref, to: ref)
    every[me] = mine[...]
    m1, m2 = total[0:1] / count, total[1:2] / count

    def middle(r, _):
        m = mask(r)
        value = m * inv2 * (acc[r] * (scale * g2) - m1 - hat2(r) * m2)
        put_shifted(p1, r + 1, value)
        return 0

    lax.fori_loop(0, rows, middle, 0)
    swap.edges_start(1, p1.at[1, 1], p1.at[1, rows], edge1)
    weight_grad(s1, p1, out1, gw1, osem.at[1])
    swap.edges_wait(1, p1.at[1, 1], p1.at[1, rows], edge1)
    put_shifted(p1, 0, edge1[0].astype(F32))
    put_shifted(p1, rows + 1, edge1[1].astype(F32))
    load1.wait()
    taps(rows, columns, p1, w1v, acc, True)

    def hat1(r):
        return (image[r].astype(F32) * mask(r) - mean1) * mask(r) * inv1

    def from_one(r):
        hat = hat1(r)
        g = acc[r] * mask(r) * slope(hat * g1)
        acc[r] = g
        return g, g * hat

    plain, crossed = column_sums(rows, from_one)
    swap.sums_start(2, stack_rows(lane_groups(plain * g1), lane_groups(crossed * g1)))
    ggains[...] = stack_rows(crossed, gain2, gain3)
    total = joint(2) / count
    m1, m2 = total[0:1], total[1:2]

    def final(r, _):
        m = mask(r)
        gimage[r] = (gres[r] + m * inv1 * (acc[r] * g1 - m1 - hat1(r) * m2)) * m
        return 0

    lax.fori_loop(0, rows, final, 0)
    for copy in copies:
        copy.wait()
    gscales[...] = every[...]
    pltpu.make_async_copy(out2, gw2, osem.at[0]).wait()
    pltpu.make_async_copy(out1, gw1, osem.at[1]).wait()


def backward(nums, image, gains, scales, stats, resid, conv_out, s1, s2, gnorm, cot, w1, w2, fsdp, sp):
    rows, columns, _ = image.shape
    field = (rows, columns, C)
    shifted = (3, rows + 2, columns, C)
    return pl.pallas_call(
        functools.partial(backward_kernel, fsdp, sp),
        out_shape=[
            jax.ShapeDtypeStruct(w1.shape, BF16),
            jax.ShapeDtypeStruct(w2.shape, BF16),
            jax.ShapeDtypeStruct(field, F32),
            jax.ShapeDtypeStruct((8, C), F32),
            jax.ShapeDtypeStruct((fsdp, 8, 128), F32),
        ],
        in_specs=[SMEM] + [VMEM] * 10 + [ANY, ANY],
        out_specs=[ANY, ANY, VMEM, VMEM, VMEM],
        scratch_shapes=[
            pltpu.VMEM(w1.shape, BF16),
            pltpu.VMEM(w2.shape, BF16),
            pltpu.VMEM(w1.shape, BF16),
            pltpu.VMEM(w2.shape, BF16),
            pltpu.VMEM(shifted, BF16),
            pltpu.VMEM(shifted, BF16),
            pltpu.VMEM((2, columns, C), BF16),
            pltpu.VMEM((2, columns, C), BF16),
            pltpu.VMEM(field, F32),
            pltpu.VMEM(field, F32),
            pltpu.VMEM((3, sp, 8, C), F32),
            pltpu.VMEM((8, 128), F32),
            pltpu.VMEM((fsdp, 8, 128), F32),
            DMA((2, 3, sp)),
            DMA((2, 2, 2)),
            DMA((2,)),
            DMA((2,)),
            DMA((2, fsdp)),
        ],
        compiler_params=params(3),
        name="backward",
    )(nums, image, gains, scales, stats, resid, conv_out, s1, s2, gnorm, cot, w1, w2)


def per_device(
    image,
    embedding,
    text,
    heights,
    gain_one,
    conv_one,
    emb_proj,
    gain_two,
    conv_two,
    gain_three,
    qkv_proj,
    text_proj,
    out_proj,
    cotangent,
):
    rows, columns = image.shape[1], image.shape[2]
    fsdp, sp = lax.axis_size("fsdp"), lax.axis_size("sp")
    x = lax.axis_index("sp")
    heads = C // HEAD // sp
    width = heads * HEAD
    share = gain_one.shape[0]
    emb_rows = emb_proj.shape[0]
    nums = numbers(heights[0], rows, columns, sp)
    emb_float = embedding.astype(F32)
    emb_act = jax.nn.silu(emb_float).astype(BF16)

    def columns_of(weight, kinds):
        blocks = weight.reshape(weight.shape[0], kinds, sp, width)
        return lax.dynamic_index_in_dim(blocks, x, 2, keepdims=False).reshape(weight.shape[0], -1)

    def lanes(array):
        return jnp.pad(array, [(0, 0)] * (array.ndim - 1) + [(0, 128 - array.shape[-1])])

    gains_row = jnp.concatenate([gain_one, gain_two, gain_three]).astype(F32)
    tiles = jnp.stack(
        [
            lanes(emb_act.astype(F32).reshape(fsdp, emb_rows)),
            jnp.broadcast_to(lanes(gains_row[None]), (fsdp, 128)),
        ],
        axis=1,
    )
    tiles = jnp.pad(tiles, ((0, 0), (0, 6), (0, 0)))
    table = jnp.pad(emb_proj, ((0, 128 - emb_rows), (0, 0)))
    (w1, w2, wq, wt, wo), tiles_in, scales = gather(
        [
            conv_one,
            conv_two,
            columns_of(qkv_proj, 3),
            columns_of(text_proj, 2),
            out_proj,
        ],
        [True, True, False, False, True],
        tiles,
        table,
        fsdp,
        sp,
    )
    scales = scales.reshape(2, C)
    gains = tiles_in[:, 1, : 3 * share].reshape(fsdp, 3, share).transpose(1, 0, 2).reshape(3, C)
    emb_cols = tiles_in[:, 0, :emb_rows].astype(BF16)
    pixels = rows * columns
    resid, normed, conv_out, s1, s2, stats = forward(nums, image[0], gains, scales, w1, w2, sp)
    output, gnorm, gq, gt, go, gtext = attention(
        nums,
        normed.reshape(pixels, C),
        text[0],
        wq,
        wt,
        wo,
        cotangent[0],
        resid.reshape(pixels, C),
        sp,
    )
    gw1, gw2, gimage, ggains, every = backward(
        nums,
        image[0],
        gains,
        scales,
        stats,
        resid,
        conv_out,
        s1,
        s2,
        gnorm.reshape(rows, columns, C),
        cotangent[0],
        w1,
        w2,
        fsdp,
        sp,
    )
    grad_scales = every.reshape(fsdp, 2 * C).astype(BF16)
    grad_emb_proj = lax.dot_general(
        emb_cols, grad_scales, (((0,), (0,)), ((), ())), preferred_element_type=F32
    )
    piece = lax.dot_general(
        grad_scales, emb_proj, (((1,), (1,)), ((), ())), preferred_element_type=F32
    )
    gain_tiles = ggains[:3].reshape(3, fsdp, share).transpose(1, 0, 2).reshape(fsdp, 3 * share)
    tiles = jnp.stack([lanes(piece), lanes(gain_tiles)], axis=1)
    tiles = jnp.pad(tiles, ((0, 0), (0, 6), (0, 0)))
    (r1, r2, rq, rt, ro), tiles_in, small = scatter(
        [gw1, gw2, gq, gt, go], ["add", "add", "join", "join", "add"], tiles, fsdp, sp
    )

    def joined(result, kinds):
        n = result.shape[1]
        return result.reshape(sp, n, kinds, width).transpose(1, 2, 0, 3).reshape(n, kinds * C)

    grad_embedding = tiles_in[:, 0, :emb_rows].reshape(1, -1)
    sigmoid = jax.nn.sigmoid(emb_float)
    grad_embedding = grad_embedding * (sigmoid * (1.0 + emb_float * (1.0 - sigmoid)))
    gain_sums = small[1, : 3 * share].reshape(3, share)
    return (
        output.reshape(1, rows, columns, C),
        gimage[None],
        grad_embedding,
        gtext[None],
        gain_sums[0],
        r1.reshape(-1, C),
        grad_emb_proj,
        gain_sums[1],
        r2.reshape(-1, C),
        gain_sums[2],
        joined(rq, 3),
        joined(rt, 2),
        ro.reshape(-1, C),
    )


def solution(mesh):
    weight = P("fsdp", None)
    gain = P("fsdp")
    field = P("fsdp", "sp", None, None)
    in_specs = (
        field,
        P("fsdp", None),
        P("fsdp", None, None),
        gain,
        gain,
        weight,
        weight,
        gain,
        weight,
        gain,
        weight,
        weight,
        weight,
        field,
    )
    out_specs = (
        field,
        field,
        P("fsdp", None),
        P("fsdp", None, None),
        gain,
        weight,
        weight,
        gain,
        weight,
        gain,
        weight,
        weight,
        weight,
    )
    return jax.shard_map(
        per_device, mesh=mesh, in_specs=in_specs, out_specs=out_specs, check_vma=False
    )
```

time: 1150 us -> 383 us (0.33)
  waiting for transfers between devices: 632 us -> 0 us
  Pallas kernels: 0 us -> 349 us
  matrix products: 187 us -> 1.21 us
  blocking collectives: 144 us -> 0 us
  local copies, waits for them, and re-layouts: 83 us -> 25.9 us
  other arithmetic: 59.3 us -> 5.27 us
  starting transfers between devices: 16.8 us -> 0 us
  between operations: 16.6 us -> 1.46 us
    reduce_scatter x7 -> x0, waiting for transfers between devices: 474 us -> none  [the longest x1 113 us: per_device(): lax.psum_scatter(grad_conv_two_w, 'fsdp', scatter_dimension=0, tiled=True)]
    pallas_call x0 -> x5, Pallas kernels: none -> 349 us  [the longest x1 111 us: scatter(): pl.pallas_call(functools.partial(scatter_kernel, dims, fsdp, sp, shapes,...]
    dot_general x73 -> x2, matrix products: 187 us -> 1.21 us  [the longest x1 1.05 us: per_device(): lax.dot_general(emb_cols, grad_scales, (((0,), (0,)), ((), ())), preferre...]
    all_gather x6 -> x0, waiting for transfers between devices: 119 us -> none  [the longest x1 28.1 us: per_device(): gathered = lax.all_gather(projected[:, C:], 'sp', axis=0, tiled=True)]
    unnamed x2 -> x0, blocking collectives: 68.5 us -> none
    psum x10 -> x0, blocking collectives: 53.2 us -> none  [the longest x3 15.2 us: norm_back(): totals = lax.psum(sums, 'sp')]
    convert_element_type x32 -> x3, other arithmetic: 28.3 us -> 0.86 us  [the longest x1 0.84 us: per_device(): grad_scales = every.reshape(fsdp, 2 * C).astype(BF16)]
    unnamed x59 -> x16, local copies, waits for them, and re-layouts: 30.6 us -> 8.29 us
  transfers between devices with their start and end apart: 23 -> 0, of which waited for: 18 -> 0; matrix products, arithmetic and copies ran while one was open for 17% -> 0% of each run, Pallas kernels for 0% -> 0%
where the time goes in v1:
time: 383 us
  Pallas kernels  349 us (91%)
  local copies, waits for them, and re-layouts  25.9 us (7%)
  other arithmetic  5.27 us (1%)
    pallas_call x1, Pallas kernels, scatter(): pl.pallas_call(functools.partial(scatter_kernel, dims, fsdp, sp, shapes,...  111 us
    pallas_call x1, Pallas kernels, attention(): pl.pallas_call(functools.partial(attention_kernel, sp, heads), out_shape=...  87.9 us
    pallas_call x1, Pallas kernels, gather(): pl.pallas_call(functools.partial(gather_kernel, dims, fsdp, sp, shapes),...  85.8 us
    pallas_call x1, Pallas kernels, backward(): pl.pallas_call(functools.partial(backward_kernel, fsdp, sp), out_shape=[j...  37.6 us
    pallas_call x1, Pallas kernels, forward(): pl.pallas_call(functools.partial(forward_kernel, sp), out_shape=[jax.Shap...  26.6 us
    unnamed x16, local copies, waits for them, and re-layouts  8.29 us

profile of v1, /device:TPU:0, one launch (start us, length us, event | category | flops | bytes accessed | tf_op | source)
XLA Modules:
  0.0 382.5 jit_solution(9242700415879123364)
XLA Ops:
  2.7 1.2 concatenate.19.nums
  5.3 0.9 reshape.178
  7.2 1.1 reshape.179
  8.4 0.9 dynamic-slice_reduce_fusion
  10.0 85.8 %gather.1 = (bf16[4,2,2,2,144,512]{5,4,3,2,1,0:T(8,128)(2,1)}, bf16[4,2,2,2,144,512]{5,4,3,2,1,0:T(8,128)(2,1)}, bf16[4,2,2,1,32,768]{5,4,3,2,1,0:T(8,128)(2,1)}...) custom-call(bf16[2,144,512]{2,1,0:T(8,128)(2,1)} %bitcast.97, ...), custom_call_target="tpu_custom_call" | custom-call | tf_op jit(solution)/shard_map/gather/pallas_call | solution.py:223
  95.8 1.3 reshape.182.scales
  97.1 0.8 slice.43
  97.9 0.9 slice_reduce_fusion
  99.6 26.6 %forward.1 = (f32[8,64,512]{2,1,0:T(8,128)}, bf16[8,64,512]{2,1,0:T(8,128)(2,1)}, f32[8,64,512]{2,1,0:T(8,128)}, bf16[3,10,64,512]{3,2,1,0:T(8,128)(2,1)}, bf16[...) custom-call(f32[30]{0:T(128)} %concatenate.19.nums, bf16[8,64,512]{2,1,0:T(8,128)(2,1)} %bitcast.80, ...), custom_call_target="tpu_custom_call" | custom-call | tf_op jit(solution)/shard_map/forward/pallas_call | solution.py:757
  126.1 87.9 %attention.1 = (bf16[512,512]{1,0:T(8,128)(2,1)}, f32[512,512]{1,0:T(8,128)}, bf16[512,768]{1,0:T(8,128)(2,1)}, bf16[2048,512]{1,0:T(8,128)(2,1)}, bf16[512,512]{1,0:T(8,128)(2,1)}, /*index=5*/f32[128,2048]{1,0:T(8,128)}) custom-call(f32[30]{0:T(128)} %concatenate.19.nums, bf16[512,512]{1,0:T(8,128)(2,1)} %bitcast.93, bf16[128,2048]{1,0:T(8,128)(2,1)} %bitcast.90, ...), custom_call_target="tpu_custom_call" | custom-call | tf_op jit(solution)/shard_map/attention/pallas_call | solution.py:981
  214.0 37.6 %backward.1 = (bf16[4608,512]{1,0:T(8,128)(2,1)}, bf16[4608,512]{1,0:T(8,128)(2,1)}, f32[8,64,512]{2,1,0:T(8,128)}, f32[8,512]{1,0:T(8,128)}, f32[16,8,128]{2,1,0:T(8,128)}) custom-call(f32[30]{0:T(128)} %concatenate.19.nums, bf16[8,64,512]{2,1,0:T(8,128)(2,1)} %bitcast.81, f32[3,512]{1,0:T(4,128)} %reshape.181.gains, f32[2,512]{1,0:T(2,128)} %reshape.182.scales, ...), custom_call_target="tpu_custom_call" | custom-call | tf_op jit(solution)/shard_map/backward/pallas_call | solution.py:1208
  252.5 0.8 convert_element_type.47
  254.2 110.9 %scatter.1 = (f32[2,144,512]{2,1,0:T(8,128)}, f32[2,144,512]{2,1,0:T(8,128)}, f32[2,32,768]{2,1,0:T(8,128)}, f32[2,128,512]{2,1,0:T(8,128)}, f32[2,16,512]{2,1,0...) custom-call(bf16[4,2,2,2,144,512]{5,4,3,2,1,0:T(8,128)(2,1)} %bitcast.72, bf16[4,2,2,2,144,512]{5,4,3,2,1,0:T(8,128)(2,1)} %bitcast.73, ...), custom_call_target="tpu_custom_call" | custom-call | tf_op jit(solution)/shard_map/scatter/pallas_call | solution.py:464
  365.2 1.6 bitcast_multiply_fusion
  366.8 1.4 slice_bitcast_fusion
  368.2 1.0 reshape.201
  370.2 1.0 fusion
  371.2 1.4 reshape.203
  373.0 1.2 reshape.204
  374.2 1.9 copy.69
  376.1 1.0 copy.70
  377.1 1.0 copy.71
  378.1 1.9 copy.72
  380.0 1.9 copy.73
  (35 shorter events, 9.1 us)
Async XLA Ops:
  214.0 39.4 %copy-start = (bf16[128,1024]{1,0:T(8,128)(2,1)S(1)}, bf16[128,1024]{1,0:T(8,128)(2,1)}, u32[]{:S(2)}) copy-start(bf16[128,1024]{1,0:T(8,128)(2,1)} %refs_6_.1) | copy-start | bytes 786436
  254.2 110.9 %copy-start.4 = (bf16[1,2048]{1,0:T(2,128)(2,1)S(1)}, bf16[1,2048]{1,0:T(2,128)(2,1)}, u32[]{:S(2)}) copy-start(bf16[1,2048]{1,0:T(2,128)(2,1)} %param.15) | copy-start | bytes 12292
  365.2 11.0 %copy-start.2 = (f32[8,64,512]{2,1,0:T(8,128)S(1)}, f32[8,64,512]{2,1,0:T(8,128)}, u32[]{:S(2)}) copy-start(f32[8,64,512]{2,1,0:T(8,128)} %get-tuple-element.59) | copy-start | bytes 3145732
  365.2 11.9 %copy-start.1 = (f32[128,2048]{1,0:T(8,128)S(1)}, f32[128,2048]{1,0:T(8,128)}, u32[]{:S(2)}) copy-start(f32[128,2048]{1,0:T(8,128)} %get-tuple-element.68) | copy-start | bytes 3145732
  372.6 9.3 %copy-start.3 = (f32[2,16,512]{2,1,0:T(8,128)S(1)}, f32[2,16,512]{2,1,0:T(8,128)}, u32[]{:S(2)}) copy-start(f32[2,16,512]{2,1,0:T(8,128)} %get-tuple-element.74) | copy-start | bytes 196612

commit v2 on v1

--- a/solution.py
+++ b/solution.py
@@ -255,239 +255,182 @@
     lax.fori_loop(0, rows // step, body, 0)
 
 
-def scatter_kernel(dims, fsdp, sp, shapes, modes, *refs):
-    zs, ys, cs = dims
-    count = len(shapes)
-    grads, tiles = refs[:count], refs[count]
-    refs = refs[count + 1 :]
-    outs, tiles_out, small_out = refs[:count], refs[count], refs[count + 1]
-    refs = refs[count + 2 :]
-    own, crecvd, xrecvd, yrecvd, zrecvd, last = (
-        refs[k * count : (k + 1) * count] for k in range(6)
-    )
-    refs = refs[6 * count :]
-    got, small = refs[0], refs[1]
-    csem, xsem, ysem, zsem, fsem, lsem, tsem, ssem = refs[2:]
-    me, x = lax.axis_index("fsdp"), lax.axis_index("sp")
-    z, y, c = me // (ys * cs), (me // cs) % ys, me % cs
-
-    def dev(zz, yy, cc):
-        return ((zz * ys + yy) * cs + cc, x)
-
-    peers = [((me + d) % fsdp, x) for d in range(1, fsdp)]
-    peers += [(me, (x + d) % sp) for d in range(1, sp)]
-    greet(peers)
-    flying = []
-
-    def launch(copy):
+class Sums:
+    def __init__(self, dims, sp, shapes, modes, grads, own, outs, bufs, sems):
+        self.dims, self.sp, self.shapes, self.modes = dims, sp, shapes, modes
+        self.grads, self.own, self.outs = grads, own, outs
+        self.crecvd, self.xrecvd, self.yrecvd, self.zrecvd, self.last = bufs
+        self.csem, self.xsem, self.ysem, self.zsem, self.fsem, self.lsem = sems
+        zs, ys, cs = dims
+        self.me, self.x = lax.axis_index("fsdp"), lax.axis_index("sp")
+        self.z, self.y, self.c = self.me // (ys * cs), (self.me // cs) % ys, self.me % cs
+        self.flying = []
+
+    def dev(self, zz, yy, cc):
+        return ((zz * self.dims[1] + yy) * self.dims[2] + cc, self.x)
+
+    def launch(self, copy):
         copy.start()
-        flying.append(copy)
-
-    first = tiles_start(fsdp, tiles, got, tsem.at[0], tsem.at[1], lambda ref, to: ref.at[to])
-    flying += first
-
-    order = [(dz, dy) for dz in range(zs - 1, -1, -1) for dy in range(ys - 1, -1, -1)]
-
-    def where(dz, dy):
-        return (z + dz) % zs, (y + dy) % ys
-
-    def ccopy(a, dz, dy):
-        zz, yy = where(dz, dy)
+        self.flying.append(copy)
+
+    def order(self):
+        zs, ys, _ = self.dims
+        return [(dz, dy) for dz in range(zs - 1, -1, -1) for dy in range(ys - 1, -1, -1)]
+
+    def grad(self, a, dz, dy, cc):
+        zs, ys, cs = self.dims
+        h, rows, _ = self.shapes[a]
+        owner = (((self.z + dz) % zs) * ys + (self.y + dy) % ys) * cs + cc
+        return self.grads[a].at[pl.ds(pl.multiple_of(owner * (h * rows), 16), h * rows)]
+
+    def part(self, a, dz, dy, k):
+        zs, ys, cs = self.dims
+        h, rows, _ = self.shapes[a]
+        if self.own[a] is not None:
+            return self.own[a].at[dz, dy, pl.ds(pl.multiple_of(k * rows, 16), rows)]
+        owner = (((self.z + dz) % zs) * ys + (self.y + dy) % ys) * cs + self.c
+        return self.grads[a].at[pl.ds(pl.multiple_of((owner * h + k) * rows, 16), rows)]
+
+    def piece(self, a):
+        return self.x if self.shapes[a][0] > 1 else 0
+
+    def ccopy(self, a, dz, dy):
         return remote(
-            grads[a].at[zz, yy, 1 - c],
-            crecvd[a].at[dz, dy],
-            csem.at[0, a, dz, dy],
-            csem.at[1, a, dz, dy],
-            dev(z, y, 1 - c),
+            self.grad(a, dz, dy, 1 - self.c),
+            self.crecvd[a].at[dz, dy],
+            self.csem.at[0, a, dz, dy],
+            self.csem.at[1, a, dz, dy],
+            self.dev(self.z, self.y, 1 - self.c),
         )
 
-    def mine(a, dz, dy):
-        zz, yy = where(dz, dy)
-        return pltpu.make_async_copy(grads[a].at[zz, yy, c], own[a].at[dz, dy], lsem.at[a, dz, dy])
-
-    def xcopy(a, dz, dy, dx):
-        to = (x + dx) % sp
+    def mine(self, a, dz, dy):
+        return pltpu.make_async_copy(
+            self.grad(a, dz, dy, self.c), self.own[a].at[dz, dy], self.lsem.at[a, dz, dy]
+        )
+
+    def xcopy(self, a, dz, dy, dx):
+        to = (self.x + dx) % self.sp
         return remote(
-            own[a].at[dz, dy, to],
-            xrecvd[a].at[dz, dy, dx - 1],
-            xsem.at[0, a, dz, dy, dx],
-            xsem.at[1, a, dz, dy, dx],
-            (me, to),
+            self.part(a, dz, dy, to),
+            self.xrecvd[a].at[dz, dy, dx - 1],
+            self.xsem.at[0, a, dz, dy, dx],
+            self.xsem.at[1, a, dz, dy, dx],
+            (self.me, to),
         )
 
-    def ycopy(a, dz, dy):
-        h = x if shapes[a][0] > 1 else 0
+    def ycopy(self, a, dz, dy):
         return remote(
-            own[a].at[dz, dy, h],
-            yrecvd[a].at[dz, dy - 1],
-            ysem.at[0, a, dz, dy],
-            ysem.at[1, a, dz, dy],
-            dev(z, (y + dy) % ys, c),
+            self.part(a, dz, dy, self.piece(a)),
+            self.yrecvd[a].at[dz, dy - 1],
+            self.ysem.at[0, a, dz, dy],
+            self.ysem.at[1, a, dz, dy],
+            self.dev(self.z, (self.y + dy) % self.dims[1], self.c),
         )
 
-    def zcopy(a, dz):
-        h = x if shapes[a][0] > 1 else 0
+    def zcopy(self, a, dz):
         return remote(
-            own[a].at[dz, 0, h],
-            zrecvd[a].at[dz - 1],
-            zsem.at[0, a, dz],
-            zsem.at[1, a, dz],
-            dev((z + dz) % zs, y, c),
+            self.part(a, dz, 0, self.piece(a)),
+            self.zrecvd[a].at[dz - 1],
+            self.zsem.at[0, a, dz],
+            self.zsem.at[1, a, dz],
+            self.dev((self.z + dz) % self.dims[0], self.y, self.c),
         )
 
-    def fcopy(a, dx):
+    def fcopy(self, a, dx):
         return remote(
-            last[a].at[x],
-            last[a].at[x],
-            fsem.at[0, a, dx],
-            fsem.at[1, a, dx],
-            (me, (x + dx) % sp),
+            self.last[a].at[self.x],
+            self.last[a].at[self.x],
+            self.fsem.at[0, a, dx],
+            self.fsem.at[1, a, dx],
+            (self.me, (self.x + dx) % self.sp),
         )
 
-    def into(ref):
+    def add(self, a, first, second, target):
         def put(at, value):
-            ref[at, :] = value.astype(BF16)
-
-        return put
-
-    for a in range(count):
-        for dz, dy in order:
-            launch(ccopy(a, dz, dy))
-            mine(a, dz, dy).start()
-
-    def over_c(a):
-        h, rows, _ = shapes[a]
-        for dz, dy in order:
-            mine(a, dz, dy).wait()
-            ccopy(a, dz, dy).wait_recv()
+            target[at, :] = value.astype(BF16)
+
+        add_rows(self.shapes[a][1], first, second, put)
+
+    def start(self, a):
+        for dz, dy in self.order():
+            self.launch(self.ccopy(a, dz, dy))
+            if self.own[a] is not None:
+                self.mine(a, dz, dy).start()
+
+    def over_c(self, a):
+        h, rows, _ = self.shapes[a]
+        for dz, dy in self.order():
+            if self.own[a] is not None:
+                self.mine(a, dz, dy).wait()
+            self.ccopy(a, dz, dy).wait_recv()
             for k in range(h):
-                ref = own[a].at[dz, dy, k]
-                add_rows(rows, ref, crecvd[a].at[dz, dy, k], into(ref))
+                ref = self.part(a, dz, dy, k)
+                self.add(a, ref, self.crecvd[a].at[dz, dy, pl.ds(k * rows, rows)], ref)
             if h > 1:
-                for dx in range(1, sp):
-                    launch(xcopy(a, dz, dy, dx))
-
-    def over_x(a):
-        h, rows, _ = shapes[a]
-        for dz, dy in order:
-            if h > 1:
-                ref = own[a].at[dz, dy, x]
-                for dx in range(1, sp):
-                    xcopy(a, dz, dy, dx).wait_recv()
-                    add_rows(rows, ref, xrecvd[a].at[dz, dy, dx - 1], into(ref))
+                for dx in range(1, self.sp):
+                    self.launch(self.xcopy(a, dz, dy, dx))
+
+    def over_x(self, a, dz):
+        for dy in range(self.dims[1] - 1, -1, -1):
+            if self.shapes[a][0] > 1:
+                ref = self.part(a, dz, dy, self.x)
+                for dx in range(1, self.sp):
+                    self.xcopy(a, dz, dy, dx).wait_recv()
+                    self.add(a, ref, self.xrecvd[a].at[dz, dy, dx - 1], ref)
             if dy:
-                launch(ycopy(a, dz, dy))
-
-    def over_y(a):
-        h, rows, _ = shapes[a]
-        k = x if h > 1 else 0
-        for dz in range(zs - 1, -1, -1):
-            ref = own[a].at[dz, 0, k]
-            for dy in range(1, ys):
-                ycopy(a, dz, dy).wait_recv()
-                add_rows(rows, ref, yrecvd[a].at[dz, dy - 1], into(ref))
-            if dz:
-                launch(zcopy(a, dz))
-
-    def over_z(a):
-        h, rows, _ = shapes[a]
-        k = x if h > 1 else 0
-        ref = own[a].at[0, 0, k]
+                self.launch(self.ycopy(a, dz, dy))
+
+    def over_y(self, a, dz):
+        ref = self.part(a, dz, 0, self.piece(a))
+        for dy in range(1, self.dims[1]):
+            self.ycopy(a, dz, dy).wait_recv()
+            self.add(a, ref, self.yrecvd[a].at[dz, dy - 1], ref)
+        if dz:
+            self.launch(self.zcopy(a, dz))
+
+    def over_z(self, a):
+        zs = self.dims[0]
+        ref = self.part(a, 0, 0, self.piece(a))
         for dz in range(1, zs):
-            zcopy(a, dz).wait_recv()
-            target = last[a].at[x] if dz == zs - 1 else ref
-            add_rows(rows, ref, zrecvd[a].at[dz - 1], into(target))
+            self.zcopy(a, dz).wait_recv()
+            target = self.last[a].at[self.x] if dz == zs - 1 else ref
+            self.add(a, ref, self.zrecvd[a].at[dz - 1], target)
         if zs == 1:
-            last[a][x] = ref[...]
-        for dx in range(1, sp):
-            launch(fcopy(a, dx))
-
-    for step in range(count + 3):
-        if step < count:
-            over_c(step)
-        if 1 <= step <= count:
-            over_x(step - 1)
-        if 2 <= step <= count + 1:
-            over_y(step - 2)
-        if step >= 3:
-            over_z(step - 3)
-
-    got[me] = tiles[me]
-    for copy in first:
-        copy.wait_recv()
-    total = got[0]
-    for f in range(1, fsdp):
-        total = total + got[f]
-    small[x] = total
-    for dx in range(1, sp):
-        launch(remote(small.at[x], small.at[x], ssem.at[0, dx], ssem.at[1, dx], (me, (x + dx) % sp)))
-    tiles_out[...] = got[...]
-    for a in range(count):
-        for dx in range(1, sp):
-            fcopy(a, dx).wait_recv()
-        if modes[a] == "add" and shapes[a][0] == 1:
-            value = last[a][0].astype(F32)
-            for k in range(1, sp):
-                value = value + last[a][k].astype(F32)
-            outs[a][0] = value
+            self.last[a][self.x] = ref[...]
+        for dx in range(1, self.sp):
+            self.launch(self.fcopy(a, dx))
+
+    def all_x(self, a):
+        for dz in range(self.dims[0] - 1, -1, -1):
+            self.over_x(a, dz)
+
+    def all_y(self, a):
+        for dz in range(self.dims[0] - 1, -1, -1):
+            self.over_y(a, dz)
+
+    def both(self, a):
+        zs = self.dims[0]
+        for dz in range(zs - 1, -2, -1):
+            if dz >= 0:
+                self.over_x(a, dz)
+            if dz < zs - 1:
+                self.over_y(a, dz + 1)
+
+    def finish(self, a):
+        for dx in range(1, self.sp):
+            self.fcopy(a, dx).wait_recv()
+        if self.modes[a] == "add" and self.shapes[a][0] == 1:
+            value = self.last[a][0].astype(F32)
+            for k in range(1, self.sp):
+                value = value + self.last[a][k].astype(F32)
+            self.outs[a][0] = value
         else:
-            for k in range(sp):
-                outs[a][k] = last[a][k].astype(F32)
-    for dx in range(1, sp):
-        remote(
-            small.at[x], small.at[x], ssem.at[0, dx], ssem.at[1, dx], (me, (x + dx) % sp)
-        ).wait_recv()
-    total = small[0]
-    for k in range(1, sp):
-        total = total + small[k]
-    small_out[...] = total
-    for copy in flying:
-        copy.wait_send()
-
-
-def scatter(grads, modes, tiles, fsdp, sp):
-    dims = sizes_of(fsdp, sp)
-    zs, ys, cs = dims
-    count = len(grads)
-    split, shapes, outs = [], [], []
-    for grad, mode in zip(grads, modes, strict=True):
-        rows, width = grad.shape[0] // fsdp, grad.shape[1]
-        h = parts_of(rows, sp) if mode == "add" else 1
-        shapes.append((h, rows // h, width))
-        split.append(grad.reshape(dims + (h, rows // h, width)))
-        copies = 1 if mode == "add" and h == 1 else sp
-        outs.append(jax.ShapeDtypeStruct((copies, rows // h, width), F32))
-
-    def scratch(shape):
-        return pltpu.VMEM(shape, BF16)
-
-    results = pl.pallas_call(
-        functools.partial(scatter_kernel, dims, fsdp, sp, shapes, modes),
-        out_shape=outs
-        + [jax.ShapeDtypeStruct((fsdp, 8, 128), F32), jax.ShapeDtypeStruct((8, 128), F32)],
-        in_specs=[ANY] * count + [VMEM],
-        out_specs=[VMEM] * (count + 2),
-        scratch_shapes=[scratch((zs, ys) + s) for s in shapes]
-        + [scratch((zs, ys) + s) for s in shapes]
-        + [scratch((zs, ys, sp - 1) + s[1:] if s[0] > 1 else (1, 1, 1, 16, 128)) for s in shapes]
-        + [scratch((zs, max(ys - 1, 1)) + s[1:]) for s in shapes]
-        + [scratch((max(zs - 1, 1),) + s[1:]) for s in shapes]
-        + [scratch((sp,) + s[1:]) for s in shapes]
-        + [pltpu.VMEM((fsdp, 8, 128), F32), pltpu.VMEM((sp, 8, 128), F32)]
-        + [
-            DMA((2, count, zs, ys)),
-            DMA((2, count, zs, ys, sp)),
-            DMA((2, count, zs, ys)),
-            DMA((2, count, zs)),
-            DMA((2, count, sp)),
-            DMA((count, zs, ys)),
-            DMA((2, fsdp)),
-            DMA((2, sp)),
-        ],
-        compiler_params=params(4),
-        name="scatter",
-    )(*split, tiles)
-    return results[:count], results[count], results[count + 1]
+            for k in range(self.sp):
+                self.outs[a][k] = self.last[a][k].astype(F32)
+
+    def drain(self):
+        for copy in self.flying:
+            copy.wait_send()
 
 
 def lane_groups(values):
@@ -1014,46 +957,23 @@
     )(nums, normed, text, wq, wt, wo, cot, resid)
 
 
-def backward_kernel(
-    fsdp,
-    sp,
-    nums,
-    image,
-    gains,
-    scales,
-    stats,
-    resid,
-    conv_out,
-    s1,
-    s2,
-    gnorm,
-    cot,
-    w1,
-    w2,
-    gw1,
-    gw2,
-    gimage,
-    ggains,
-    gscales,
-    w1v,
-    w2v,
-    out1,
-    out2,
-    p1,
-    p2,
-    edge1,
-    edge2,
-    gres,
-    acc,
-    sums,
-    mine,
-    every,
-    ssem,
-    hsem,
-    wsem,
-    osem,
-    tsem,
-):
+def backward_kernel(dims, fsdp, sp, shapes, modes, *refs):
+    n = len(shapes)
+    (nums, image, gains, scales, stats, resid, conv_out, s1, s2, gnorm, cot, table, w1, w2), refs = (
+        refs[:14],
+        refs[14:],
+    )
+    attn, refs = refs[: n - 2], refs[n - 2 :]
+    outs, gimage, gscales, etiles, gtotal, refs = refs[:n], *refs[n : n + 4], refs[n + 4 :]
+    (w1v, w2v, out1, out2, p1, p2, edge1, edge2, gres, acc, sums, mine, every, pieces, got_e), refs = (
+        refs[:15],
+        refs[15:],
+    )
+    (ggains, got_g, gsmall), refs = refs[:3], refs[3:]
+    own, refs = (None, None) + tuple(refs[: n - 2]), refs[n - 2 :]
+    bufs, refs = [refs[i * n : (i + 1) * n] for i in range(5)], refs[5 * n :]
+    (ssem, hsem, wsem, tsem, esem, gsem, rsem), sems = refs[:7], refs[7:]
+    total_of = Sums(dims, sp, shapes, modes, (out1, out2) + tuple(attn), own, outs, bufs, sems)
     rows, columns = image.shape[0], image.shape[1]
     pixels = rows * columns
     me, x = lax.axis_index("fsdp"), lax.axis_index("sp")
@@ -1065,6 +985,9 @@
     edge1[...] = jnp.zeros_like(edge1)
     edge2[...] = jnp.zeros_like(edge2)
     greet(swap.peers() + [((me + d) % fsdp, x) for d in range(1, fsdp)])
+    late = list(range(2, n))
+    for a in late:
+        total_of.start(a)
     count = nums[rows + 2]
     g1, g2, g3 = gains[0:1], gains[1:2], gains[2:3]
     mean1, inv1, mean2, inv2, mean3, inv3 = (stats[k : k + 1] for k in range(6))
@@ -1079,7 +1002,7 @@
             total = total + m
         return total
 
-    def weight_grad(shifted, padded, store, target, sem):
+    def weight_grad(shifted, padded, store):
         grad = padded[1, 1 : rows + 1].reshape(pixels, C)
 
         def body(t, _):
@@ -1092,7 +1015,6 @@
             return 0
 
         lax.fori_loop(0, 3, body, 0)
-        pltpu.make_async_copy(store, target, sem).start()
 
     def hat3(r):
         return (resid[r] - mean3) * mask(r) * inv3
@@ -1117,12 +1039,21 @@
 
     lax.fori_loop(0, rows, residual, 0)
     swap.edges_start(0, p2.at[1, 1], p2.at[1, rows], edge2)
-    weight_grad(s2, p2, out2, gw2, osem.at[0])
+    weight_grad(s2, p2, out2)
+    total_of.start(1)
+    for a in late:
+        total_of.over_c(a)
+        if shapes[a][0] == 1:
+            total_of.all_x(a)
     swap.edges_wait(0, p2.at[1, 1], p2.at[1, rows], edge2)
     put_shifted(p2, 0, edge2[0].astype(F32))
     put_shifted(p2, rows + 1, edge2[1].astype(F32))
     load2.wait()
     taps(rows, columns, p2, w2v, acc, True)
+    total_of.over_c(1)
+    for a in late:
+        if shapes[a][0] > 1:
+            total_of.all_x(a)
     scale, shift = 1.0 + scales[0:1], scales[1:2]
 
     def hat2(r):
@@ -1166,12 +1097,17 @@
 
     lax.fori_loop(0, rows, middle, 0)
     swap.edges_start(1, p1.at[1, 1], p1.at[1, rows], edge1)
-    weight_grad(s1, p1, out1, gw1, osem.at[1])
+    for a in late:
+        total_of.all_y(a)
+    weight_grad(s1, p1, out1)
+    total_of.start(0)
     swap.edges_wait(1, p1.at[1, 1], p1.at[1, rows], edge1)
     put_shifted(p1, 0, edge1[0].astype(F32))
     put_shifted(p1, rows + 1, edge1[1].astype(F32))
     load1.wait()
+    total_of.over_c(0)
     taps(rows, columns, p1, w1v, acc, True)
+    total_of.both(1)
 
     def hat1(r):
         return (image[r].astype(F32) * mask(r) - mean1) * mask(r) * inv1
@@ -1185,6 +1121,28 @@
     plain, crossed = column_sums(rows, from_one)
     swap.sums_start(2, stack_rows(lane_groups(plain * g1), lane_groups(crossed * g1)))
     ggains[...] = stack_rows(crossed, gain2, gain3)
+    share = C // fsdp
+
+    def gain_block(ref, to):
+        return ref.at[:, pl.ds(pl.multiple_of((to * share) // 128 * 128, 128), 128)]
+
+    gcopies = tiles_start(fsdp, ggains, got_g, gsem.at[0], gsem.at[1], gain_block)
+    got_g[me] = ggains[:, pl.ds(pl.multiple_of((me * share) // 128 * 128, 128), 128)]
+    for copy in copies:
+        copy.wait()
+    gscales[...] = every[...]
+    piece = None
+    for j in range(8):
+        term = lax.dot_general(
+            every[:, j, :].astype(BF16),
+            table[:, j * 128 : (j + 1) * 128],
+            (((1,), (1,)), ((), ())),
+            preferred_element_type=F32,
+        )
+        piece = term if piece is None else piece + term
+    pieces[...] = jnp.broadcast_to(piece[:, None, :], pieces.shape)
+    ecopies = tiles_start(fsdp, pieces, got_e, esem.at[0], esem.at[1], lambda ref, to: ref.at[to])
+    got_e[me] = pieces[me]
     total = joint(2) / count
     m1, m2 = total[0:1], total[1:2]
 
@@ -1194,51 +1152,120 @@
         return 0
 
     lax.fori_loop(0, rows, final, 0)
-    for copy in copies:
+    for a in late:
+        total_of.over_z(a)
+    total_of.over_z(1)
+    total_of.both(0)
+    for copy in gcopies:
         copy.wait()
-    gscales[...] = every[...]
-    pltpu.make_async_copy(out2, gw2, osem.at[0]).wait()
-    pltpu.make_async_copy(out1, gw1, osem.at[1]).wait()
-
-
-def backward(nums, image, gains, scales, stats, resid, conv_out, s1, s2, gnorm, cot, w1, w2, fsdp, sp):
+    total = got_g[0]
+    for f in range(1, fsdp):
+        total = total + got_g[f]
+    gsmall[x] = total
+
+    def small_copy(d):
+        to = (me, (x + d) % sp)
+        return remote(gsmall.at[x], gsmall.at[x], rsem.at[0, d], rsem.at[1, d], to)
+
+    for d in range(1, sp):
+        small_copy(d).start()
+    for a in late:
+        total_of.finish(a)
+    total_of.finish(1)
+    for copy in ecopies:
+        copy.wait()
+    etiles[...] = got_e[...]
+    for d in range(1, sp):
+        small_copy(d).wait()
+    total = gsmall[0]
+    for i in range(1, sp):
+        total = total + gsmall[i]
+    gtotal[...] = total
+    total_of.over_z(0)
+    total_of.finish(0)
+    total_of.drain()
+
+
+def backward(
+    nums, image, gains, scales, stats, resid, conv_out, s1, s2, gnorm, cot, table, w1, w2, attn, fsdp, sp
+):
     rows, columns, _ = image.shape
     field = (rows, columns, C)
     shifted = (3, rows + 2, columns, C)
+    dims = sizes_of(fsdp, sp)
+    zs, ys, _ = dims
+    shapes, outs = [], []
+    grads = [w1, w2] + [g for g, _ in attn]
+    modes = ["add", "add"] + [m for _, m in attn]
+    for grad, mode in zip(grads, modes, strict=True):
+        r, width = grad.shape[0] // fsdp, grad.shape[1]
+        h = parts_of(r, sp) if mode == "add" else 1
+        shapes.append((h, r // h, width))
+        copies = 1 if mode == "add" and h == 1 else sp
+        outs.append(jax.ShapeDtypeStruct((copies, r // h, width), F32))
+    count = len(grads)
+
+    def scratch(*shape):
+        return pltpu.VMEM(shape, BF16)
+
+    tile = jax.ShapeDtypeStruct((fsdp, 8, 128), F32)
+    tiles = pltpu.VMEM((fsdp, 8, 128), F32)
     return pl.pallas_call(
-        functools.partial(backward_kernel, fsdp, sp),
-        out_shape=[
-            jax.ShapeDtypeStruct(w1.shape, BF16),
-            jax.ShapeDtypeStruct(w2.shape, BF16),
-            jax.ShapeDtypeStruct(field, F32),
-            jax.ShapeDtypeStruct((8, C), F32),
-            jax.ShapeDtypeStruct((fsdp, 8, 128), F32),
-        ],
-        in_specs=[SMEM] + [VMEM] * 10 + [ANY, ANY],
-        out_specs=[ANY, ANY, VMEM, VMEM, VMEM],
+        functools.partial(backward_kernel, dims, fsdp, sp, shapes, modes),
+        out_shape=outs
+        + [jax.ShapeDtypeStruct(field, F32), tile, tile, jax.ShapeDtypeStruct((8, 128), F32)],
+        in_specs=[SMEM] + [VMEM] * 11 + [ANY] * count,
+        out_specs=[VMEM] * (count + 4),
         scratch_shapes=[
-            pltpu.VMEM(w1.shape, BF16),
-            pltpu.VMEM(w2.shape, BF16),
-            pltpu.VMEM(w1.shape, BF16),
-            pltpu.VMEM(w2.shape, BF16),
-            pltpu.VMEM(shifted, BF16),
-            pltpu.VMEM(shifted, BF16),
-            pltpu.VMEM((2, columns, C), BF16),
-            pltpu.VMEM((2, columns, C), BF16),
+            scratch(*w1.shape),
+            scratch(*w2.shape),
+            scratch(*w1.shape),
+            scratch(*w2.shape),
+            scratch(*shifted),
+            scratch(*shifted),
+            scratch(2, columns, C),
+            scratch(2, columns, C),
             pltpu.VMEM(field, F32),
             pltpu.VMEM(field, F32),
             pltpu.VMEM((3, sp, 8, C), F32),
             pltpu.VMEM((8, 128), F32),
-            pltpu.VMEM((fsdp, 8, 128), F32),
+            tiles,
+            tiles,
+            tiles,
+            pltpu.VMEM((8, C), F32),
+            tiles,
+            pltpu.VMEM((sp, 8, 128), F32),
+        ]
+        + [scratch(zs, ys, s[0] * s[1], s[2]) for s in shapes[2:]]
+        + [scratch(zs, ys, s[0] * s[1], s[2]) for s in shapes]
+        + [
+            scratch(zs, ys, sp - 1, *s[1:]) if s[0] > 1 else scratch(1, 1, 1, 16, 128)
+            for s in shapes
+        ]
+        + [scratch(zs, max(ys - 1, 1), *s[1:]) for s in shapes]
+        + [scratch(max(zs - 1, 1), *s[1:]) for s in shapes]
+        + [scratch(sp, *s[1:]) for s in shapes]
+        + [
             DMA((2, 3, sp)),
             DMA((2, 2, 2)),
             DMA((2,)),
-            DMA((2,)),
             DMA((2, fsdp)),
+            DMA((2, fsdp)),
+            DMA((2, fsdp)),
+            DMA((2, sp)),
+            DMA((2, count, zs, ys)),
+            DMA((2, count, zs, ys, sp)),
+            DMA((2, count, zs, ys)),
+            DMA((2, count, zs)),
+            DMA((2, count, sp)),
+            DMA((count, zs, ys)),
         ],
         compiler_params=params(3),
         name="backward",
-    )(nums, image, gains, scales, stats, resid, conv_out, s1, s2, gnorm, cot, w1, w2)
+    )(
+        nums, image, gains, scales, stats, resid, conv_out, s1, s2, gnorm, cot, table, w1, w2,
+        *[g for g, _ in attn],
+    )
 
 
 def per_device(
@@ -1315,7 +1342,7 @@
         resid.reshape(pixels, C),
         sp,
     )
-    gw1, gw2, gimage, ggains, every = backward(
+    (r1, r2, rt, rq, ro, gimage, every, tiles_in, small) = backward(
         nums,
         image[0],
         gains,
@@ -1327,8 +1354,10 @@
         s2,
         gnorm.reshape(rows, columns, C),
         cotangent[0],
+        table,
         w1,
         w2,
+        [(gt, "join"), (gq, "join"), (go, "add")],
         fsdp,
         sp,
     )
@@ -1336,15 +1365,6 @@
     grad_emb_proj = lax.dot_general(
         emb_cols, grad_scales, (((0,), (0,)), ((), ())), preferred_element_type=F32
     )
-    piece = lax.dot_general(
-        grad_scales, emb_proj, (((1,), (1,)), ((), ())), preferred_element_type=F32
-    )
-    gain_tiles = ggains[:3].reshape(3, fsdp, share).transpose(1, 0, 2).reshape(fsdp, 3 * share)
-    tiles = jnp.stack([lanes(piece), lanes(gain_tiles)], axis=1)
-    tiles = jnp.pad(tiles, ((0, 0), (0, 6), (0, 0)))
-    (r1, r2, rq, rt, ro), tiles_in, small = scatter(
-        [gw1, gw2, gq, gt, go], ["add", "add", "join", "join", "add"], tiles, fsdp, sp
-    )
 
     def joined(result, kinds):
         n = result.shape[1]
@@ -1353,7 +1373,8 @@
     grad_embedding = tiles_in[:, 0, :emb_rows].reshape(1, -1)
     sigmoid = jax.nn.sigmoid(emb_float)
     grad_embedding = grad_embedding * (sigmoid * (1.0 + emb_float * (1.0 - sigmoid)))
-    gain_sums = small[1, : 3 * share].reshape(3, share)
+    lane = (lax.axis_index("fsdp") * share) % 128
+    gain_sums = lax.dynamic_slice(small, (0, lane), (3, share))
     return (
         output.reshape(1, rows, columns, C),
         gimage[None],

time: 383 us -> 341 us (0.89)
  Pallas kernels: 349 us -> 313 us
  local copies, waits for them, and re-layouts: 25.9 us -> 20.6 us
    pallas_call x2 -> x1, Pallas kernels: 149 us -> 113 us  [backward(): pl.pallas_call(functools.partial(backward_kernel, dims, fsdp, sp, shapes,...]
    unnamed x16 -> x22, local copies, waits for them, and re-layouts: 8.29 us -> 5.03 us
where the time goes in v2:
time: 341 us
  Pallas kernels  313 us (92%)
  local copies, waits for them, and re-layouts  20.6 us (6%)
  other arithmetic  4.51 us (1%)
    pallas_call x1, Pallas kernels, backward(): pl.pallas_call(functools.partial(backward_kernel, dims, fsdp, sp, shapes,...  113 us
    pallas_call x1, Pallas kernels, attention(): pl.pallas_call(functools.partial(attention_kernel, sp, heads), out_shape=...  87.9 us
    pallas_call x1, Pallas kernels, gather(): pl.pallas_call(functools.partial(gather_kernel, dims, fsdp, sp, shapes),...  85.8 us
    pallas_call x1, Pallas kernels, forward(): pl.pallas_call(functools.partial(forward_kernel, sp), out_shape=[jax.Shap...  26.6 us

profile of v2, /device:TPU:0, one launch (start us, length us, event | category | flops | bytes accessed | tf_op | source)
XLA Modules:
  0.0 340.6 jit_solution(2021396084919465989)
XLA Ops:
  1.9 0.8 fusion.6
  2.7 1.2 concatenate.19.nums.refs_0_
  5.3 0.9 reshape.150
  7.3 1.1 reshape.151
  8.4 0.9 dynamic-slice_reduce_fusion
  9.3 0.7 reshape_reshape.7.refs_3_
  10.0 85.8 %gather.1 = (bf16[4,2,2,2,144,512]{5,4,3,2,1,0:T(8,128)(2,1)}, bf16[4,2,2,2,144,512]{5,4,3,2,1,0:T(8,128)(2,1)}, bf16[4,2,2,1,32,768]{5,4,3,2,1,0:T(8,128)(2,1)}...) custom-call(bf16[2,144,512]{2,1,0:T(8,128)(2,1)} %bitcast.77, ...), custom_call_target="tpu_custom_call" | custom-call | tf_op jit(solution)/shard_map/gather/pallas_call | solution.py:223
  95.8 1.3 reshape.154.scales.refs_3_
  97.1 0.8 slice.32
  97.9 0.9 slice_reduce_fusion
  99.6 26.6 %forward.1 = (f32[8,64,512]{2,1,0:T(8,128)}, bf16[8,64,512]{2,1,0:T(8,128)(2,1)}, f32[8,64,512]{2,1,0:T(8,128)}, bf16[3,10,64,512]{3,2,1,0:T(8,128)(2,1)}, bf16[...) custom-call(f32[30]{0:T(128)} %concatenate.19.nums.refs_0_, bf16[8,64,512]{2,1,0:T(8,128)(2,1)} %bitcast.64, ...), custom_call_target="tpu_custom_call" | custom-call | tf_op jit(solution)/shard_map/forward/pallas_call | solution.py:700
  126.2 87.9 %attention.1 = (bf16[512,512]{1,0:T(8,128)(2,1)}, f32[512,512]{1,0:T(8,128)}, bf16[512,768]{1,0:T(8,128)(2,1)}, bf16[2048,512]{1,0:T(8,128)(2,1)}, bf16[512,512]{1,0:T(8,128)(2,1)}, /*index=5*/f32[128,2048]{1,0:T(8,128)}) custom-call(f32[30]{0:T(128)} %concatenate.19.nums.refs_0_, bf16[512,512]{1,0:T(8,128)(2,1)} %bitcast.75, bf16[128,2048]{1,0:T(8,128)(2,1)} %bitcast.73, ...), custom_call_target="tpu_custom_call" | custom-call | tf_op jit(solution)/shard_map/attention/pallas_call | solution.py:924
  214.0 112.8 %backward.1 = (f32[2,144,512]{2,1,0:T(8,128)}, f32[2,144,512]{2,1,0:T(8,128)}, f32[2,128,512]{2,1,0:T(8,128)}, f32[2,32,768]{2,1,0:T(8,128)}, f32[2,16,512]{2,1,...) custom-call(f32[30]{0:T(128)} %concatenate.19.nums.refs_0_, ...), custom_call_target="tpu_custom_call" | custom-call | tf_op jit(solution)/shard_map/backward/pallas_call | solution.py:1213
  326.9 1.5 bitcast_multiply_fusion
  329.7 0.8 convert_element_type.44
  330.5 1.0 reshape.166
  331.7 0.8 reshape.167
  332.5 1.0 fusion
  334.3 1.2 reshape.169
  335.6 0.8 copy.60
  336.4 1.0 copy.61
  337.3 1.0 copy.62
  338.3 0.8 copy.63
  339.1 0.8 copy.64
  (34 shorter events, 6.6 us)
Async XLA Ops:
  214.0 112.8 %copy-start.7 = (bf16[1,2048]{1,0:T(2,128)(2,1)S(1)}, bf16[1,2048]{1,0:T(2,128)(2,1)}, u32[]{:S(2)}) copy-start(bf16[1,2048]{1,0:T(2,128)(2,1)} %param.15) | copy-start | bytes 12292
  326.9 6.7 %copy-start.5 = (f32[2,128,512]{2,1,0:T(8,128)S(1)}, f32[2,128,512]{2,1,0:T(8,128)}, u32[]{:S(2)}) copy-start(f32[2,128,512]{2,1,0:T(8,128)} %get-tuple-element.67) | copy-start | bytes 1572868
  331.7 3.9 %copy-start.4 = (bf16[512,512]{1,0:T(8,128)(2,1)S(1)}, bf16[512,512]{1,0:T(8,128)(2,1)}, u32[]{:S(2)}) copy-start(bf16[512,512]{1,0:T(8,128)(2,1)} %get-tuple-element.50) | copy-start | bytes 1572868
  333.6 2.8 copy-start.1
  334.3 3.0 copy-start
  336.4 2.0 copy-start.3
  337.3 1.8 copy-start.2
  337.3 2.6 copy-start.6

commit v3 on v2

--- a/solution.py
+++ b/solution.py
@@ -59,189 +59,139 @@
     return copies
 
 
-def gather_kernel(dims, fsdp, sp, shapes, *refs):
-    zs, ys, cs = dims
-    count = len(shapes)
-    shards, tiles, table = refs[:count], refs[count], refs[count + 1]
-    refs = refs[count + 2 :]
-    outs, tiles_out, scales_out = refs[:count], refs[count], refs[count + 1]
-    refs = refs[count + 2 :]
-    bufs, got, part, part_in = refs[:count], refs[count], refs[count + 1], refs[count + 2]
-    zsend, zrecv, ysend, yrecv, xsend, xrecv, csend, crecv, local, tsem, psem = refs[count + 3 :]
-    me, x = lax.axis_index("fsdp"), lax.axis_index("sp")
-    z, y, c = me // (ys * cs), (me // cs) % ys, me % cs
-
-    def dev(zz, yy, cc):
-        return ((zz * ys + yy) * cs + cc, x)
-
-    peers = [((me + d) % fsdp, x) for d in range(1, fsdp)]
-    peers += [(me, (x + d) % sp) for d in range(1, sp)]
-    greet(peers)
-    flying = tiles_start(fsdp, tiles, got, tsem.at[0], tsem.at[1], lambda ref, to: ref.at[to])
-
-    def owner(dz, dy):
-        return (z - dz + zs) % zs, (y - dy + ys) % ys
-
-    def piece(a):
-        return x if shapes[a][0] > 1 else 0
-
-    def zcopy(a, dz):
-        h = piece(a)
+def span(index, rows, size):
+    return pl.ds(pl.multiple_of(index * rows, 16 if rows % 16 == 0 else 8), size)
+
+
+class Gather:
+    def __init__(self, dims, sp, shapes, shards, homes, sems):
+        self.dims, self.sp, self.shapes, self.shards, self.homes = dims, sp, shapes, shards, homes
+        self.zsem, self.ysem, self.xsem, self.csem = sems
+        zs, ys, cs = dims
+        self.me, self.x = lax.axis_index("fsdp"), lax.axis_index("sp")
+        self.z, self.y, self.c = self.me // (ys * cs), (self.me // cs) % ys, self.me % cs
+        self.flying = []
+
+    def dev(self, zz, yy, cc):
+        return ((zz * self.dims[1] + yy) * self.dims[2] + cc, self.x)
+
+    def launch(self, copy):
+        copy.start()
+        self.flying.append(copy)
+
+    def owner(self, dz, dy):
+        zs, ys, _ = self.dims
+        return (self.z - dz + zs) % zs, (self.y - dy + ys) % ys
+
+    def piece(self, a):
+        return self.x if self.shapes[a][0] > 1 else 0
+
+    def home(self, a, zz, yy, cc, k=None):
+        h, rows, _ = self.shapes[a]
+        index = (zz * self.dims[1] + yy) * self.dims[2] + cc
+        if k is None:
+            return self.homes[a].at[span(index, h * rows, h * rows)]
+        return self.homes[a].at[span(index * h + k, rows, rows)]
+
+    def mine(self, a):
+        h, rows, _ = self.shapes[a]
+        return self.shards[a].at[span(self.piece(a), rows, rows)] if h > 1 else self.shards[a]
+
+    def zcopy(self, a, dz):
         return remote(
-            shards[a].at[h],
-            outs[a].at[z, y, c, h],
-            zsend.at[a, dz],
-            zrecv.at[a, dz],
-            dev((z + dz) % zs, y, c),
-        )
-
-    def ycopy(a, dz, dy):
-        h = piece(a)
-        zz, _ = owner(dz, 0)
-        src = shards[a].at[h] if dz == 0 else outs[a].at[zz, y, c, h]
+            self.mine(a),
+            self.home(a, self.z, self.y, self.c, self.piece(a)),
+            self.zsem.at[0, a, dz],
+            self.zsem.at[1, a, dz],
+            self.dev((self.z + dz) % self.dims[0], self.y, self.c),
+        )
+
+    def ycopy(self, a, dz, dy):
+        zz, _ = self.owner(dz, 0)
+        place = self.home(a, zz, self.y, self.c, self.piece(a))
+        return remote(
+            self.mine(a) if dz == 0 else place,
+            place,
+            self.ysem.at[0, a, dz, dy],
+            self.ysem.at[1, a, dz, dy],
+            self.dev(self.z, (self.y + dy) % self.dims[1], self.c),
+        )
+
+    def xcopy(self, a, dz, dy, dx):
+        zz, yy = self.owner(dz, dy)
+        place = self.home(a, zz, yy, self.c, self.x)
+        return remote(
+            place,
+            place,
+            self.xsem.at[0, a, dz, dy, dx],
+            self.xsem.at[1, a, dz, dy, dx],
+            (self.me, (self.x + dx) % self.sp),
+        )
+
+    def ccopy(self, a, dz, dy, dx):
+        zz, yy = self.owner(dz, dy)
+        if dz == 0 and dy == 0:
+            src, dst = self.shards[a], self.home(a, zz, yy, self.c)
+        else:
+            k = (self.x - dx + self.sp) % self.sp if self.shapes[a][0] > 1 else 0
+            src = dst = self.home(a, zz, yy, self.c, k)
         return remote(
             src,
-            outs[a].at[zz, y, c, h],
-            ysend.at[a, dz, dy],
-            yrecv.at[a, dz, dy],
-            dev(z, (y + dy) % ys, c),
-        )
-
-    def xcopy(a, dz, dy, dx):
-        zz, yy = owner(dz, dy)
-        return remote(
-            outs[a].at[zz, yy, c, x],
-            outs[a].at[zz, yy, c, x],
-            xsend.at[a, dz, dy, dx],
-            xrecv.at[a, dz, dy, dx],
-            (me, (x + dx) % sp),
-        )
-
-    def ccopy(a, dz, dy, dx):
-        zz, yy = owner(dz, dy)
-        if dz == 0 and dy == 0:
-            src, dst = shards[a], outs[a].at[zz, yy, c]
-        else:
-            h = (x - dx + sp) % sp if shapes[a][0] > 1 else 0
-            src = dst = outs[a].at[zz, yy, c, h]
-        return remote(src, dst, csend.at[a, dz, dy, dx], crecv.at[a, dz, dy, dx], dev(z, y, 1 - c))
-
-    def launch(copy):
-        copy.start()
-        flying.append(copy)
-
-    def onward(a, dz, dy):
-        if shapes[a][0] > 1:
-            for dx in range(1, sp):
-                launch(xcopy(a, dz, dy, dx))
-        launch(ccopy(a, dz, dy, 0))
-
-    for a in range(count):
-        for dz in range(1, zs):
-            launch(zcopy(a, dz))
-        for dy in range(1, ys):
-            launch(ycopy(a, 0, dy))
-        launch(ccopy(a, 0, 0, 0))
-        pltpu.make_async_copy(shards[a], bufs[a], local.at[a]).start()
-
-    got[me] = tiles[me]
-    for copy in flying[: fsdp - 1]:
-        copy.wait_recv()
-    rows = got[:, 0, :].astype(BF16)
-    for j in range(8):
-        part[:, j, :] = jnp.dot(
-            rows, table[:, j * 128 : (j + 1) * 128], preferred_element_type=F32
-        )
-    part_in[me] = part[me]
-    for a in range(count):
-        pltpu.make_async_copy(shards[a], bufs[a], local.at[a]).wait()
-        pltpu.make_async_copy(bufs[a], outs[a].at[z, y, c], local.at[a]).start()
-    second = tiles_start(fsdp, part, part_in, psem.at[0], psem.at[1], lambda ref, to: ref.at[to])
-    flying += second
-
-    def over_z(a):
-        for dz in range(1, zs):
-            zcopy(a, dz).wait_recv()
-            for dy in range(1, ys):
-                launch(ycopy(a, dz, dy))
-            onward(a, dz, 0)
-
-    def over_y(a):
-        for dz in range(zs):
-            for dy in range(1, ys):
-                ycopy(a, dz, dy).wait_recv()
-                onward(a, dz, dy)
-
-    def over_x(a):
-        if shapes[a][0] > 1:
-            for dz in range(zs):
-                for dy in range(ys):
+            dst,
+            self.csem.at[0, a, dz, dy, dx],
+            self.csem.at[1, a, dz, dy, dx],
+            self.dev(self.z, self.y, 1 - self.c),
+        )
+
+    def onward(self, a, dz, dy):
+        if self.shapes[a][0] > 1:
+            for dx in range(1, self.sp):
+                self.launch(self.xcopy(a, dz, dy, dx))
+        self.launch(self.ccopy(a, dz, dy, 0))
+
+    def start(self, a):
+        for dz in range(1, self.dims[0]):
+            self.launch(self.zcopy(a, dz))
+        for dy in range(1, self.dims[1]):
+            self.launch(self.ycopy(a, 0, dy))
+        self.launch(self.ccopy(a, 0, 0, 0))
+
+    def over_z(self, a):
+        for dz in range(1, self.dims[0]):
+            self.zcopy(a, dz).wait_recv()
+            for dy in range(1, self.dims[1]):
+                self.launch(self.ycopy(a, dz, dy))
+            self.onward(a, dz, 0)
+
+    def over_y(self, a):
+        for dz in range(self.dims[0]):
+            for dy in range(1, self.dims[1]):
+                self.ycopy(a, dz, dy).wait_recv()
+                self.onward(a, dz, dy)
+
+    def over_x(self, a):
+        if self.shapes[a][0] > 1:
+            for dz in range(self.dims[0]):
+                for dy in range(self.dims[1]):
                     if dz + dy:
-                        for dx in range(1, sp):
-                            xcopy(a, dz, dy, dx).wait_recv()
-                            launch(ccopy(a, dz, dy, dx))
-
-    for step in range(count + 2):
-        if step < count:
-            over_z(step)
-        if 1 <= step <= count:
-            over_y(step - 1)
-        if step >= 2:
-            over_x(step - 2)
-    for copy in second:
-        copy.wait_recv()
-    total = part_in[0]
-    for f in range(1, fsdp):
-        total = total + part_in[f]
-    scales_out[...] = total
-    tiles_out[...] = got[...]
-    for a in range(count):
-        for dz in range(zs):
-            for dy in range(ys):
-                many = sp if shapes[a][0] > 1 and dz + dy else 1
+                        for dx in range(1, self.sp):
+                            self.xcopy(a, dz, dy, dx).wait_recv()
+                            self.launch(self.ccopy(a, dz, dy, dx))
+
+    def finish(self, a):
+        for dz in range(self.dims[0]):
+            for dy in range(self.dims[1]):
+                many = self.sp if self.shapes[a][0] > 1 and dz + dy else 1
                 for dx in range(many):
-                    ccopy(a, dz, dy, dx).wait_recv()
-        pltpu.make_async_copy(bufs[a], outs[a].at[z, y, c], local.at[a]).wait()
-    for copy in flying:
-        copy.wait_send()
+                    self.ccopy(a, dz, dy, dx).wait_recv()
+
+    def drain(self):
+        for copy in self.flying:
+            copy.wait_send()
 
 
 def parts_of(rows, sp):
     return sp if rows % (16 * sp) == 0 else 1
-
-
-def gather(shards, kinds, tiles, table, fsdp, sp):
-    dims = sizes_of(fsdp, sp)
-    zs, ys, cs = dims
-    count = len(shards)
-    split = []
-    for shard, kind in zip(shards, kinds, strict=True):
-        rows, width = shard.shape
-        h = parts_of(rows, sp) if kind else 1
-        split.append(shard.reshape(h, rows // h, width))
-    shapes = [s.shape for s in split]
-    outs = pl.pallas_call(
-        functools.partial(gather_kernel, dims, fsdp, sp, shapes),
-        out_shape=[jax.ShapeDtypeStruct(dims + s, BF16) for s in shapes]
-        + [
-            jax.ShapeDtypeStruct((fsdp, 8, 128), F32),
-            jax.ShapeDtypeStruct((8, 128), F32),
-        ],
-        in_specs=[ANY] * count + [VMEM] * 2,
-        out_specs=[ANY] * count + [VMEM] * 2,
-        scratch_shapes=[pltpu.VMEM(s, BF16) for s in shapes]
-        + [pltpu.VMEM((fsdp, 8, 128), F32)] * 3
-        + [DMA((count, zs))] * 2
-        + [DMA((count, zs, ys))] * 2
-        + [DMA((count, zs, ys, sp))] * 4
-        + [DMA((count,)), DMA((2, fsdp)), DMA((2, fsdp))],
-        compiler_params=params(0),
-        name="gather",
-    )(*split, tiles, table)
-    whole = [
-        o.reshape(fsdp * s.shape[0], s.shape[1]) for o, s in zip(outs[:count], shards, strict=True)
-    ]
-    return whole, outs[count], outs[count + 1]
 
 
 def add_rows(rows, first, second, put):
@@ -281,15 +231,15 @@
         zs, ys, cs = self.dims
         h, rows, _ = self.shapes[a]
         owner = (((self.z + dz) % zs) * ys + (self.y + dy) % ys) * cs + cc
-        return self.grads[a].at[pl.ds(pl.multiple_of(owner * (h * rows), 16), h * rows)]
+        return self.grads[a].at[span(owner, h * rows, h * rows)]
 
     def part(self, a, dz, dy, k):
         zs, ys, cs = self.dims
         h, rows, _ = self.shapes[a]
         if self.own[a] is not None:
-            return self.own[a].at[dz, dy, pl.ds(pl.multiple_of(k * rows, 16), rows)]
+            return self.own[a].at[dz, dy, span(k, rows, rows)]
         owner = (((self.z + dz) % zs) * ys + (self.y + dy) % ys) * cs + self.c
-        return self.grads[a].at[pl.ds(pl.multiple_of((owner * h + k) * rows, 16), rows)]
+        return self.grads[a].at[span(owner * h + k, rows, rows)]
 
     def piece(self, a):
         return self.x if self.shapes[a][0] > 1 else 0
@@ -595,39 +545,42 @@
     return mean, lax.rsqrt(square / count + EPSILON)
 
 
-def forward_kernel(
-    sp,
-    nums,
-    image,
-    gains,
-    scales,
-    w1,
-    w2,
-    resid,
-    normed,
-    conv_out,
-    s1,
-    s2,
-    stats,
-    w1v,
-    w2v,
-    edge1,
-    edge2,
-    acc,
-    sums,
-    ssem,
-    hsem,
-    wsem,
-):
+def forward_kernel(dims, fsdp, sp, shapes, kinds, *refs):
+    n = len(shapes)
+    (nums, image, tiles, table), shards, refs = refs[:4], refs[4 : 4 + n], refs[4 + n :]
+    (resid, normed, conv_out, s1, s2, stats, gains, scales, got), refs = refs[:9], refs[9:]
+    outs, refs = refs[:n], refs[n:]
+    (w1v, w2v), bufs, refs = refs[:2], refs[2:n], refs[n:]
+    (edge1, edge2, acc, sums, part, part_in), refs = refs[:6], refs[6:]
+    (ssem, hsem, wsem, lsem, tsem, psem), sems = refs[:6], refs[6:]
+    move = Gather(dims, sp, shapes, shards[:2] + bufs, (w1v, w2v) + outs[2:], sems)
+    me, x = move.me, move.x
+    late = list(range(2, n))
     rows, columns = image.shape[0], image.shape[1]
     swap = Swap(sp, sums, ssem, hsem)
-    load1 = pltpu.make_async_copy(w1, w1v, wsem.at[0])
-    load2 = pltpu.make_async_copy(w2, w2v, wsem.at[1])
-    load1.start()
-    load2.start()
+    homes = [move.home(a, move.z, move.y, move.c) for a in range(n)]
+    loads = [pltpu.make_async_copy(shards[a], homes[a], wsem.at[a]) for a in range(2)]
+    staged = []
+    for a in late:
+        width = shapes[a][2] // kinds[a]
+        for j in range(kinds[a]):
+            if shards[a].shape[1] == shapes[a][2]:
+                src = shards[a]
+            else:
+                start = pl.multiple_of((j * sp + x) * width, 128)
+                src = shards[a].at[:, pl.ds(start, width)]
+            dst = bufs[a - 2].at[:, j * width : (j + 1) * width]
+            staged.append((a, pltpu.make_async_copy(src, dst, lsem.at[a, j])))
+    for load in loads + [copy for _, copy in staged]:
+        load.start()
     edge1[...] = jnp.zeros_like(edge1)
     edge2[...] = jnp.zeros_like(edge2)
-    greet(swap.peers())
+    greet(swap.peers() + [((me + d) % fsdp, x) for d in range(1, fsdp)])
+    first_tiles = tiles_start(
+        fsdp, tiles, got, tsem.at[0], tsem.at[1], lambda ref, to: ref.at[to]
+    )
+    got[me] = tiles[me]
+    move.start(0)
     swap.edges_start(0, image.at[0], image.at[rows - 1], edge1)
     count = nums[rows + 2]
     counts = [nums[rows + 3 + i] for i in range(sp)]
@@ -640,9 +593,35 @@
         return image[r].astype(F32) * mask(r)
 
     swap.sums_start(0, local_moments(rows, masked, mask, held))
+    move.start(1)
+    for _, copy in staged:
+        copy.wait()
+    for a in late:
+        move.start(a)
+    stores = [pltpu.make_async_copy(bufs[a - 2], homes[a], wsem.at[a]) for a in late]
+    for copy in stores:
+        copy.start()
+    for copy in first_tiles:
+        copy.wait_recv()
+    share = C // fsdp
+    many = 128 // share
+    for b in range(C // 128):
+        block = got[b * many]
+        for f in range(b * many + 1, (b + 1) * many):
+            block = block + got[f]
+        gains[:, b * 128 : (b + 1) * 128] = block
+    act = got[:, 0, :].astype(BF16)
+    for j in range(8):
+        part[:, j, :] = jnp.dot(
+            act, table[:, j * 128 : (j + 1) * 128], preferred_element_type=F32
+        )
+    part_in[me] = part[me]
+    second_tiles = tiles_start(
+        fsdp, part, part_in, psem.at[0], psem.at[1], lambda ref, to: ref.at[to]
+    )
     mean1, inv1 = joint_moments(swap.sums_wait(0), counts, count)
     swap.edges_wait(0, image.at[0], image.at[rows - 1], edge1)
-    g1, g2, g3 = gains[0:1], gains[1:2], gains[2:3]
+    g1, g2, g3 = gains[1:2], gains[2:3], gains[3:4]
 
     def first(at, value):
         m = nums[at]
@@ -652,7 +631,14 @@
     lax.fori_loop(0, rows, lambda r, _: (first(r + 1, image[r]), 0)[1], 0)
     first(0, edge1[0])
     first(rows + 1, edge1[1])
-    load1.wait()
+    move.over_z(0)
+    move.over_y(0)
+    move.over_z(1)
+    move.over_x(0)
+    loads[0].wait()
+    move.finish(0)
+    pltpu.make_async_copy(w1v, outs[0], wsem.at[0]).start()
+    move.over_y(1)
     taps(rows, columns, s1, w1v, acc, False)
 
     def keep(r, _):
@@ -664,6 +650,15 @@
     swap.sums_start(1, local_moments(rows, lambda r: conv_out[r], mask, held))
     mean2, inv2 = joint_moments(swap.sums_wait(1), counts, count)
     swap.edges_wait(1, conv_out.at[0], conv_out.at[rows - 1], edge2)
+    for copy in second_tiles:
+        copy.wait_recv()
+    total = part_in[0]
+    for f in range(1, fsdp):
+        total = total + part_in[f]
+    scales[...] = jnp.zeros_like(scales)
+    for j in range(8):
+        lanes = slice(j % 4 * 128, (j % 4 + 1) * 128)
+        scales[j // 4 : j // 4 + 1, lanes] = total[j : j + 1]
     scale, shift = 1.0 + scales[0:1], scales[1:2]
 
     def second(at, value):
@@ -674,8 +669,15 @@
     lax.fori_loop(0, rows, lambda r, _: (second(r + 1, conv_out[r]), 0)[1], 0)
     second(0, edge2[0])
     second(rows + 1, edge2[1])
-    load2.wait()
+    for a in late:
+        move.over_z(a)
+    move.over_x(1)
+    loads[1].wait()
+    move.finish(1)
+    pltpu.make_async_copy(w2v, outs[1], wsem.at[1]).start()
     taps(rows, columns, s2, w2v, acc, False)
+    for a in late:
+        move.over_y(a)
 
     def add(r, _):
         resid[r] = masked(r) + acc[r] * mask(r)
@@ -691,14 +693,35 @@
 
     lax.fori_loop(0, rows, third, 0)
     stats[...] = stack_rows(mean1, inv1, mean2, inv2, mean3, inv3)
-
-
-def forward(nums, image, gains, scales, w1, w2, sp):
+    for a in late:
+        move.over_x(a)
+    for a in late:
+        move.finish(a)
+        stores[a - 2].wait()
+    for copy in first_tiles + second_tiles:
+        copy.wait_send()
+    move.drain()
+    pltpu.make_async_copy(w1v, outs[0], wsem.at[0]).wait()
+    pltpu.make_async_copy(w2v, outs[1], wsem.at[1]).wait()
+
+
+def forward(nums, image, tiles, table, shards, kinds, fsdp, sp):
     rows, columns, _ = image.shape
     field = (rows, columns, C)
     shifted = (3, rows + 2, columns, C)
+    dims = sizes_of(fsdp, sp)
+    zs, ys, _ = dims
+    n = len(shards)
+    shapes = []
+    for shard, kind in zip(shards, kinds, strict=True):
+        r, width = shard.shape
+        h = 1 if kind else parts_of(r, sp)
+        shapes.append((h, r // h, width // sp if kind else width))
+    wholes = [jax.ShapeDtypeStruct((fsdp * h * r, w), BF16) for h, r, w in shapes]
+    staged = [pltpu.VMEM((h * r, w), BF16) for h, r, w in shapes[2:]]
+    tile = pltpu.VMEM((fsdp, 8, 128), F32)
     return pl.pallas_call(
-        functools.partial(forward_kernel, sp),
+        functools.partial(forward_kernel, dims, fsdp, sp, shapes, [max(k, 1) for k in kinds]),
         out_shape=[
             jax.ShapeDtypeStruct(field, F32),
             jax.ShapeDtypeStruct(field, BF16),
@@ -706,23 +729,39 @@
             jax.ShapeDtypeStruct(shifted, BF16),
             jax.ShapeDtypeStruct(shifted, BF16),
             jax.ShapeDtypeStruct((8, C), F32),
-        ],
-        in_specs=[SMEM, VMEM, VMEM, VMEM, ANY, ANY],
-        out_specs=[VMEM] * 6,
+            jax.ShapeDtypeStruct((8, C), F32),
+            jax.ShapeDtypeStruct((8, C), F32),
+            jax.ShapeDtypeStruct((fsdp, 8, 128), F32),
+        ]
+        + wholes,
+        in_specs=[SMEM] + [VMEM] * 3 + [ANY] * n,
+        out_specs=[VMEM] * 9 + [ANY] * n,
         scratch_shapes=[
-            pltpu.VMEM(w1.shape, BF16),
-            pltpu.VMEM(w2.shape, BF16),
+            pltpu.VMEM(wholes[0].shape, BF16),
+            pltpu.VMEM(wholes[1].shape, BF16),
+        ]
+        + staged
+        + [
             pltpu.VMEM((2, columns, C), BF16),
             pltpu.VMEM((2, columns, C), F32),
             pltpu.VMEM(field, F32),
             pltpu.VMEM((3, sp, 8, C), F32),
+            tile,
+            tile,
             DMA((2, 3, sp)),
             DMA((2, 2, 2)),
-            DMA((2,)),
+            DMA((n,)),
+            DMA((n, 3)),
+            DMA((2, fsdp)),
+            DMA((2, fsdp)),
+            DMA((2, n, zs)),
+            DMA((2, n, zs, ys)),
+            DMA((2, n, zs, ys, sp)),
+            DMA((2, n, zs, ys, sp)),
         ],
         compiler_params=params(1),
         name="forward",
-    )(nums, image, gains, scales, w1, w2)
+    )(nums, image, tiles, table, *shards)
 
 
 def attention_kernel(
@@ -989,7 +1028,7 @@
     for a in late:
         total_of.start(a)
     count = nums[rows + 2]
-    g1, g2, g3 = gains[0:1], gains[1:2], gains[2:3]
+    g1, g2, g3 = gains[1:2], gains[2:3], gains[3:4]
     mean1, inv1, mean2, inv2, mean3, inv3 = (stats[k : k + 1] for k in range(6))
 
     def mask(r):
@@ -1286,7 +1325,6 @@
 ):
     rows, columns = image.shape[1], image.shape[2]
     fsdp, sp = lax.axis_size("fsdp"), lax.axis_size("sp")
-    x = lax.axis_index("sp")
     heads = C // HEAD // sp
     width = heads * HEAD
     share = gain_one.shape[0]
@@ -1295,42 +1333,34 @@
     emb_float = embedding.astype(F32)
     emb_act = jax.nn.silu(emb_float).astype(BF16)
 
-    def columns_of(weight, kinds):
-        blocks = weight.reshape(weight.shape[0], kinds, sp, width)
-        return lax.dynamic_index_in_dim(blocks, x, 2, keepdims=False).reshape(weight.shape[0], -1)
-
     def lanes(array):
         return jnp.pad(array, [(0, 0)] * (array.ndim - 1) + [(0, 128 - array.shape[-1])])
 
-    gains_row = jnp.concatenate([gain_one, gain_two, gain_three]).astype(F32)
-    tiles = jnp.stack(
+    many = 128 // share
+    place = lax.broadcasted_iota(jnp.int32, (3, 128), 1) // share == lax.axis_index("fsdp") % many
+    gain_rows = jnp.stack([gain_one, gain_two, gain_three]).astype(F32)
+    gain_rows = jnp.where(place, jnp.tile(gain_rows, (1, many)), 0.0)
+    tiles = jnp.concatenate(
         [
-            lanes(emb_act.astype(F32).reshape(fsdp, emb_rows)),
-            jnp.broadcast_to(lanes(gains_row[None]), (fsdp, 128)),
+            lanes(emb_act.astype(F32).reshape(fsdp, 1, emb_rows)),
+            jnp.broadcast_to(gain_rows[None], (fsdp, 3, 128)),
+            jnp.zeros((fsdp, 4, 128), F32),
         ],
         axis=1,
     )
-    tiles = jnp.pad(tiles, ((0, 0), (0, 6), (0, 0)))
     table = jnp.pad(emb_proj, ((0, 128 - emb_rows), (0, 0)))
-    (w1, w2, wq, wt, wo), tiles_in, scales = gather(
-        [
-            conv_one,
-            conv_two,
-            columns_of(qkv_proj, 3),
-            columns_of(text_proj, 2),
-            out_proj,
-        ],
-        [True, True, False, False, True],
+    resid, normed, conv_out, s1, s2, stats, gains, scales, tiles_in, w1, w2, wt, wq, wo = forward(
+        nums,
+        image[0],
         tiles,
         table,
+        [conv_one, conv_two, text_proj, qkv_proj, out_proj],
+        [0, 0, 2, 3, 0],
         fsdp,
         sp,
     )
-    scales = scales.reshape(2, C)
-    gains = tiles_in[:, 1, : 3 * share].reshape(fsdp, 3, share).transpose(1, 0, 2).reshape(3, C)
     emb_cols = tiles_in[:, 0, :emb_rows].astype(BF16)
     pixels = rows * columns
-    resid, normed, conv_out, s1, s2, stats = forward(nums, image[0], gains, scales, w1, w2, sp)
     output, gnorm, gq, gt, go, gtext = attention(
         nums,
         normed.reshape(pixels, C),

time: 341 us -> 325 us (0.953)
  Pallas kernels: 313 us -> 305 us
  local copies, waits for them, and re-layouts: 20.6 us -> 13.1 us
    pallas_call x2 -> x1, Pallas kernels: 112 us -> 97.9 us  [forward(): pl.pallas_call(functools.partial(forward_kernel, dims, fsdp, sp, shapes,...]
    pallas_call x1, Pallas kernels: 87.9 us -> 93.3 us  [attention(): pl.pallas_call(functools.partial(attention_kernel, sp, heads), out_shape=...]
    reshape x4 -> x0, local copies, waits for them, and re-layouts: 4.03 us -> none  [the longest x2 2.06 us: columns_of(): blocks = weight.reshape(weight.shape[0], kinds, sp, width)]
where the time goes in v3:
time: 325 us
  Pallas kernels  305 us (94%)
  local copies, waits for them, and re-layouts  13.1 us (4%)
  other arithmetic  4.52 us (1%)
    pallas_call x1, Pallas kernels, backward(): pl.pallas_call(functools.partial(backward_kernel, dims, fsdp, sp, shapes,...  113 us
    pallas_call x1, Pallas kernels, forward(): pl.pallas_call(functools.partial(forward_kernel, dims, fsdp, sp, shapes,...  97.9 us
    pallas_call x1, Pallas kernels, attention(): pl.pallas_call(functools.partial(attention_kernel, sp, heads), out_shape=...  93.3 us

profile of v3, /device:TPU:0, one launch (start us, length us, event | category | flops | bytes accessed | tf_op | source)
XLA Modules:
  0.0 324.8 jit_solution(14209350202621900317)
XLA Ops:
  1.3 0.6 dynamic_slice.6
  1.9 1.2 concatenate.10.refs_0_.nums
  3.3 0.7 maximum_convert_fusion
  4.1 0.7 bitcast_convert_fusion
  4.8 0.7 maximum_maximum_fusion.refs_2_
  5.5 97.9 %forward.1 = (f32[8,64,512]{2,1,0:T(8,128)}, bf16[8,64,512]{2,1,0:T(8,128)(2,1)}, f32[8,64,512]{2,1,0:T(8,128)}, bf16[3,10,64,512]{3,2,1,0:T(8,128)(2,1)}, bf16[...) custom-call(f32[30]{0:T(128)} %concatenate.10.refs_0_.nums, ...), custom_call_target="tpu_custom_call" | custom-call | tf_op jit(solution)/shard_map/forward/pallas_call | solution.py:723
  103.4 0.8 slice.27
  104.3 93.3 %attention.1 = (bf16[512,512]{1,0:T(8,128)(2,1)}, f32[512,512]{1,0:T(8,128)}, bf16[512,768]{1,0:T(8,128)(2,1)}, bf16[2048,512]{1,0:T(8,128)(2,1)}, bf16[512,512]{1,0:T(8,128)(2,1)}, /*index=5*/f32[128,2048]{1,0:T(8,128)}) custom-call(f32[30]{0:T(128)} %concatenate.10.refs_0_.nums, bf16[512,512]{1,0:T(8,128)(2,1)} %bitcast.54, bf16[128,2048]{1,0:T(8,128)(2,1)} %bitcast.53, ...), custom_call_target="tpu_custom_call" | custom-call | tf_op jit(solution)/shard_map/attention/pallas_call | solution.py:963
  197.6 113.5 %backward.1 = (f32[2,144,512]{2,1,0:T(8,128)}, f32[2,144,512]{2,1,0:T(8,128)}, f32[2,128,512]{2,1,0:T(8,128)}, f32[2,32,768]{2,1,0:T(8,128)}, f32[2,16,512]{2,1,...) custom-call(f32[30]{0:T(128)} %concatenate.10.refs_0_.nums, ...), custom_call_target="tpu_custom_call" | custom-call | tf_op jit(solution)/shard_map/backward/pallas_call | solution.py:1252
  311.1 1.5 bitcast_multiply_fusion
  312.6 0.7 constant_dynamic-slice_fusion
  313.3 0.5 slice_bitcast_fusion
  313.8 0.8 convert_element_type.40
  314.7 1.0 reshape.157
  315.9 0.8 reshape.158
  316.7 1.0 fusion
  318.1 0.4 copy.31
  318.5 1.2 reshape.160
  319.7 0.8 copy.49
  320.5 1.0 copy.50
  321.5 1.0 copy.51
  322.5 0.8 copy.52
  323.3 0.8 copy.53
  324.1 0.6 copy.54
  (29 shorter events, 0.7 us)
Async XLA Ops:
  197.6 113.5 %copy-start.7 = (bf16[1,2048]{1,0:T(2,128)(2,1)S(1)}, bf16[1,2048]{1,0:T(2,128)(2,1)}, u32[]{:S(2)}) copy-start(bf16[1,2048]{1,0:T(2,128)(2,1)} %param.15) | copy-start | bytes 12292
  311.0 6.7 %copy-start.5 = (f32[2,128,512]{2,1,0:T(8,128)S(1)}, f32[2,128,512]{2,1,0:T(8,128)}, u32[]{:S(2)}) copy-start(f32[2,128,512]{2,1,0:T(8,128)} %get-tuple-element.69) | copy-start | bytes 1572868
  315.9 3.9 %copy-start.4 = (bf16[512,512]{1,0:T(8,128)(2,1)S(1)}, bf16[512,512]{1,0:T(8,128)(2,1)}, u32[]{:S(2)}) copy-start(bf16[512,512]{1,0:T(8,128)(2,1)} %get-tuple-element.47) | copy-start | bytes 1572868
  317.8 2.8 copy-start.1
  318.5 3.0 copy-start
  320.5 2.0 copy-start.3
  321.5 1.8 copy-start.2
  321.5 2.6 copy-start.6

commit v4 on v3

--- a/solution.py
+++ b/solution.py
@@ -63,9 +63,15 @@
     return pl.ds(pl.multiple_of(index * rows, 16 if rows % 16 == 0 else 8), size)
 
 
+def aligned(index, *steps):
+    if isinstance(index, int):
+        return index
+    return pl.multiple_of(index, 16 if all(step % 16 == 0 for step in steps) else 8)
+
+
 class Gather:
-    def __init__(self, dims, sp, shapes, shards, homes, sems):
-        self.dims, self.sp, self.shapes, self.shards, self.homes = dims, sp, shapes, shards, homes
+    def __init__(self, dims, sp, entries, sems):
+        self.dims, self.sp, self.entries = dims, sp, entries
         self.zsem, self.ysem, self.xsem, self.csem = sems
         zs, ys, cs = dims
         self.me, self.x = lax.axis_index("fsdp"), lax.axis_index("sp")
@@ -75,27 +81,36 @@
     def dev(self, zz, yy, cc):
         return ((zz * self.dims[1] + yy) * self.dims[2] + cc, self.x)
 
-    def launch(self, copy):
-        copy.start()
-        self.flying.append(copy)
+    def launch(self, make, *args):
+        make(*args).start()
+        self.flying.append((make, args))
 
     def owner(self, dz, dy):
         zs, ys, _ = self.dims
         return (self.z - dz + zs) % zs, (self.y - dy + ys) % ys
 
+    def split(self, a):
+        return self.entries[a][2] > 1
+
     def piece(self, a):
-        return self.x if self.shapes[a][0] > 1 else 0
+        return self.x if self.split(a) else 0
 
     def home(self, a, zz, yy, cc, k=None):
-        h, rows, _ = self.shapes[a]
-        index = (zz * self.dims[1] + yy) * self.dims[2] + cc
+        _, whole, h, rows, offset, stride = self.entries[a]
+        index = ((zz * self.dims[1] + yy) * self.dims[2] + cc) * stride + offset
         if k is None:
-            return self.homes[a].at[span(index, h * rows, h * rows)]
-        return self.homes[a].at[span(index * h + k, rows, rows)]
+            return whole.at[pl.ds(aligned(index, stride, offset), h * rows)]
+        return whole.at[pl.ds(aligned(index + k * rows, stride, offset, rows), rows)]
 
     def mine(self, a):
-        h, rows, _ = self.shapes[a]
-        return self.shards[a].at[span(self.piece(a), rows, rows)] if h > 1 else self.shards[a]
+        shard, _, h, rows, offset, stride = self.entries[a]
+        if h * rows == stride and h == 1:
+            return shard
+        return shard.at[pl.ds(aligned(offset + self.piece(a) * rows, offset, rows), rows)]
+
+    def own(self, a):
+        shard, _, h, rows, offset, stride = self.entries[a]
+        return shard if h * rows == stride else shard.at[offset : offset + h * rows]
 
     def zcopy(self, a, dz):
         return remote(
@@ -131,9 +146,9 @@
     def ccopy(self, a, dz, dy, dx):
         zz, yy = self.owner(dz, dy)
         if dz == 0 and dy == 0:
-            src, dst = self.shards[a], self.home(a, zz, yy, self.c)
+            src, dst = self.own(a), self.home(a, zz, yy, self.c)
         else:
-            k = (self.x - dx + self.sp) % self.sp if self.shapes[a][0] > 1 else 0
+            k = (self.x - dx + self.sp) % self.sp if self.split(a) else 0
             src = dst = self.home(a, zz, yy, self.c, k)
         return remote(
             src,
@@ -144,50 +159,56 @@
         )
 
     def onward(self, a, dz, dy):
-        if self.shapes[a][0] > 1:
+        if self.split(a):
             for dx in range(1, self.sp):
-                self.launch(self.xcopy(a, dz, dy, dx))
-        self.launch(self.ccopy(a, dz, dy, 0))
-
-    def start(self, a):
+                self.launch(self.xcopy, a, dz, dy, dx)
+        self.launch(self.ccopy, a, dz, dy, 0)
+
+    def start_z(self, a):
         for dz in range(1, self.dims[0]):
-            self.launch(self.zcopy(a, dz))
+            self.launch(self.zcopy, a, dz)
+
+    def start_y(self, a):
         for dy in range(1, self.dims[1]):
-            self.launch(self.ycopy(a, 0, dy))
-        self.launch(self.ccopy(a, 0, 0, 0))
-
-    def over_z(self, a):
-        for dz in range(1, self.dims[0]):
-            self.zcopy(a, dz).wait_recv()
-            for dy in range(1, self.dims[1]):
-                self.launch(self.ycopy(a, dz, dy))
-            self.onward(a, dz, 0)
-
-    def over_y(self, a):
-        for dz in range(self.dims[0]):
-            for dy in range(1, self.dims[1]):
-                self.ycopy(a, dz, dy).wait_recv()
-                self.onward(a, dz, dy)
+            self.launch(self.ycopy, a, 0, dy)
+        self.launch(self.ccopy, a, 0, 0, 0)
+
+    def from_z(self, a, dz):
+        self.zcopy(a, dz).wait_recv()
+        for dy in range(1, self.dims[1]):
+            self.launch(self.ycopy, a, dz, dy)
+        self.onward(a, dz, 0)
+
+    def from_y(self, a, dz):
+        for dy in range(1, self.dims[1]):
+            self.ycopy(a, dz, dy).wait_recv()
+            self.onward(a, dz, dy)
+
+    def relay(self, a, dz):
+        if 0 < dz < self.dims[0]:
+            self.from_z(a, dz)
+        if 0 < dz <= self.dims[0]:
+            self.from_y(a, dz - 1)
 
     def over_x(self, a):
-        if self.shapes[a][0] > 1:
+        if self.split(a):
             for dz in range(self.dims[0]):
                 for dy in range(self.dims[1]):
                     if dz + dy:
                         for dx in range(1, self.sp):
                             self.xcopy(a, dz, dy, dx).wait_recv()
-                            self.launch(self.ccopy(a, dz, dy, dx))
+                            self.launch(self.ccopy, a, dz, dy, dx)
 
     def finish(self, a):
         for dz in range(self.dims[0]):
             for dy in range(self.dims[1]):
-                many = self.sp if self.shapes[a][0] > 1 and dz + dy else 1
+                many = self.sp if self.split(a) and dz + dy else 1
                 for dx in range(many):
                     self.ccopy(a, dz, dy, dx).wait_recv()
 
     def drain(self):
-        for copy in self.flying:
-            copy.wait_send()
+        for make, args in self.flying:
+            make(*args).wait_send()
 
 
 def parts_of(rows, sp):
@@ -478,10 +499,12 @@
     dst[2, at] = jnp.where(col == columns - 1, 0.0, pltpu.roll(value, columns - 1, 0)).astype(BF16)
 
 
-def taps(rows, columns, shifted, weight, acc, back):
+def taps(rows, columns, shifted, weight, acc, back, hooks=()):
     pixels = rows * columns
 
     def body(t, _):
+        for k, hook in enumerate(hooks):
+            pl.when(t == k)(hook)
         total = None
         for dc in range(3):
             if back:
@@ -545,7 +568,7 @@
     return mean, lax.rsqrt(square / count + EPSILON)
 
 
-def forward_kernel(dims, fsdp, sp, shapes, kinds, *refs):
+def forward_kernel(dims, fsdp, sp, shapes, kinds, plan, *refs):
     n = len(shapes)
     (nums, image, tiles, table), shards, refs = refs[:4], refs[4 : 4 + n], refs[4 + n :]
     (resid, normed, conv_out, s1, s2, stats, gains, scales, got), refs = refs[:9], refs[9:]
@@ -553,25 +576,29 @@
     (w1v, w2v), bufs, refs = refs[:2], refs[2:n], refs[n:]
     (edge1, edge2, acc, sums, part, part_in), refs = refs[:6], refs[6:]
     (ssem, hsem, wsem, lsem, tsem, psem), sems = refs[:6], refs[6:]
-    move = Gather(dims, sp, shapes, shards[:2] + bufs, (w1v, w2v) + outs[2:], sems)
+    sources, wholes = shards[:2] + bufs, (w1v, w2v) + outs[2:]
+    entries = [(sources[a], wholes[a], h, r, at, shapes[a][0]) for a, h, r, at in plan]
+    move = Gather(dims, sp, entries, sems)
     me, x = move.me, move.x
-    late = list(range(2, n))
+    first_of, second_of, late = (
+        [e for e, p in enumerate(plan) if min(p[0], 2) == a] for a in range(3)
+    )
     rows, columns = image.shape[0], image.shape[1]
     swap = Swap(sp, sums, ssem, hsem)
-    homes = [move.home(a, move.z, move.y, move.c) for a in range(n)]
+    homes = [wholes[a].at[span(me, shapes[a][0], shapes[a][0])] for a in range(n)]
     loads = [pltpu.make_async_copy(shards[a], homes[a], wsem.at[a]) for a in range(2)]
     staged = []
-    for a in late:
-        width = shapes[a][2] // kinds[a]
+    for a in range(2, n):
+        width = shapes[a][1] // kinds[a]
         for j in range(kinds[a]):
-            if shards[a].shape[1] == shapes[a][2]:
+            if shards[a].shape[1] == shapes[a][1]:
                 src = shards[a]
             else:
                 start = pl.multiple_of((j * sp + x) * width, 128)
                 src = shards[a].at[:, pl.ds(start, width)]
             dst = bufs[a - 2].at[:, j * width : (j + 1) * width]
-            staged.append((a, pltpu.make_async_copy(src, dst, lsem.at[a, j])))
-    for load in loads + [copy for _, copy in staged]:
+            staged.append(pltpu.make_async_copy(src, dst, lsem.at[a, j]))
+    for load in loads + staged:
         load.start()
     edge1[...] = jnp.zeros_like(edge1)
     edge2[...] = jnp.zeros_like(edge2)
@@ -580,7 +607,9 @@
         fsdp, tiles, got, tsem.at[0], tsem.at[1], lambda ref, to: ref.at[to]
     )
     got[me] = tiles[me]
-    move.start(0)
+    for e in first_of:
+        move.start_y(e)
+        move.start_z(e)
     swap.edges_start(0, image.at[0], image.at[rows - 1], edge1)
     count = nums[rows + 2]
     counts = [nums[rows + 3 + i] for i in range(sp)]
@@ -593,12 +622,11 @@
         return image[r].astype(F32) * mask(r)
 
     swap.sums_start(0, local_moments(rows, masked, mask, held))
-    move.start(1)
-    for _, copy in staged:
+    for copy in staged:
         copy.wait()
-    for a in late:
-        move.start(a)
-    stores = [pltpu.make_async_copy(bufs[a - 2], homes[a], wsem.at[a]) for a in late]
+    for e in first_of:
+        move.relay(e, 1)
+    stores = [pltpu.make_async_copy(bufs[a - 2], homes[a], wsem.at[a]) for a in range(2, n)]
     for copy in stores:
         copy.start()
     for copy in first_tiles:
@@ -619,6 +647,8 @@
     second_tiles = tiles_start(
         fsdp, part, part_in, psem.at[0], psem.at[1], lambda ref, to: ref.at[to]
     )
+    for e in second_of + late:
+        move.start_z(e)
     mean1, inv1 = joint_moments(swap.sums_wait(0), counts, count)
     swap.edges_wait(0, image.at[0], image.at[rows - 1], edge1)
     g1, g2, g3 = gains[1:2], gains[2:3], gains[3:4]
@@ -631,15 +661,30 @@
     lax.fori_loop(0, rows, lambda r, _: (first(r + 1, image[r]), 0)[1], 0)
     first(0, edge1[0])
     first(rows + 1, edge1[1])
-    move.over_z(0)
-    move.over_y(0)
-    move.over_z(1)
-    move.over_x(0)
+    for dz in range(2, dims[0] + 1):
+        for e in first_of:
+            move.relay(e, dz)
+    for e in second_of:
+        move.start_y(e)
+        move.relay(e, 1)
+    for e in first_of:
+        move.over_x(e)
     loads[0].wait()
-    move.finish(0)
+    for e in first_of:
+        move.finish(e)
     pltpu.make_async_copy(w1v, outs[0], wsem.at[0]).start()
-    move.over_y(1)
-    taps(rows, columns, s1, w1v, acc, False)
+
+    def along(group, dz):
+        for e in group:
+            move.relay(e, dz)
+
+    zs = dims[0]
+    hooks = [functools.partial(along, second_of, dz) for dz in range(2, min(4, zs + 1))]
+    taps(rows, columns, s1, w1v, acc, False, hooks)
+    for dz in range(len(hooks) + 2, zs + 1):
+        along(second_of, dz)
+    for e in late:
+        move.start_y(e)
 
     def keep(r, _):
         conv_out[r] = acc[r] * mask(r)
@@ -648,6 +693,8 @@
     lax.fori_loop(0, rows, keep, 0)
     swap.edges_start(1, conv_out.at[0], conv_out.at[rows - 1], edge2)
     swap.sums_start(1, local_moments(rows, lambda r: conv_out[r], mask, held))
+    along(late, 1)
+    along(late, 2)
     mean2, inv2 = joint_moments(swap.sums_wait(1), counts, count)
     swap.edges_wait(1, conv_out.at[0], conv_out.at[rows - 1], edge2)
     for copy in second_tiles:
@@ -669,15 +716,16 @@
     lax.fori_loop(0, rows, lambda r, _: (second(r + 1, conv_out[r]), 0)[1], 0)
     second(0, edge2[0])
     second(rows + 1, edge2[1])
-    for a in late:
-        move.over_z(a)
-    move.over_x(1)
+    along(late, 3)
+    for e in second_of:
+        move.over_x(e)
     loads[1].wait()
-    move.finish(1)
+    for e in second_of:
+        move.finish(e)
     pltpu.make_async_copy(w2v, outs[1], wsem.at[1]).start()
     taps(rows, columns, s2, w2v, acc, False)
-    for a in late:
-        move.over_y(a)
+    for dz in range(4, zs + 1):
+        along(late, dz)
 
     def add(r, _):
         resid[r] = masked(r) + acc[r] * mask(r)
@@ -693,11 +741,12 @@
 
     lax.fori_loop(0, rows, third, 0)
     stats[...] = stack_rows(mean1, inv1, mean2, inv2, mean3, inv3)
-    for a in late:
-        move.over_x(a)
-    for a in late:
-        move.finish(a)
-        stores[a - 2].wait()
+    for e in late:
+        move.over_x(e)
+    for e in late:
+        move.finish(e)
+    for copy in stores:
+        copy.wait()
     for copy in first_tiles + second_tiles:
         copy.wait_send()
     move.drain()
@@ -712,16 +761,20 @@
     dims = sizes_of(fsdp, sp)
     zs, ys, _ = dims
     n = len(shards)
-    shapes = []
-    for shard, kind in zip(shards, kinds, strict=True):
+    shapes, plan = [], []
+    for a, (shard, kind) in enumerate(zip(shards, kinds, strict=True)):
         r, width = shard.shape
+        shapes.append((r, width // sp if kind else width))
         h = 1 if kind else parts_of(r, sp)
-        shapes.append((h, r // h, width // sp if kind else width))
-    wholes = [jax.ShapeDtypeStruct((fsdp * h * r, w), BF16) for h, r, w in shapes]
-    staged = [pltpu.VMEM((h * r, w), BF16) for h, r, w in shapes[2:]]
+        plan.append((a, h, r // h, 0))
+    m = len(plan)
+    wholes = [jax.ShapeDtypeStruct((fsdp * r, w), BF16) for r, w in shapes]
+    staged = [pltpu.VMEM(shape, BF16) for shape in shapes[2:]]
     tile = pltpu.VMEM((fsdp, 8, 128), F32)
     return pl.pallas_call(
-        functools.partial(forward_kernel, dims, fsdp, sp, shapes, [max(k, 1) for k in kinds]),
+        functools.partial(
+            forward_kernel, dims, fsdp, sp, shapes, [max(k, 1) for k in kinds], plan
+        ),
         out_shape=[
             jax.ShapeDtypeStruct(field, F32),
             jax.ShapeDtypeStruct(field, BF16),
@@ -754,10 +807,10 @@
             DMA((n, 3)),
             DMA((2, fsdp)),
             DMA((2, fsdp)),
-            DMA((2, n, zs)),
-            DMA((2, n, zs, ys)),
-            DMA((2, n, zs, ys, sp)),
-            DMA((2, n, zs, ys, sp)),
+            DMA((2, m, zs)),
+            DMA((2, m, zs, ys)),
+            DMA((2, m, zs, ys, sp)),
+            DMA((2, m, zs, ys, sp)),
         ],
         compiler_params=params(1),
         name="forward",
@@ -795,13 +848,11 @@
     gtkv,
     gpart,
     grecv,
-    tpart,
     low,
     nsem,
     gsem,
     asem,
     psem,
-    tsem,
 ):
     rows, columns = cot.shape[0], cot.shape[1]
     pixels = rows * columns
@@ -925,11 +976,9 @@
         gpart[to] = to_normed(to).astype(BF16)
     pmoves = send(psem, lambda to: gpart.at[to], grecv)
     start(pmoves)
-    tpart[x] = lax.dot_general(
+    gtext[...] = lax.dot_general(
         gtkv[...], wt[...], (((1,), (1,)), ((), ())), preferred_element_type=F32
     ).astype(BF16)
-    tmoves = send(tsem, lambda to: tpart.at[x], tpart)
-    start(tmoves)
     gnorm[...] = to_normed(x)
     wait(amoves)
     joined = jnp.concatenate([attin[k] for k in range(sp)], axis=1)
@@ -946,11 +995,6 @@
     wait(pmoves)
     for d in range(1, sp):
         gnorm[...] += grecv[(x + d) % sp].astype(F32)
-    wait(tmoves)
-    total = tpart[0].astype(F32)
-    for k in range(1, sp):
-        total = total + tpart[k].astype(F32)
-    gtext[...] = total
 
 
 def attention(nums, normed, text, wq, wt, wo, cot, resid, sp):
@@ -958,7 +1002,7 @@
     pixels = rows * columns
     heads = C // HEAD // sp
     width = heads * HEAD
-    tokens, wide = text.shape
+    tokens = text.shape[0]
     n_keys = sp * pixels + tokens
     return pl.pallas_call(
         functools.partial(attention_kernel, sp, heads),
@@ -968,7 +1012,7 @@
             jax.ShapeDtypeStruct(wq.shape, BF16),
             jax.ShapeDtypeStruct(wt.shape, BF16),
             jax.ShapeDtypeStruct(wo.shape, BF16),
-            jax.ShapeDtypeStruct(text.shape, F32),
+            jax.ShapeDtypeStruct(text.shape, BF16),
         ],
         in_specs=[SMEM] + [VMEM] * 7,
         out_specs=[VMEM] * 6,
@@ -987,10 +1031,9 @@
             pltpu.VMEM((tokens, 2 * width), BF16),
             pltpu.VMEM((sp, pixels, C), BF16),
             pltpu.VMEM((sp, pixels, C), BF16),
-            pltpu.VMEM((sp, tokens, wide), BF16),
             pltpu.VMEM((rows, columns, C), BF16),
         ]
-        + [DMA((2, sp))] * 5,
+        + [DMA((2, sp))] * 4,
         compiler_params=params(2),
         name="attention",
     )(nums, normed, text, wq, wt, wo, cot, resid)
@@ -998,20 +1041,20 @@
 
 def backward_kernel(dims, fsdp, sp, shapes, modes, *refs):
     n = len(shapes)
-    (nums, image, gains, scales, stats, resid, conv_out, s1, s2, gnorm, cot, table, w1, w2), refs = (
-        refs[:14],
-        refs[14:],
+    (nums, image, gains, scales, stats, resid, conv_out, s1, s2, gnorm, cot, table, tpart, w1, w2), refs = (
+        refs[:15],
+        refs[15:],
     )
     attn, refs = refs[: n - 2], refs[n - 2 :]
-    outs, gimage, gscales, etiles, gtotal, refs = refs[:n], *refs[n : n + 4], refs[n + 4 :]
+    outs, gimage, gscales, etiles, gtotal, gtext, refs = refs[:n], *refs[n : n + 5], refs[n + 5 :]
     (w1v, w2v, out1, out2, p1, p2, edge1, edge2, gres, acc, sums, mine, every, pieces, got_e), refs = (
         refs[:15],
         refs[15:],
     )
-    (ggains, got_g, gsmall), refs = refs[:3], refs[3:]
+    (ggains, got_g, gsmall, trecv), refs = refs[:4], refs[4:]
     own, refs = (None, None) + tuple(refs[: n - 2]), refs[n - 2 :]
     bufs, refs = [refs[i * n : (i + 1) * n] for i in range(5)], refs[5 * n :]
-    (ssem, hsem, wsem, tsem, esem, gsem, rsem), sems = refs[:7], refs[7:]
+    (ssem, hsem, wsem, tsem, esem, gsem, rsem, xsem), sems = refs[:8], refs[8:]
     total_of = Sums(dims, sp, shapes, modes, (out1, out2) + tuple(attn), own, outs, bufs, sems)
     rows, columns = image.shape[0], image.shape[1]
     pixels = rows * columns
@@ -1078,6 +1121,11 @@
 
     lax.fori_loop(0, rows, residual, 0)
     swap.edges_start(0, p2.at[1, 1], p2.at[1, rows], edge2)
+    tmoves = []
+    for d in range(1, sp):
+        to = (me, (x + d) % sp)
+        tmoves.append(remote(tpart, trecv.at[d - 1], xsem.at[0, d], xsem.at[1, d], to))
+        tmoves[-1].start()
     weight_grad(s2, p2, out2)
     total_of.start(1)
     for a in late:
@@ -1090,9 +1138,7 @@
     load2.wait()
     taps(rows, columns, p2, w2v, acc, True)
     total_of.over_c(1)
-    for a in late:
-        if shapes[a][0] > 1:
-            total_of.all_x(a)
+    total_of.all_x(1)
     scale, shift = 1.0 + scales[0:1], scales[1:2]
 
     def hat2(r):
@@ -1137,16 +1183,19 @@
     lax.fori_loop(0, rows, middle, 0)
     swap.edges_start(1, p1.at[1, 1], p1.at[1, rows], edge1)
     for a in late:
-        total_of.all_y(a)
+        if shapes[a][0] > 1:
+            total_of.all_x(a)
     weight_grad(s1, p1, out1)
     total_of.start(0)
+    for a in late:
+        if shapes[a][0] == 1:
+            total_of.all_y(a)
     swap.edges_wait(1, p1.at[1, 1], p1.at[1, rows], edge1)
     put_shifted(p1, 0, edge1[0].astype(F32))
     put_shifted(p1, rows + 1, edge1[1].astype(F32))
     load1.wait()
     total_of.over_c(0)
     taps(rows, columns, p1, w1v, acc, True)
-    total_of.both(1)
 
     def hat1(r):
         return (image[r].astype(F32) * mask(r) - mean1) * mask(r) * inv1
@@ -1167,6 +1216,10 @@
 
     gcopies = tiles_start(fsdp, ggains, got_g, gsem.at[0], gsem.at[1], gain_block)
     got_g[me] = ggains[:, pl.ds(pl.multiple_of((me * share) // 128 * 128, 128), 128)]
+    total_of.all_y(1)
+    for a in late:
+        if shapes[a][0] > 1:
+            total_of.all_y(a)
     for copy in copies:
         copy.wait()
     gscales[...] = every[...]
@@ -1182,6 +1235,9 @@
     pieces[...] = jnp.broadcast_to(piece[:, None, :], pieces.shape)
     ecopies = tiles_start(fsdp, pieces, got_e, esem.at[0], esem.at[1], lambda ref, to: ref.at[to])
     got_e[me] = pieces[me]
+    total_of.both(0)
+    for a in late:
+        total_of.over_z(a)
     total = joint(2) / count
     m1, m2 = total[0:1], total[1:2]
 
@@ -1191,10 +1247,20 @@
         return 0
 
     lax.fori_loop(0, rows, final, 0)
-    for a in late:
-        total_of.over_z(a)
     total_of.over_z(1)
-    total_of.both(0)
+    for copy in tmoves:
+        copy.wait()
+    text_rows = 32
+
+    def text_sum(r, _):
+        at = span(r, text_rows, text_rows)
+        value = tpart[at, :].astype(F32)
+        for i in range(sp - 1):
+            value = value + trecv[i, at, :].astype(F32)
+        gtext[at, :] = value
+        return 0
+
+    lax.fori_loop(0, tpart.shape[0] // text_rows, text_sum, 0)
     for copy in gcopies:
         copy.wait()
     total = got_g[0]
@@ -1210,7 +1276,6 @@
         small_copy(d).start()
     for a in late:
         total_of.finish(a)
-    total_of.finish(1)
     for copy in ecopies:
         copy.wait()
     etiles[...] = got_e[...]
@@ -1221,12 +1286,13 @@
         total = total + gsmall[i]
     gtotal[...] = total
     total_of.over_z(0)
+    total_of.finish(1)
     total_of.finish(0)
     total_of.drain()
 
 
 def backward(
-    nums, image, gains, scales, stats, resid, conv_out, s1, s2, gnorm, cot, table, w1, w2, attn, fsdp, sp
+    nums, image, gains, scales, stats, resid, conv_out, s1, s2, gnorm, cot, table, tpart, w1, w2, attn, fsdp, sp
 ):
     rows, columns, _ = image.shape
     field = (rows, columns, C)
@@ -1236,9 +1302,9 @@
     shapes, outs = [], []
     grads = [w1, w2] + [g for g, _ in attn]
     modes = ["add", "add"] + [m for _, m in attn]
-    for grad, mode in zip(grads, modes, strict=True):
+    for a, (grad, mode) in enumerate(zip(grads, modes, strict=True)):
         r, width = grad.shape[0] // fsdp, grad.shape[1]
-        h = parts_of(r, sp) if mode == "add" else 1
+        h = parts_of(r, sp) if mode == "add" and a != 1 else 1
         shapes.append((h, r // h, width))
         copies = 1 if mode == "add" and h == 1 else sp
         outs.append(jax.ShapeDtypeStruct((copies, r // h, width), F32))
@@ -1252,9 +1318,10 @@
     return pl.pallas_call(
         functools.partial(backward_kernel, dims, fsdp, sp, shapes, modes),
         out_shape=outs
-        + [jax.ShapeDtypeStruct(field, F32), tile, tile, jax.ShapeDtypeStruct((8, 128), F32)],
-        in_specs=[SMEM] + [VMEM] * 11 + [ANY] * count,
-        out_specs=[VMEM] * (count + 4),
+        + [jax.ShapeDtypeStruct(field, F32), tile, tile, jax.ShapeDtypeStruct((8, 128), F32)]
+        + [jax.ShapeDtypeStruct(tpart.shape, F32)],
+        in_specs=[SMEM] + [VMEM] * 12 + [ANY] * count,
+        out_specs=[VMEM] * (count + 5),
         scratch_shapes=[
             scratch(*w1.shape),
             scratch(*w2.shape),
@@ -1274,6 +1341,7 @@
             pltpu.VMEM((8, C), F32),
             tiles,
             pltpu.VMEM((sp, 8, 128), F32),
+            scratch(max(sp - 1, 1), *tpart.shape),
         ]
         + [scratch(zs, ys, s[0] * s[1], s[2]) for s in shapes[2:]]
         + [scratch(zs, ys, s[0] * s[1], s[2]) for s in shapes]
@@ -1292,6 +1360,7 @@
             DMA((2, fsdp)),
             DMA((2, fsdp)),
             DMA((2, sp)),
+            DMA((2, sp)),
             DMA((2, count, zs, ys)),
             DMA((2, count, zs, ys, sp)),
             DMA((2, count, zs, ys)),
@@ -1302,7 +1371,7 @@
         compiler_params=params(3),
         name="backward",
     )(
-        nums, image, gains, scales, stats, resid, conv_out, s1, s2, gnorm, cot, table, w1, w2,
+        nums, image, gains, scales, stats, resid, conv_out, s1, s2, gnorm, cot, table, tpart, w1, w2,
         *[g for g, _ in attn],
     )
 
@@ -1361,7 +1430,7 @@
     )
     emb_cols = tiles_in[:, 0, :emb_rows].astype(BF16)
     pixels = rows * columns
-    output, gnorm, gq, gt, go, gtext = attention(
+    output, gnorm, gq, gt, go, tpart = attention(
         nums,
         normed.reshape(pixels, C),
         text[0],
@@ -1372,7 +1441,7 @@
         resid.reshape(pixels, C),
         sp,
     )
-    (r1, r2, rt, rq, ro, gimage, every, tiles_in, small) = backward(
+    (r1, r2, rt, rq, ro, gimage, every, tiles_in, small, gtext) = backward(
         nums,
         image[0],
         gains,
@@ -1385,6 +1454,7 @@
         gnorm.reshape(rows, columns, C),
         cotangent[0],
         table,
+        tpart,
         w1,
         w2,
         [(gt, "join"), (gq, "join"), (go, "add")],

time: 325 us -> 293 us (0.902)
  Pallas kernels: 305 us -> 273 us
    pallas_call x1, Pallas kernels: 97.9 us -> 83.7 us  [forward(): pl.pallas_call(functools.partial(forward_kernel, dims, fsdp, sp, shapes,...]
    pallas_call x1, Pallas kernels: 93.3 us -> 80.1 us  [attention(): pl.pallas_call(functools.partial(attention_kernel, sp, heads), out_shape=...]
    pallas_call x1, Pallas kernels: 113 us -> 109 us  [backward(): pl.pallas_call(functools.partial(backward_kernel, dims, fsdp, sp, shapes,...]
where the time goes in v4:
time: 293 us
  Pallas kernels  273 us (93%)
  local copies, waits for them, and re-layouts  13.1 us (4%)
  other arithmetic  4.52 us (2%)
    pallas_call x1, Pallas kernels, backward(): pl.pallas_call(functools.partial(backward_kernel, dims, fsdp, sp, shapes,...  109 us
    pallas_call x1, Pallas kernels, forward(): pl.pallas_call(functools.partial(forward_kernel, dims, fsdp, sp, shapes,...  83.7 us
    pallas_call x1, Pallas kernels, attention(): pl.pallas_call(functools.partial(attention_kernel, sp, heads), out_shape=...  80.1 us

profile of v4, /device:TPU:0, one launch (start us, length us, event | category | flops | bytes accessed | tf_op | source)
XLA Modules:
  0.0 292.8 jit_solution(9897567516566417218)
XLA Ops:
  1.3 0.6 dynamic_slice.6
  1.9 1.2 concatenate.10.refs_0_.nums
  3.3 0.7 maximum_convert_fusion
  4.1 0.7 bitcast_convert_fusion
  4.8 0.7 maximum_maximum_fusion.refs_2_
  5.5 83.7 %forward.1 = (f32[8,64,512]{2,1,0:T(8,128)}, bf16[8,64,512]{2,1,0:T(8,128)(2,1)}, f32[8,64,512]{2,1,0:T(8,128)}, bf16[3,10,64,512]{3,2,1,0:T(8,128)(2,1)}, bf16[...) custom-call(f32[30]{0:T(128)} %concatenate.10.refs_0_.nums, ...), custom_call_target="tpu_custom_call" | custom-call | tf_op jit(solution)/shard_map/forward/pallas_call | solution.py:774
  89.2 0.8 slice.27
  90.1 80.1 %attention.1 = (bf16[512,512]{1,0:T(8,128)(2,1)}, f32[512,512]{1,0:T(8,128)}, bf16[512,768]{1,0:T(8,128)(2,1)}, bf16[2048,512]{1,0:T(8,128)(2,1)}, bf16[512,512]{1,0:T(8,128)(2,1)}, /*index=5*/bf16[128,2048]{1,0:T(8,128)(2,1)}) custom-call(f32[30]{0:T(128)} %concatenate.10.refs_0_.nums, bf16[512,512]{1,0:T(8,128)(2,1)} %bitcast.54, ...), custom_call_target="tpu_custom_call" | custom-call | tf_op jit(solution)/shard_map/attention/pallas_call | solution.py:1007
  170.2 108.8 %backward.1 = (f32[2,144,512]{2,1,0:T(8,128)}, f32[1,288,512]{2,1,0:T(8,128)}, f32[2,128,512]{2,1,0:T(8,128)}, f32[2,32,768]{2,1,0:T(8,128)}, f32[2,16,512]{2,1,...) custom-call(f32[30]{0:T(128)} %concatenate.10.refs_0_.nums, ...), custom_call_target="tpu_custom_call" | custom-call | tf_op jit(solution)/shard_map/backward/pallas_call | solution.py:1318
  279.1 1.5 bitcast_multiply_fusion
  280.6 0.7 constant_dynamic-slice_fusion
  281.3 0.5 slice_bitcast_fusion
  281.8 0.8 convert_element_type.40
  282.7 1.0 reshape.157
  283.9 0.8 reshape.158
  284.7 1.0 fusion
  286.1 0.4 copy.31
  286.5 1.2 reshape.160
  287.8 0.8 copy.49
  288.6 1.0 copy.50
  289.5 1.0 copy.51
  290.5 0.8 copy.52
  291.3 0.8 copy.53
  292.1 0.6 copy.54
  (29 shorter events, 0.7 us)
Async XLA Ops:
  170.2 108.9 %copy-start.7 = (bf16[1,2048]{1,0:T(2,128)(2,1)S(1)}, bf16[1,2048]{1,0:T(2,128)(2,1)}, u32[]{:S(2)}) copy-start(bf16[1,2048]{1,0:T(2,128)(2,1)} %param.15) | copy-start | bytes 12292
  279.0 6.7 %copy-start.5 = (f32[2,128,512]{2,1,0:T(8,128)S(1)}, f32[2,128,512]{2,1,0:T(8,128)}, u32[]{:S(2)}) copy-start(f32[2,128,512]{2,1,0:T(8,128)} %get-tuple-element.71) | copy-start | bytes 1572868
  283.9 3.9 %copy-start.4 = (bf16[512,512]{1,0:T(8,128)(2,1)S(1)}, bf16[512,512]{1,0:T(8,128)(2,1)}, u32[]{:S(2)}) copy-start(bf16[512,512]{1,0:T(8,128)(2,1)} %get-tuple-element.48) | copy-start | bytes 1572868
  285.8 2.8 copy-start.1
  286.5 3.0 %copy-start = (f32[128,2048]{1,0:T(8,128)S(1)}, f32[128,2048]{1,0:T(8,128)}, u32[]{:S(2)}) copy-start(f32[128,2048]{1,0:T(8,128)} %get-tuple-element.64) | copy-start | bytes 3145732
  288.6 2.0 copy-start.3
  289.5 1.8 copy-start.2
  289.5 2.6 copy-start.6

commit v5 on v4

--- a/solution.py
+++ b/solution.py
@@ -571,11 +571,21 @@
 def forward_kernel(dims, fsdp, sp, shapes, kinds, plan, *refs):
     n = len(shapes)
     (nums, image, tiles, table), shards, refs = refs[:4], refs[4 : 4 + n], refs[4 + n :]
-    (resid, normed, conv_out, s1, s2, stats, gains, scales, got), refs = refs[:9], refs[9:]
+    (resid_out, normed, conv_out_out, s1_out, s2_out, stats, gains, scales, got), refs = (
+        refs[:9],
+        refs[9:],
+    )
     outs, refs = refs[:n], refs[n:]
     (w1v, w2v), bufs, refs = refs[:2], refs[2:n], refs[n:]
     (edge1, edge2, acc, sums, part, part_in), refs = refs[:6], refs[6:]
-    (ssem, hsem, wsem, lsem, tsem, psem), sems = refs[:6], refs[6:]
+    (resid, conv_out, s1, s2), refs = refs[:4], refs[4:]
+    (ssem, hsem, wsem, lsem, tsem, psem, osem), sems = refs[:7], refs[7:]
+    results = [
+        pltpu.make_async_copy(src, dst, osem.at[i])
+        for i, (src, dst) in enumerate(
+            [(s1, s1_out), (conv_out, conv_out_out), (s2, s2_out), (resid, resid_out)]
+        )
+    ]
     sources, wholes = shards[:2] + bufs, (w1v, w2v) + outs[2:]
     entries = [(sources[a], wholes[a], h, r, at, shapes[a][0]) for a, h, r, at in plan]
     move = Gather(dims, sp, entries, sems)
@@ -661,6 +671,7 @@
     lax.fori_loop(0, rows, lambda r, _: (first(r + 1, image[r]), 0)[1], 0)
     first(0, edge1[0])
     first(rows + 1, edge1[1])
+    results[0].start()
     for dz in range(2, dims[0] + 1):
         for e in first_of:
             move.relay(e, dz)
@@ -691,6 +702,7 @@
         return 0
 
     lax.fori_loop(0, rows, keep, 0)
+    results[1].start()
     swap.edges_start(1, conv_out.at[0], conv_out.at[rows - 1], edge2)
     swap.sums_start(1, local_moments(rows, lambda r: conv_out[r], mask, held))
     along(late, 1)
@@ -716,6 +728,7 @@
     lax.fori_loop(0, rows, lambda r, _: (second(r + 1, conv_out[r]), 0)[1], 0)
     second(0, edge2[0])
     second(rows + 1, edge2[1])
+    results[2].start()
     along(late, 3)
     for e in second_of:
         move.over_x(e)
@@ -732,6 +745,7 @@
         return 0
 
     lax.fori_loop(0, rows, add, 0)
+    results[3].start()
     swap.sums_start(2, local_moments(rows, lambda r: resid[r], mask, held))
     mean3, inv3 = joint_moments(swap.sums_wait(2), counts, count)
 
@@ -745,7 +759,7 @@
         move.over_x(e)
     for e in late:
         move.finish(e)
-    for copy in stores:
+    for copy in stores + results:
         copy.wait()
     for copy in first_tiles + second_tiles:
         copy.wait_send()
@@ -788,7 +802,7 @@
         ]
         + wholes,
         in_specs=[SMEM] + [VMEM] * 3 + [ANY] * n,
-        out_specs=[VMEM] * 9 + [ANY] * n,
+        out_specs=[ANY, VMEM, ANY, ANY, ANY] + [VMEM] * 4 + [ANY] * n,
         scratch_shapes=[
             pltpu.VMEM(wholes[0].shape, BF16),
             pltpu.VMEM(wholes[1].shape, BF16),
@@ -801,12 +815,17 @@
             pltpu.VMEM((3, sp, 8, C), F32),
             tile,
             tile,
+            pltpu.VMEM(field, F32),
+            pltpu.VMEM(field, F32),
+            pltpu.VMEM(shifted, BF16),
+            pltpu.VMEM(shifted, BF16),
             DMA((2, 3, sp)),
             DMA((2, 2, 2)),
             DMA((n,)),
             DMA((n, 3)),
             DMA((2, fsdp)),
             DMA((2, fsdp)),
+            DMA((4,)),
             DMA((2, m, zs)),
             DMA((2, m, zs, ys)),
             DMA((2, m, zs, ys, sp)),
@@ -817,43 +836,27 @@
     )(nums, image, tiles, table, *shards)
 
 
-def attention_kernel(
-    sp,
-    heads,
-    nums,
-    normed,
-    text,
-    wq,
-    wt,
-    wo,
-    cot,
-    resid,
-    output,
-    gnorm,
-    gq,
-    gt,
-    go,
-    gtext,
-    nall,
-    gown,
-    gall,
-    qkv,
-    keys,
-    values,
-    dk,
-    dv,
-    att,
-    attin,
-    dqkv,
-    gtkv,
-    gpart,
-    grecv,
-    low,
-    nsem,
-    gsem,
-    asem,
-    psem,
-):
+def attention_kernel(sp, heads, *refs):
+    (nums, normed, text_in, wq, wt_in, wo, cot, resid_in), refs = refs[:8], refs[8:]
+    (output_out, gnorm, gq_out, gt_out, go_out, gtext_out), refs = refs[:6], refs[6:]
+    (nall, gown, gall, qkv, keys, values, dk, dv, att, attin, dqkv, gtkv, gpart, grecv, low), refs = (
+        refs[:15],
+        refs[15:],
+    )
+    (text, wt, resid, output, gq, gt, go, gtext), refs = refs[:8], refs[8:]
+    nsem, gsem, asem, psem, isem, osem = refs
+    load_text, load_wt, load_resid = (
+        pltpu.make_async_copy(src, dst, isem.at[i])
+        for i, (src, dst) in enumerate([(text_in, text), (wt_in, wt), (resid_in, resid)])
+    )
+    results = [
+        pltpu.make_async_copy(src, dst, osem.at[i])
+        for i, (src, dst) in enumerate(
+            [(gtext, gtext_out), (output, output_out), (go, go_out), (gq, gq_out), (gt, gt_out)]
+        )
+    ]
+    for load in (load_text, load_wt, load_resid):
+        load.start()
     rows, columns = cot.shape[0], cot.shape[1]
     pixels = rows * columns
     width = heads * HEAD
@@ -897,6 +900,8 @@
     start(gmoves)
     gall[x] = gown[x]
     nall[x] = normed[...]
+    load_text.wait()
+    load_wt.wait()
     text_kv = jnp.dot(text[...], wt[...], preferred_element_type=F32).astype(BF16)
     keys[total_px:, :] = text_kv[:, :width]
     values[total_px:, :] = text_kv[:, width:]
@@ -979,22 +984,30 @@
     gtext[...] = lax.dot_general(
         gtkv[...], wt[...], (((1,), (1,)), ((), ())), preferred_element_type=F32
     ).astype(BF16)
+    results[0].start()
     gnorm[...] = to_normed(x)
+    load_resid.wait()
     wait(amoves)
     joined = jnp.concatenate([attin[k] for k in range(sp)], axis=1)
     branch = jnp.dot(joined, wo[...], preferred_element_type=F32)
     for r in range(rows):
         at = slice(r * columns, (r + 1) * columns)
         output[at, :] = (resid[at, :] + branch[at] * nums[r + 1]).astype(BF16)
+    results[1].start()
     down = (((0,), (0,)), ((), ()))
     go[...] = lax.dot_general(joined, low2, down, preferred_element_type=F32).astype(BF16)
+    results[2].start()
     gq[...] = lax.dot_general(
         nall[...].reshape(total_px, C), dqkv[...], down, preferred_element_type=F32
     ).astype(BF16)
+    results[3].start()
     gt[...] = lax.dot_general(text[...], gtkv[...], down, preferred_element_type=F32).astype(BF16)
+    results[4].start()
     wait(pmoves)
     for d in range(1, sp):
         gnorm[...] += grecv[(x + d) % sp].astype(F32)
+    for copy in results:
+        copy.wait()
 
 
 def attention(nums, normed, text, wq, wt, wo, cot, resid, sp):
@@ -1014,8 +1027,8 @@
             jax.ShapeDtypeStruct(wo.shape, BF16),
             jax.ShapeDtypeStruct(text.shape, BF16),
         ],
-        in_specs=[SMEM] + [VMEM] * 7,
-        out_specs=[VMEM] * 6,
+        in_specs=[SMEM, VMEM, ANY, VMEM, ANY, VMEM, VMEM, ANY],
+        out_specs=[ANY, VMEM, ANY, ANY, ANY, ANY],
         scratch_shapes=[
             pltpu.VMEM((sp, pixels, C), BF16),
             pltpu.VMEM((sp, pixels, width), BF16),
@@ -1032,8 +1045,17 @@
             pltpu.VMEM((sp, pixels, C), BF16),
             pltpu.VMEM((sp, pixels, C), BF16),
             pltpu.VMEM((rows, columns, C), BF16),
+            pltpu.VMEM(text.shape, BF16),
+            pltpu.VMEM(wt.shape, BF16),
+            pltpu.VMEM((pixels, C), F32),
+            pltpu.VMEM((pixels, C), BF16),
+            pltpu.VMEM(wq.shape, BF16),
+            pltpu.VMEM(wt.shape, BF16),
+            pltpu.VMEM(wo.shape, BF16),
+            pltpu.VMEM(text.shape, BF16),
         ]
-        + [DMA((2, sp))] * 4,
+        + [DMA((2, sp))] * 4
+        + [DMA((3,)), DMA((5,))],
         compiler_params=params(2),
         name="attention",
     )(nums, normed, text, wq, wt, wo, cot, resid)
@@ -1041,20 +1063,28 @@
 
 def backward_kernel(dims, fsdp, sp, shapes, modes, *refs):
     n = len(shapes)
-    (nums, image, gains, scales, stats, resid, conv_out, s1, s2, gnorm, cot, table, tpart, w1, w2), refs = (
-        refs[:15],
-        refs[15:],
-    )
+    (nums, image_in, gains, scales, stats, resid, conv_in, s1_in, s2_in, gnorm, cot), refs = (
+        refs[:11],
+        refs[11:],
+    )
+    (table, tpart, w1, w2), refs = refs[:4], refs[4:]
     attn, refs = refs[: n - 2], refs[n - 2 :]
     outs, gimage, gscales, etiles, gtotal, gtext, refs = refs[:n], *refs[n : n + 5], refs[n + 5 :]
     (w1v, w2v, out1, out2, p1, p2, edge1, edge2, gres, acc, sums, mine, every, pieces, got_e), refs = (
         refs[:15],
         refs[15:],
     )
-    (ggains, got_g, gsmall, trecv), refs = refs[:4], refs[4:]
+    (ggains, got_g, gsmall, trecv, image, conv_out, s1, s2), refs = refs[:8], refs[8:]
     own, refs = (None, None) + tuple(refs[: n - 2]), refs[n - 2 :]
     bufs, refs = [refs[i * n : (i + 1) * n] for i in range(5)], refs[5 * n :]
-    (ssem, hsem, wsem, tsem, esem, gsem, rsem, xsem), sems = refs[:8], refs[8:]
+    (ssem, hsem, wsem, tsem, esem, gsem, rsem, xsem, isem), sems = refs[:9], refs[9:]
+    load_s2, load_conv, load_s1, load_image = (
+        pltpu.make_async_copy(src, dst, isem.at[i])
+        for i, (src, dst) in enumerate(
+            [(s2_in, s2), (conv_in, conv_out), (s1_in, s1), (image_in, image)]
+        )
+    )
+    load_s2.start()
     total_of = Sums(dims, sp, shapes, modes, (out1, out2) + tuple(attn), own, outs, bufs, sems)
     rows, columns = image.shape[0], image.shape[1]
     pixels = rows * columns
@@ -1063,7 +1093,8 @@
     load1 = pltpu.make_async_copy(w1, w1v, wsem.at[0])
     load2 = pltpu.make_async_copy(w2, w2v, wsem.at[1])
     load2.start()
-    load1.start()
+    for load in (load_conv, load_s1, load1, load_image):
+        load.start()
     edge1[...] = jnp.zeros_like(edge1)
     edge2[...] = jnp.zeros_like(edge2)
     greet(swap.peers() + [((me + d) % fsdp, x) for d in range(1, fsdp)])
@@ -1126,6 +1157,7 @@
         to = (me, (x + d) % sp)
         tmoves.append(remote(tpart, trecv.at[d - 1], xsem.at[0, d], xsem.at[1, d], to))
         tmoves[-1].start()
+    load_s2.wait()
     weight_grad(s2, p2, out2)
     total_of.start(1)
     for a in late:
@@ -1154,6 +1186,7 @@
         acc[r] = g
         return g, g * hat
 
+    load_conv.wait()
     plain, crossed = column_sums(rows, from_two)
     gain2 = crossed * scale
     swap.sums_start(
@@ -1185,6 +1218,7 @@
     for a in late:
         if shapes[a][0] > 1:
             total_of.all_x(a)
+    load_s1.wait()
     weight_grad(s1, p1, out1)
     total_of.start(0)
     for a in late:
@@ -1206,6 +1240,7 @@
         acc[r] = g
         return g, g * hat
 
+    load_image.wait()
     plain, crossed = column_sums(rows, from_one)
     swap.sums_start(2, stack_rows(lane_groups(plain * g1), lane_groups(crossed * g1)))
     ggains[...] = stack_rows(crossed, gain2, gain3)
@@ -1320,7 +1355,7 @@
         out_shape=outs
         + [jax.ShapeDtypeStruct(field, F32), tile, tile, jax.ShapeDtypeStruct((8, 128), F32)]
         + [jax.ShapeDtypeStruct(tpart.shape, F32)],
-        in_specs=[SMEM] + [VMEM] * 12 + [ANY] * count,
+        in_specs=[SMEM, ANY, VMEM, VMEM, VMEM, VMEM, ANY, ANY, ANY] + [VMEM] * 4 + [ANY] * count,
         out_specs=[VMEM] * (count + 5),
         scratch_shapes=[
             scratch(*w1.shape),
@@ -1342,6 +1377,10 @@
             tiles,
             pltpu.VMEM((sp, 8, 128), F32),
             scratch(max(sp - 1, 1), *tpart.shape),
+            scratch(*field),
+            pltpu.VMEM(field, F32),
+            scratch(*shifted),
+            scratch(*shifted),
         ]
         + [scratch(zs, ys, s[0] * s[1], s[2]) for s in shapes[2:]]
         + [scratch(zs, ys, s[0] * s[1], s[2]) for s in shapes]
@@ -1361,6 +1400,7 @@
             DMA((2, fsdp)),
             DMA((2, sp)),
             DMA((2, sp)),
+            DMA((4,)),
             DMA((2, count, zs, ys)),
             DMA((2, count, zs, ys, sp)),
             DMA((2, count, zs, ys)),

time: 293 us -> 287 us (0.980)
  Pallas kernels: 273 us -> 267 us
where the time goes in v5:
time: 287 us
  Pallas kernels  267 us (93%)
  local copies, waits for them, and re-layouts  13.1 us (5%)
  other arithmetic  4.52 us (2%)
    pallas_call x1, Pallas kernels, backward(): pl.pallas_call(functools.partial(backward_kernel, dims, fsdp, sp, shapes,...  107 us
    pallas_call x1, Pallas kernels, forward(): pl.pallas_call(functools.partial(forward_kernel, dims, fsdp, sp, shapes,...  81.8 us
    pallas_call x1, Pallas kernels, attention(): pl.pallas_call(functools.partial(attention_kernel, sp, heads), out_shape=...  77.8 us

profile of v5, /device:TPU:0, one launch (start us, length us, event | category | flops | bytes accessed | tf_op | source)
XLA Modules:
  0.0 287.0 jit_solution(8944740030053775074)
XLA Ops:
  1.3 0.6 dynamic_slice.6
  1.9 1.2 concatenate.10.refs_0_
  3.3 0.7 maximum_convert_fusion
  4.1 0.7 bitcast_convert_fusion
  4.8 0.7 maximum_maximum_fusion.refs_2_
  5.5 81.8 %forward.1 = (f32[8,64,512]{2,1,0:T(8,128)}, bf16[8,64,512]{2,1,0:T(8,128)(2,1)}, f32[8,64,512]{2,1,0:T(8,128)}, bf16[3,10,64,512]{3,2,1,0:T(8,128)(2,1)}, bf16[...) custom-call(f32[30]{0:T(128)} %concatenate.10.refs_0_, ...), custom_call_target="tpu_custom_call" | custom-call | tf_op jit(solution)/shard_map/forward/pallas_call | solution.py:788
  87.3 0.8 slice.27
  88.2 77.8 %attention.1 = (bf16[512,512]{1,0:T(8,128)(2,1)}, f32[512,512]{1,0:T(8,128)}, bf16[512,768]{1,0:T(8,128)(2,1)}, bf16[2048,512]{1,0:T(8,128)(2,1)}, bf16[512,512]{1,0:T(8,128)(2,1)}, /*index=5*/bf16[128,2048]{1,0:T(8,128)(2,1)}) custom-call(f32[30]{0:T(128)} %concatenate.10.refs_0_, bf16[512,512]{1,0:T(8,128)(2,1)} %bitcast.54, bf16[128,2048]{1,0:T(8,128)(2,1)} %bitcast.53, ...), custom_call_target="tpu_custom_call" | custom-call | tf_op jit(solution)/shard_map/attention/pallas_call | solution.py:1020
  166.0 107.3 %backward.1 = (f32[2,144,512]{2,1,0:T(8,128)}, f32[1,288,512]{2,1,0:T(8,128)}, f32[2,128,512]{2,1,0:T(8,128)}, f32[2,32,768]{2,1,0:T(8,128)}, f32[2,16,512]{2,1,...) custom-call(f32[30]{0:T(128)} %concatenate.10.refs_0_, ...), custom_call_target="tpu_custom_call" | custom-call | tf_op jit(solution)/shard_map/backward/pallas_call | solution.py:1353
  273.3 1.5 bitcast_multiply_fusion
  274.8 0.7 constant_dynamic-slice_fusion
  275.5 0.5 slice_bitcast_fusion
  276.1 0.8 convert_element_type.40
  276.9 1.0 reshape.157
  278.1 0.8 reshape.158
  278.9 1.0 fusion
  280.3 0.4 copy.31
  280.8 1.2 reshape.160
  282.0 0.8 copy.49
  282.8 1.0 copy.50
  283.7 1.0 copy.51
  284.7 0.8 copy.52
  285.5 0.8 copy.53
  286.4 0.6 copy.54
  (29 shorter events, 0.7 us)
Async XLA Ops:
  166.0 107.3 %copy-start.7 = (bf16[1,2048]{1,0:T(2,128)(2,1)S(1)}, bf16[1,2048]{1,0:T(2,128)(2,1)}, u32[]{:S(2)}) copy-start(bf16[1,2048]{1,0:T(2,128)(2,1)} %param.15) | copy-start | bytes 12292
  273.3 6.7 %copy-start.5 = (f32[2,128,512]{2,1,0:T(8,128)S(1)}, f32[2,128,512]{2,1,0:T(8,128)}, u32[]{:S(2)}) copy-start(f32[2,128,512]{2,1,0:T(8,128)} %get-tuple-element.71) | copy-start | bytes 1572868
  278.1 3.9 %copy-start.4 = (bf16[512,512]{1,0:T(8,128)(2,1)S(1)}, bf16[512,512]{1,0:T(8,128)(2,1)}, u32[]{:S(2)}) copy-start(bf16[512,512]{1,0:T(8,128)(2,1)} %get-tuple-element.48) | copy-start | bytes 1572868
  280.0 2.8 copy-start.1
  280.7 3.0 %copy-start = (f32[128,2048]{1,0:T(8,128)S(1)}, f32[128,2048]{1,0:T(8,128)}, u32[]{:S(2)}) copy-start(f32[128,2048]{1,0:T(8,128)} %get-tuple-element.64) | copy-start | bytes 3145732
  282.8 2.0 copy-start.3
  283.7 1.8 copy-start.2
  283.7 2.6 copy-start.6

commit v6 on v5

--- a/solution.py
+++ b/solution.py
@@ -395,6 +395,15 @@
             for k in range(1, self.sp):
                 value = value + self.last[a][k].astype(F32)
             self.outs[a][0] = value
+        elif self.modes[a] != "add":
+            kinds = self.modes[a]
+            width = self.shapes[a][2] // kinds
+            for k in range(self.sp):
+                for j in range(kinds):
+                    at = (j * self.sp + k) * width
+                    self.outs[a][:, at : at + width] = self.last[a][
+                        k, :, j * width : (j + 1) * width
+                    ].astype(F32)
         else:
             for k in range(self.sp):
                 self.outs[a][k] = self.last[a][k].astype(F32)
@@ -1283,6 +1292,7 @@
 
     lax.fori_loop(0, rows, final, 0)
     total_of.over_z(1)
+    total_of.over_z(0)
     for copy in tmoves:
         copy.wait()
     text_rows = 32
@@ -1320,7 +1330,6 @@
     for i in range(1, sp):
         total = total + gsmall[i]
     gtotal[...] = total
-    total_of.over_z(0)
     total_of.finish(1)
     total_of.finish(0)
     total_of.drain()
@@ -1341,8 +1350,10 @@
         r, width = grad.shape[0] // fsdp, grad.shape[1]
         h = parts_of(r, sp) if mode == "add" and a != 1 else 1
         shapes.append((h, r // h, width))
-        copies = 1 if mode == "add" and h == 1 else sp
-        outs.append(jax.ShapeDtypeStruct((copies, r // h, width), F32))
+        if mode == "add":
+            outs.append(jax.ShapeDtypeStruct((h, r // h, width), F32))
+        else:
+            outs.append(jax.ShapeDtypeStruct((r, sp * width), F32))
     count = len(grads)
 
     def scratch(*shape):
@@ -1497,7 +1508,7 @@
         tpart,
         w1,
         w2,
-        [(gt, "join"), (gq, "join"), (go, "add")],
+        [(gt, 2), (gq, 3), (go, "add")],
         fsdp,
         sp,
     )
@@ -1505,10 +1516,6 @@
     grad_emb_proj = lax.dot_general(
         emb_cols, grad_scales, (((0,), (0,)), ((), ())), preferred_element_type=F32
     )
-
-    def joined(result, kinds):
-        n = result.shape[1]
-        return result.reshape(sp, n, kinds, width).transpose(1, 2, 0, 3).reshape(n, kinds * C)
 
     grad_embedding = tiles_in[:, 0, :emb_rows].reshape(1, -1)
     sigmoid = jax.nn.sigmoid(emb_float)
@@ -1526,8 +1533,8 @@
         gain_sums[1],
         r2.reshape(-1, C),
         gain_sums[2],
-        joined(rq, 3),
-        joined(rt, 2),
+        rq,
+        rt,
         ro.reshape(-1, C),
     )
 

time: 287 us -> 283 us (0.986)
  Pallas kernels: 267 us -> 264 us
    reshape x4 -> x0, local copies, waits for them, and re-layouts: 3.41 us -> none  [joined(): result.reshape(sp, n, kinds, width).transpose(1, 2, 0, 3)]
    pallas_call x1, Pallas kernels: 107 us -> 104 us  [backward(): pl.pallas_call(functools.partial(backward_kernel, dims, fsdp, sp, shapes,...]
    unnamed x22 -> x24, local copies, waits for them, and re-layouts: 5.03 us -> 7.85 us
where the time goes in v6:
time: 283 us
  Pallas kernels  264 us (93%)
  local copies, waits for them, and re-layouts  12 us (4%)
  other arithmetic  4.55 us (2%)
    pallas_call x1, Pallas kernels, backward(): pl.pallas_call(functools.partial(backward_kernel, dims, fsdp, sp, shapes,...  104 us
    pallas_call x1, Pallas kernels, forward(): pl.pallas_call(functools.partial(forward_kernel, dims, fsdp, sp, shapes,...  81.8 us
    pallas_call x1, Pallas kernels, attention(): pl.pallas_call(functools.partial(attention_kernel, sp, heads), out_shape=...  77.8 us
    unnamed x24, local copies, waits for them, and re-layouts  7.85 us

profile of v6, /device:TPU:0, one launch (start us, length us, event | category | flops | bytes accessed | tf_op | source)
XLA Modules:
  0.0 282.8 jit_solution(9516974394674483271)
XLA Ops:
  1.3 0.6 dynamic_slice.6
  1.9 1.2 concatenate.10.refs_0_
  3.2 0.1 pad.2.clone
  3.3 0.7 maximum_convert_fusion
  4.0 0.1 tile.10
  4.1 0.7 bitcast_convert_fusion
  4.8 0.7 maximum_maximum_fusion.refs_2_
  5.5 81.8 %forward.1 = (f32[8,64,512]{2,1,0:T(8,128)}, bf16[8,64,512]{2,1,0:T(8,128)(2,1)}, f32[8,64,512]{2,1,0:T(8,128)}, bf16[3,10,64,512]{3,2,1,0:T(8,128)(2,1)}, bf16[...) custom-call(f32[30]{0:T(128)} %concatenate.10.refs_0_, ...), custom_call_target="tpu_custom_call" | custom-call | tf_op jit(solution)/shard_map/forward/pallas_call | solution.py:797
  87.3 0.8 slice.27
  88.2 77.8 %attention.1 = (bf16[512,512]{1,0:T(8,128)(2,1)}, f32[512,512]{1,0:T(8,128)}, bf16[512,768]{1,0:T(8,128)(2,1)}, bf16[2048,512]{1,0:T(8,128)(2,1)}, bf16[512,512]{1,0:T(8,128)(2,1)}, /*index=5*/bf16[128,2048]{1,0:T(8,128)(2,1)}) custom-call(f32[30]{0:T(128)} %concatenate.10.refs_0_, bf16[512,512]{1,0:T(8,128)(2,1)} %bitcast.50, bf16[128,2048]{1,0:T(8,128)(2,1)} %bitcast.49, ...), custom_call_target="tpu_custom_call" | custom-call | tf_op jit(solution)/shard_map/attention/pallas_call | solution.py:1029
  166.0 104.2 %backward.1 = (f32[2,144,512]{2,1,0:T(8,128)}, f32[1,288,512]{2,1,0:T(8,128)}, f32[128,1024]{1,0:T(8,128)}, f32[32,1536]{1,0:T(8,128)}, f32[2,16,512]{2,1,0:T(8,...) custom-call(f32[30]{0:T(128)} %concatenate.10.refs_0_, ...), custom_call_target="tpu_custom_call" | custom-call | tf_op jit(solution)/shard_map/backward/pallas_call | solution.py:1364
  270.2 1.5 bitcast_multiply_fusion
  271.7 0.7 constant_dynamic-slice_fusion
  272.5 0.5 slice_bitcast_fusion
  273.0 0.8 convert_element_type.40
  273.9 1.0 fusion
  274.9 0.8 copy.46
  275.7 2.3 copy.47
  278.0 1.0 copy.48
  279.0 0.8 copy.49
  279.8 0.8 copy.50
  280.7 0.7 copy.51
  281.3 0.8 copy.52
  282.1 0.6 copy.53
  (25 shorter events, 0.1 us)
Async XLA Ops:
  166.0 104.2 %copy-start.7 = (bf16[1,2048]{1,0:T(2,128)(2,1)S(1)}, bf16[1,2048]{1,0:T(2,128)(2,1)}, u32[]{:S(2)}) copy-start(bf16[1,2048]{1,0:T(2,128)(2,1)} %param.15) | copy-start | bytes 12292
  166.0 108.9 %copy-start.3 = (bf16[512,512]{1,0:T(8,128)(2,1)S(1)}, bf16[512,512]{1,0:T(8,128)(2,1)}, u32[]{:S(2)}) copy-start(bf16[512,512]{1,0:T(8,128)(2,1)} %get-tuple-element.48) | copy-start | bytes 1572868
  270.2 7.8 %copy-start = (f32[128,2048]{1,0:T(8,128)S(1)}, f32[128,2048]{1,0:T(8,128)}, u32[]{:S(2)}) copy-start(f32[128,2048]{1,0:T(8,128)} %get-tuple-element.64) | copy-start | bytes 3145732
  275.7 3.3 %copy-start.2 = (f32[2,144,512]{2,1,0:T(8,128)S(1)}, f32[2,144,512]{2,1,0:T(8,128)}, u32[]{:S(2)}) copy-start(f32[2,144,512]{2,1,0:T(8,128)} %get-tuple-element.66) | copy-start | bytes 1769476
  278.0 1.8 copy-start.1
  278.0 2.6 copy-start.5
  278.0 3.3 %copy-start.4 = (f32[128,1024]{1,0:T(8,128)S(1)}, f32[128,1024]{1,0:T(8,128)}, u32[]{:S(2)}) copy-start(f32[128,1024]{1,0:T(8,128)} %get-tuple-element.104) | copy-start | bytes 1572868
  279.0 3.1 %copy-start.6 = (f32[2,16,512]{2,1,0:T(8,128)S(1)}, f32[2,16,512]{2,1,0:T(8,128)}, u32[]{:S(2)}) copy-start(f32[2,16,512]{2,1,0:T(8,128)} %get-tuple-element.72) | copy-start | bytes 196612
